TPU v7x, 512 devices: a whole 4x8x8 slice. The times are simulated.
512 devices in a mesh: dp: 64 (over y, z_hi, core), expert: 8 (over x, z_lo).
Axes of the slice: x: 4, y: 8, z: 8 (z_hi: 4, z_lo: 2; z = z_hi * 2 + z_lo), core: 2. Of those that a mesh axis runs over, the one named last changes fastest.
Arguments:
- activations: bfloat16 [4096, 4096], P('expert', 'dp'), may hold values from -6 to 6
- out_grad: bfloat16 [4096, 4096], P('expert', 'dp'), may hold values from -6 to 6
- w_in: bfloat16 [8, 4096, 8192], P('expert', None, 'dp'), may hold values from -0.25 to 0.25
- w_out: bfloat16 [8, 8192, 4096], P('expert', 'dp'), may hold values from -0.0625 to 0.0625
- chosen: int32 [8, 256], replicated, may hold values from 0 to 4095, as said below
- gate_scores: float32 [8, 256], P('expert'), may hold values from 0.2 to 1
Outputs:
- w_in_grad: bfloat16 [8, 4096, 8192], P('expert', None, 'dp')
- w_out_grad: bfloat16 [8, 8192, 4096], P('expert', 'dp')
- act_grad: bfloat16 [4096, 4096], P('expert', 'dp')
- gate_grad: float32 [8, 256], P('expert')
Inputs may be any that keep to these rules, and one draw needn't show every extreme that they name: Each row of chosen holds 256 distinct token numbers.
All inputs are finite; a program needn't handle non-finite values.
Results may differ from a plain program's by a relative error of at most 0.0075.
Values may be sent and summed in bfloat16 or wider, within the bound.
No kernel may reach another device: no remote copies, remote signals or barrier semaphores. Data moves between devices by JAX's collectives and lax.ppermute only.
A program may use at most 64 MiB of HBM per device.

v0:
```python
import jax
import jax.numpy as jnp
from jax import lax
from jax.sharding import PartitionSpec as P

GELU_SCALE = 0.7978845608
CUBIC_COEF = 0.044715


def gelu_parts(preact):
    inner = GELU_SCALE * (preact + CUBIC_COEF * preact * preact * preact)
    tanh_part = jnp.tanh(inner)
    gelu_val = 0.5 * preact * (1.0 + tanh_part)
    gelu_slope = 0.5 * (1.0 + tanh_part) + 0.5 * preact * (
        1.0 - tanh_part * tanh_part
    ) * GELU_SCALE * (1.0 + 3.0 * CUBIC_COEF * preact * preact)
    return (gelu_val, gelu_slope)


def contract(left_operand, right_operand, left_axis, right_axis):
    return lax.dot_general(
        left_operand,
        right_operand,
        (((left_axis,), (right_axis,)), ((), ())),
        preferred_element_type=jnp.float32,
    )


def exact_contract(left_operand, right_operand, left_axis, right_axis):
    return lax.dot_general(
        left_operand,
        right_operand,
        (((left_axis,), (right_axis,)), ((), ())),
        precision=lax.Precision.HIGHEST,
        preferred_element_type=jnp.float32,
    )


def input_sum(weight_in, preact_back):
    return lax.psum_scatter(
        contract(weight_in, preact_back, 1, 1), "dp", scatter_dimension=0, tiled=True
    )


def per_device(activations, out_grad, w_in, w_out, chosen, gate_scores):
    expert_id = lax.axis_index("expert")
    experts = lax.axis_size("expert")
    own_rows = activations.shape[0]
    every_act, every_grad = (
        lax.all_gather(activations, "expert", axis=0, tiled=True),
        lax.all_gather(out_grad, "expert", axis=0, tiled=True),
    )
    picked = lax.dynamic_index_in_dim(chosen, expert_id, 0, keepdims=False)
    inputs, upstream = (
        lax.all_gather(jnp.take(every_act, picked, axis=0), "dp", axis=1, tiled=True),
        lax.all_gather(jnp.take(every_grad, picked, axis=0), "dp", axis=1, tiled=True),
    )
    weight_in = w_in[0]
    weight_out = w_out[0]
    scores = gate_scores[0]
    gated_grad = (scores[:, None] * upstream.astype(jnp.float32)).astype(jnp.bfloat16)
    preact = jnp.dot(inputs, weight_in, preferred_element_type=jnp.float32)
    gelu_val, gelu_slope = gelu_parts(preact)
    hidden = gelu_val.astype(jnp.bfloat16)
    raw_back = contract(upstream, weight_out, 1, 1)
    gate_grad = lax.psum(jnp.sum(hidden.astype(jnp.float32) * raw_back, axis=1), "dp")
    hidden_back = contract(gated_grad, weight_out, 1, 1)
    preact_back = (hidden_back * gelu_slope).astype(jnp.bfloat16)
    weight_in_grad = contract(inputs, preact_back, 0, 0).astype(jnp.bfloat16)
    weight_out_grad = contract(hidden, gated_grad, 0, 0).astype(jnp.bfloat16)
    summed = input_sum(weight_in, preact_back)
    accumulated = jnp.zeros((summed.shape[0], own_rows), jnp.float32)
    expert_terms = lax.all_gather(summed[None], "expert", axis=0, tiled=True)
    token_ids = expert_id * own_rows + lax.iota(jnp.int32, own_rows)
    for expert_num in range(experts):
        onehot = (chosen[expert_num][None, :] == token_ids[:, None]).astype(jnp.float32)
        accumulated = accumulated + exact_contract(expert_terms[expert_num], onehot, 1, 1)
    act_grad = accumulated.T.astype(jnp.bfloat16)
    return (weight_in_grad[None], weight_out_grad[None], act_grad, gate_grad[None])


def solution(mesh):
    return jax.shard_map(
        per_device,
        mesh=mesh,
        in_specs=(
            P("expert", "dp"),
            P("expert", "dp"),
            P("expert", None, "dp"),
            P("expert", "dp", None),
            P(),
            P("expert", None),
        ),
        out_specs=(
            P("expert", None, "dp"),
            P("expert", "dp", None),
            P("expert", "dp"),
            P("expert", None),
        ),
        check_vma=False,
    )
```

profile of v0, /device:TPU:16, one launch (start us, length us, event | category | flops | bytes accessed | tf_op | source)
XLA Modules:
  0.0 458.6 jit_solution(974488165680355465)
XLA Ops:
  7.2 1.0 fusion.50
  8.3 1.0 copy.20
  9.3 1.0 copy.22
  10.2 33.9 %all_gather.17 = bf16[4096,64]{1,0:T(8,128)(2,1)S(1)} all-gather(bf16[512,64]{1,0:T(8,128)(2,1)S(1)} %copy.22), channel_id=1, replica_groups=mesh['dp'=64,'expert'=8] {'expert'}, dimensions={0}, use_global_device_ids=true | all-gather | bytes 589824 | tf_op jit(solution)/shard_map/all_gather | solution.py:51
  44.1 32.9 %all_gather.15 = bf16[4096,64]{1,0:T(8,128)(2,1)S(1)} all-gather(bf16[512,64]{1,0:T(8,128)(2,1)S(1)} %copy.20), channel_id=1, replica_groups=mesh['dp'=64,'expert'=8] {'expert'}, dimensions={0}, use_global_device_ids=true | all-gather | bytes 589824 | tf_op jit(solution)/shard_map/all_gather | solution.py:50
  77.0 0.9 gather_fusion.1
  77.9 0.9 gather_fusion
  78.9 0.7 copy.21
  79.7 0.7 copy.23
  80.5 87.1 %all-gather.4.cloned.1.call-done = bf16[256,4096]{0,1:T(8,128)(2,1)} async-done(((bf16[256,64]{0,1:T(8,128)(2,1)}), bf16[256,4096]{0,1:T(8,128)(2,1)}) %all-gather.4.cloned.1.call-update) | async-done | bytes 2097168 | tf_op jit(solution)/shard_map/all_gather | solution.py:55
  167.5 2.3 fusion.8
  169.9 83.2 %all-gather.6.cloned.1.call-done = bf16[256,4096]{0,1:T(8,128)(2,1)} async-done(((bf16[256,64]{0,1:T(8,128)(2,1)}), bf16[256,4096]{0,1:T(8,128)(2,1)}) %all-gather.6.cloned.1.call-update) | async-done | bytes 2097168 | tf_op jit(solution)/shard_map/all_gather | solution.py:56
  253.1 2.4 fusion.4
  255.5 2.7 convolution_bitcast_fusion
  258.2 5.6 %copy.35 = f32[4096,256]{1,0:T(8,128)} copy(f32[4096,256]{0,1:T(8,128)} %convolution_bitcast_fusion) | data formatting | bytes 8388608
  263.9 2.8 fusion.6
  266.7 121.4 %psum.7 = f32[1,256]{1,0:T(1,128)} all-reduce(f32[1,256]{1,0:T(1,128)S(1)} %bitcast.45), channel_id=1, replica_groups=mesh['dp'=64,'expert'=8] {'dp'}, use_global_device_ids=true, to_apply=%region_2.4 | all-reduce | flops 256 | bytes 2048 | tf_op jit(solution)/shard_map/psum | solution.py:66
  388.1 1.7 fusion
  389.8 1.8 fusion.1
  391.6 26.0 %reduce-scatter.4.cloned.1.call-done = f32[64,256]{1,0:T(8,128)} async-done(((f32[4096,256]{1,0:T(8,128)}), f32[64,256]{1,0:T(8,128)}) %reduce-scatter.4.cloned.1.call-update) | async-done | bytes 65552 | tf_op jit(solution)/shard_map/reduce_scatter | solution.py:40
  417.6 30.3 %all-gather = f32[512,256]{1,0:T(8,128)S(1)} all-gather(f32[64,256]{1,0:T(8,128)} %reduce-scatter.4.cloned.1.call-done), channel_id=2, replica_groups=mesh['dp'=64,'expert'=8] {'expert'}, dimensions={0}, use_global_device_ids=true | all-gather | bytes 589824 | tf_op jit(solution)/shard_map/all_gather | solution.py:73
  448.3 0.4 convolution_add_fusion.6
  449.7 0.4 convolution_add_fusion.3
  451.0 1.1 fusion.5
  (26 shorter events, 2.5 us)
Async XLA Ops:
  7.2 160.4 %copy-start = (bf16[1,4096,128]{2,1,0:T(8,128)(2,1)S(1)}, bf16[1,4096,128]{2,1,0:T(8,128)(2,1)}, u32[]{:S(2)}) copy-start(bf16[1,4096,128]{2,1,0:T(8,128)(2,1)} %param.10) | copy-start | bytes 3145732
  7.2 160.3 %all-gather.4.cloned.1.call-start = ((), (), s32[]{:S(2)}) async-start(), calls=%async_computation.1 | async-start | bytes 2129920 | tf_op jit(solution)/shard_map/all_gather | solution.py:55
  77.9 175.2 %copy-start.3 = (f32[1,256]{1,0:T(1,128)S(1)}, f32[1,256]{1,0:T(1,128)}, u32[]{:S(2)}) copy-start(f32[1,256]{1,0:T(1,128)} %param.13) | copy-start | bytes 3076
  78.9 174.2 %copy-start.4 = (bf16[1,128,4096]{2,1,0:T(8,128)(2,1)S(1)}, bf16[1,128,4096]{2,1,0:T(8,128)(2,1)}, u32[]{:S(2)}) copy-start(bf16[1,128,4096]{2,1,0:T(8,128)(2,1)} %param.11) | copy-start | bytes 3145732
  79.6 173.5 %all-gather.6.cloned.1.call-start = ((), (), s32[]{:S(2)}) async-start(), calls=%async_computation.2 | async-start | bytes 2129920 | tf_op jit(solution)/shard_map/all_gather | solution.py:56
  80.4 337.2 %reduce-scatter.4.cloned.1.call-start = ((), (), s32[]{:S(2)}) async-start(), calls=%async_computation.3 | async-start | bytes 4259840 | tf_op jit(solution)/shard_map/reduce_scatter | solution.py:40
  263.8 124.3 %copy-start.1 = (bf16[256,4096]{0,1:T(8,128)(2,1)S(1)}, bf16[256,4096]{0,1:T(8,128)(2,1)}, u32[]{:S(2)}) copy-start(bf16[256,4096]{0,1:T(8,128)(2,1)} %all-gather.4.cloned.1.call-done) | copy-start | bytes 6291460
  388.1 1.7 copy-start.2
Sparse Core Ops, SparseCore 0:
  79.7 87.7 all-gather.3
  171.4 81.6 all-gather.5
  264.0 153.6 reduce-scatter.3
where the time goes:
time: 459 us
  blocking collectives  218 us (47%)
  waiting for transfers between devices  196 us (43%)
  matrix products  18 us (4%)
  between operations  13.9 us (3%)
  local copies, waits for them, and re-layouts  11.7 us (3%)
    psum x1, blocking collectives, per_device(): lax.psum(jnp.sum(hidden.astype(jnp.float32) * raw_back, axis=1), 'dp')  121 us
    all_gather x1, waiting for transfers between devices, per_device(): lax.all_gather(jnp.take(every_act, picked, axis=0), 'dp', axis=1, tiled=T...  87.1 us
    all_gather x1, waiting for transfers between devices, per_device(): lax.all_gather(jnp.take(every_grad, picked, axis=0), 'dp', axis=1, tiled=...  83.2 us
    all_gather x1, blocking collectives, per_device(): lax.all_gather(out_grad, 'expert', axis=0, tiled=True)  33.9 us
    all_gather x1, blocking collectives, per_device(): lax.all_gather(activations, 'expert', axis=0, tiled=True)  32.9 us
    all_gather x1, blocking collectives, per_device(): expert_terms = lax.all_gather(summed[None], 'expert', axis=0, tiled=True)  30.3 us
    reduce_scatter x1, waiting for transfers between devices, input_sum(): lax.psum_scatter(contract(weight_in, preact_back, 1, 1), 'dp', scatter_di...  26 us
    dot_general x5, matrix products, contract(): lax.dot_general(left_operand, right_operand, (((left_axis,), (right_axis,...  11.5 us
  transfers between devices with their start and end apart: 3, of which 3 were waited for; matrix products, arithmetic and copies ran while one was open for 2% of the time, Pallas kernels for 0%

commit v1 on v0

v1 whole, which is shorter than its diff:
```python
import jax
import jax.numpy as jnp
import numpy as np
from jax import lax
from jax.experimental import pallas as pl
from jax.experimental.pallas import tpu as pltpu
from jax.sharding import PartitionSpec as P

GELU_SCALE = 0.7978845608
CUBIC_COEF = 0.044715

NY, NZ = 8, 4
NQ = NY // 2
VMEM_BYTES = 48 * 1024 * 1024
BF, F32 = jnp.bfloat16, jnp.float32


def dp_index(y, z, core):
    return (y * NZ + z) * 2 + core


INNER = [[dp_index(y, z, 0) for y in range(NY)] for z in range(NZ)] + [
    [dp_index(2 * q + p, z, 1) for p in range(2) for z in range(NZ)] for q in range(NQ)
]
OUTER = [[dp_index(y, z, 0) for z in range(NZ)] for y in range(NY)] + [
    [dp_index(2 * q + p, z, 1) for q in range(NQ)] for p in range(2) for z in range(NZ)
]
SWAP = [(d, d ^ 1) for d in range(NY * NZ * 2)]
SLOTS = [
    np.array([dp_index(i, o, 0) for o in range(NZ) for i in range(NY)], np.int32),
    np.array(
        [dp_index(2 * o + i // NZ, i % NZ, 1) for o in range(NQ) for i in range(8)],
        np.int32,
    ),
]


def gelu_parts(preact):
    inner = GELU_SCALE * (preact + CUBIC_COEF * preact * preact * preact)
    tanh_part = jnp.tanh(inner)
    gelu_val = 0.5 * preact * (1.0 + tanh_part)
    gelu_slope = 0.5 * (1.0 + tanh_part) + 0.5 * preact * (
        1.0 - tanh_part * tanh_part
    ) * GELU_SCALE * (1.0 + 3.0 * CUBIC_COEF * preact * preact)
    return gelu_val, gelu_slope


def contract(left, right, left_axis, right_axis):
    return lax.dot_general(
        left, right, (((left_axis,), (right_axis,)), ((), ())), preferred_element_type=F32
    )


def onehot(base, chosen_row, tokens):
    rows = chosen_row.shape[1]
    ids = base + lax.broadcasted_iota(jnp.int32, (tokens, rows), 0)
    return jnp.where(ids == chosen_row, 1.0, 0.0).astype(BF)


def hi_lo(value):
    high = value.astype(BF)
    low = (value - high.astype(F32)).astype(BF)
    return high, low


def pick_kernel(base_ref, act_ref, grad_ref, chosen_ref, out_ref):
    both = jnp.concatenate([act_ref[...], grad_ref[...]], axis=0)
    for e in range(out_ref.shape[0]):
        sel = onehot(base_ref[0], chosen_ref[e : e + 1, :], both.shape[1])
        out_ref[e] = contract(both, sel, 1, 0).astype(BF)


def merge_kernel(parts_ref, out_ref):
    total = parts_ref[0].astype(F32)
    for k in range(1, parts_ref.shape[0]):
        total = total + parts_ref[k].astype(F32)
    total = total.astype(BF)
    for k in range(out_ref.shape[0]):
        out_ref[k] = total


def main_kernel(
    slots_ref, own_ref, oth_ref, w_in_ref, w_out_ref, score_ref,
    gin_ref, gout_ref, keep_ref, send_ref, x_ref, u_ref,
):
    feats = own_ref.shape[2] // 2
    slots = own_ref.shape[0] * own_ref.shape[1]
    for half, ref in enumerate((own_ref, oth_ref)):
        for s in range(slots):
            at = pl.ds(pl.multiple_of(slots_ref[half * slots + s] * feats, feats), feats)
            o, i = s // ref.shape[1], s % ref.shape[1]
            x_ref[at, :] = ref[o, i, :feats, :]
            u_ref[at, :] = ref[o, i, feats:, :]
    preact = contract(w_in_ref[...], x_ref[...], 0, 0)
    raw = contract(w_out_ref[...], u_ref[...], 1, 0)
    val, slope = gelu_parts(preact)
    hidden = val.astype(BF).astype(F32)
    score = score_ref[...]
    gate = jnp.sum(hidden * raw, axis=0, keepdims=True)
    back = (score * raw * slope).astype(BF)
    scaled = (score * hidden).astype(BF)
    for half, ref in enumerate((keep_ref, send_ref)):
        for s in range(slots):
            at = pl.ds(pl.multiple_of(slots_ref[half * slots + s] * feats, feats), feats)
            ref[pl.ds(s * feats, feats), :] = contract(w_in_ref[at, :], back, 1, 0).astype(BF)
        high, low = hi_lo(gate)
        pad = jnp.zeros((14, gate.shape[1]), F32)
        tile = jnp.concatenate([high.astype(F32), low.astype(F32), pad], axis=0)
        ref[pl.ds(slots * feats, 16), :] = tile.astype(BF)
    gin_ref[...] = contract(x_ref[...], back, 1, 1).astype(BF)
    gout_ref[...] = contract(scaled, u_ref[...], 1, 1).astype(BF)


def pair_kernel(keep_ref, got_ref, out_ref):
    parts, rows = out_ref.shape[0], out_ref.shape[1] - 16
    base = parts * rows
    gates = keep_ref[pl.ds(base, 16), :].astype(F32), got_ref[pl.ds(base, 16), :].astype(F32)
    gate = (gates[0][0:1] + gates[0][1:2]) + (gates[1][0:1] + gates[1][1:2])
    high, low = hi_lo(gate)
    pad = jnp.zeros((14, gate.shape[1]), F32)
    tile = jnp.concatenate([high.astype(F32), low.astype(F32), pad], axis=0).astype(BF)
    for k in range(parts):
        at = pl.ds(k * rows, rows)
        out_ref[k, :rows, :] = (keep_ref[at, :].astype(F32) + got_ref[at, :].astype(F32)).astype(BF)
        out_ref[k, rows:, :] = tile


def outer_kernel(got_ref, out_ref):
    parts, rows = out_ref.shape[0], out_ref.shape[1] - 16
    sources, base = got_ref.shape[0], parts * rows
    gates = [got_ref[o, pl.ds(base, 16), :].astype(F32)[0:2] for o in range(sources)]
    pad = jnp.zeros((16 - 2 * sources, got_ref.shape[2]), F32)
    tile = jnp.concatenate(gates + [pad], axis=0).astype(BF)
    for k in range(parts):
        at = pl.ds(k * rows, rows)
        total = got_ref[0, at, :].astype(F32)
        for o in range(1, sources):
            total = total + got_ref[o, at, :].astype(F32)
        out_ref[k, :rows, :] = total.astype(BF)
        out_ref[k, rows:, :] = tile


def inner_kernel(core_ref, got_ref, out_ref, gate_ref):
    rows = out_ref.shape[1]
    sources = got_ref.shape[0]
    total = got_ref[0, :rows, :].astype(F32)
    for i in range(1, sources):
        total = total + got_ref[i, :rows, :].astype(F32)
    total = total.astype(BF)
    for k in range(out_ref.shape[0]):
        out_ref[k] = total
    tiles = [got_ref[i, rows:, :].astype(F32) for i in range(sources)]
    gates = [[t[2 * o : 2 * o + 1] + t[2 * o + 1 : 2 * o + 2] for o in range(NZ)] for t in tiles]
    first = core_ref[0] == 0
    gate = jnp.zeros((1, got_ref.shape[2]), F32)
    for y in range(NY):
        for z in range(NZ):
            gate = gate + jnp.where(first, gates[y][z], gates[(y % 2) * NZ + z][y // 2])
    gate_ref[...] = gate


def scatter_kernel(base_ref, terms_ref, chosen_ref, out_ref):
    tokens = out_ref.shape[1]
    total = jnp.zeros(out_ref.shape, F32)
    for e in range(terms_ref.shape[0]):
        sel = onehot(base_ref[0], chosen_ref[e : e + 1, :], tokens)
        total = total + contract(terms_ref[e], sel, 1, 1)
    out_ref[...] = total.astype(BF)


SMEM = pl.BlockSpec(memory_space=pltpu.SMEM)
VMEM = pl.BlockSpec(memory_space=pltpu.VMEM)


def call(kernel, specs, outs, *args, scratch=()):
    shapes = [jax.ShapeDtypeStruct(s, t) for s, t in outs]
    single = len(shapes) == 1
    return pl.pallas_call(
        kernel,
        out_shape=shapes[0] if single else shapes,
        in_specs=specs,
        out_specs=VMEM if single else [VMEM] * len(shapes),
        scratch_shapes=scratch,
        compiler_params=pltpu.CompilerParams(vmem_limit_bytes=VMEM_BYTES),
    )(*args)


def exchange(parts, axis, groups=None):
    return lax.all_to_all(parts, axis, 0, 0, axis_index_groups=groups)


def per_device(activations, out_grad, w_in, w_out, chosen, gate_scores):
    tokens, feats = activations.shape
    experts, rows = chosen.shape
    depth, units = w_in.shape[1], w_in.shape[2]
    base = (lax.axis_index("expert") * tokens).astype(jnp.int32).reshape(1)
    core = (lax.axis_index("dp") % 2).astype(jnp.int32).reshape(1)
    own = jnp.where(core == 0, jnp.asarray(SLOTS[0]), jnp.asarray(SLOTS[1]))
    oth = jnp.where(core == 0, jnp.asarray(SLOTS[1]), jnp.asarray(SLOTS[0]))
    slots = jnp.concatenate([own, oth])
    count = own.shape[0]

    picked = call(
        pick_kernel, [SMEM, VMEM, VMEM, VMEM], [((experts, 2 * feats, rows), BF)],
        base, activations.T, out_grad.T, chosen,
    )
    picked = exchange(picked, "expert")
    mine = call(merge_kernel, [VMEM], [((8, 2 * feats, rows), BF)], picked)
    inner = exchange(mine, "dp", INNER)
    outer = exchange(jnp.broadcast_to(inner[None], (4,) + inner.shape), "dp", OUTER)
    other = lax.ppermute(outer, "dp", SWAP)

    weight_in_grad, weight_out_grad, keep, send = call(
        main_kernel,
        [SMEM, VMEM, VMEM, VMEM, VMEM, VMEM],
        [
            ((depth, units), BF),
            ((units, depth), BF),
            ((count * feats + 16, rows), BF),
            ((count * feats + 16, rows), BF),
        ],
        slots, outer, other, w_in[0], w_out[0], gate_scores,
        scratch=[pltpu.VMEM((depth, rows), BF), pltpu.VMEM((depth, rows), BF)],
    )
    got = lax.ppermute(send, "dp", SWAP)
    part = call(pair_kernel, [VMEM, VMEM], [((4, 8 * feats + 16, rows), BF)], keep, got)
    part = exchange(part, "dp", OUTER)
    part = call(outer_kernel, [VMEM], [((8, feats + 16, rows), BF)], part)
    part = exchange(part, "dp", INNER)
    term, gate_grad = call(
        inner_kernel, [SMEM, VMEM], [((experts, feats, rows), BF), ((1, rows), F32)], core, part
    )
    terms = exchange(term, "expert")
    act_grad = call(
        scatter_kernel, [SMEM, VMEM, VMEM], [((feats, tokens), BF)], base, terms, chosen
    )
    return weight_in_grad[None], weight_out_grad[None], act_grad.T, gate_grad


def solution(mesh):
    return jax.shard_map(
        per_device,
        mesh=mesh,
        in_specs=(
            P("expert", "dp"),
            P("expert", "dp"),
            P("expert", None, "dp"),
            P("expert", "dp", None),
            P(),
            P("expert", None),
        ),
        out_specs=(
            P("expert", None, "dp"),
            P("expert", "dp", None),
            P("expert", "dp"),
            P("expert", None),
        ),
        check_vma=False,
    )
```

time: 459 us -> 144 us (0.31)
  the two profiles are of different devices: /device:TPU:16 before, /device:TPU:8 now
where the time goes in v1:
time: 144 us
  blocking collectives  120 us (83%)
  Pallas kernels  9.38 us (7%)
  waiting for transfers between devices  6.86 us (5%)
  starting transfers between devices  3.94 us (3%)
  local copies, waits for them, and re-layouts  2.65 us (2%)
    all_to_all x6, blocking collectives, exchange(): return lax.all_to_all(parts, axis, 0, 0, axis_index_groups=groups)  120 us
    pallas_call x7, Pallas kernels, call(): pl.pallas_call(kernel, out_shape=shapes[0] if single else shapes, in_spec...  9.38 us
    ppermute x1, waiting for transfers between devices, per_device(): other = lax.ppermute(outer, 'dp', SWAP)  4.35 us
  transfers between devices with their start and end apart: 2, of which 2 were waited for; matrix products, arithmetic and copies ran while one was open for 0% of the time, Pallas kernels for 0%

profile of v1, /device:TPU:8, one launch (start us, length us, event | category | flops | bytes accessed | tf_op | source)
XLA Modules:
  0.0 143.5 jit_solution(10825720215614090171)
XLA Ops:
  0.6 0.8 copy-done.2
  1.5 0.8 copy-done.3
  2.3 0.7 copy-done.4
  3.0 0.4 shard_map.111
  3.5 16.0 %all_to_all.30.parts_ref = bf16[8,128,256]{2,1,0:T(8,128)(2,1)S(1)} all-to-all(bf16[8,128,256]{2,1,0:T(8,128)(2,1)S(1)} %shard_map.111), channel_id=1, replica_groups=mesh['dp'=64,'expert'=8] {'expert'}, dimensions={0} | all-to-all | bytes 1048576 | tf_op jit(solution)/shard_map/all_to_all | solution.py:189
  19.5 0.1 shard_map.112
  19.6 21.2 %all_to_all.31 = bf16[8,128,256]{2,1,0:T(8,128)(2,1)S(1)} all-to-all(bf16[8,128,256]{2,1,0:T(8,128)(2,1)S(1)} %shard_map.112), channel_id=1, replica_groups={{0,64,128,192,256,320,384,448},{16,80,144,208,272,336,400,464},{32,96,1..., dimensions={0} | all-to-all | bytes 1048576 | tf_op jit(solution)/shard_map/all_to_all | solution.py:189
  40.7 0.2 broadcast_in_dim.27
  41.0 0.0 copy-start.7
  41.0 0.0 copy-start.8
  41.1 37.8 %all_to_all.32.own_ref = bf16[4,8,128,256]{3,2,1,0:T(8,128)(2,1)} all-to-all(bf16[4,8,128,256]{3,2,1,0:T(8,128)(2,1)S(1)} %broadcast_in_dim.27), channel_id=1, replica_groups={{0,16,32,48},{64,80,96,112},{128,144,160,176},{192,208,224,240},{256,27..., dimensions={0} | all-to-all | bytes 4194304 | tf_op jit(solution)/shard_map/all_to_all | solution.py:189
  78.9 1.9 %collective-permute-start = (bf16[4,8,128,256]{3,2,1,0:T(8,128)(2,1)}, bf16[4,8,128,256]{3,2,1,0:T(8,128)(2,1)}, u32[]{:S(2)}, u32[]{:S(2)}) collective-permute-start(bf16[4,8,128,256]{3,2,1,0:T(8,128)(2,1)} %all_to_all.32.own_ref), channel_id=1, source_target_pairs={{0,8},{8,0},{16,24},{24,16},{32,40},{40,32},{48,56},{56,48},{64,72... | collective-permute-start | bytes 6291464 | tf_op jit(solution)/shard_map/ppermute | solution.py:211
  80.9 0.1 pad_add_fusion.slots_ref
  80.9 4.3 %collective-permute-done.oth_ref = bf16[4,8,128,256]{3,2,1,0:T(8,128)(2,1)} collective-permute-done((bf16[4,8,128,256]{3,2,1,0:T(8,128)(2,1)}, bf16[4,8,128,256]{3,2,1,0:T(8,128)(2,1)}, u32[]{:S(2)}, u32[]{:S(2)}) %collective-permute-start) | collective-permute-done | bytes 2097184 | tf_op jit(solution)/shard_map/ppermute | solution.py:211
  85.3 6.5 %shard_map.113 = (bf16[4096,128]{1,0:T(8,128)(2,1)}, bf16[128,4096]{1,0:T(8,128)(2,1)}, bf16[2064,256]{1,0:T(8,128)(2,1)S(1)}, bf16[2064,256]{1,0:T(8,128)(2,1)S(1)}) custom-call(s32[64]{0:T(128)S(1)} %pad_add_fusion.slots_ref, bf16[4,8,128,256]{3,2,1,0:T(8,128)(2,1)} %all_to_all.32.own_ref, bf16[4,8,128,256]{3,2,1,0:T(8,128)(2,1)} %collective-permute-done.oth_ref, ...), custom_call_target="tpu_custom_call" | custom-call | tf_op jit(solution)/shard_map/pallas_call | solution.py:178
  91.8 2.0 %collective-permute-start.1 = (bf16[2064,256]{1,0:T(8,128)(2,1)S(1)}, bf16[2064,256]{1,0:T(8,128)(2,1)S(1)}, u32[]{:S(2)}, u32[]{:S(2)}) collective-permute-start(bf16[2064,256]{1,0:T(8,128)(2,1)S(1)} %get-tuple-element.13), channel_id=1, source_target_pairs={{0,8},{8,0},{16,24},{24,16},{32,40},{40,32},{48,56},{56,48},{64,72... | collective-permute-start | bytes 3170312 | tf_op jit(solution)/shard_map/ppermute | solution.py:225
  93.8 2.5 %collective-permute-done.1.got_ref = bf16[2064,256]{1,0:T(8,128)(2,1)S(1)} collective-permute-done((bf16[2064,256]{1,0:T(8,128)(2,1)S(1)}, bf16[2064,256]{1,0:T(8,128)(2,1)S(1)}, u32[]{:S(2)}, u32[]{:S(2)}) %collective-permute-start.1) | collective-permute-done | bytes 1056800 | tf_op jit(solution)/shard_map/ppermute | solution.py:225
  96.3 0.2 shard_map.114
  96.6 21.5 %all_to_all.33.got_ref = bf16[4,528,256]{2,1,0:T(8,128)(2,1)S(1)} all-to-all(bf16[4,528,256]{2,1,0:T(8,128)(2,1)S(1)} %shard_map.114), channel_id=1, replica_groups={{0,16,32,48},{64,80,96,112},{128,144,160,176},{192,208,224,240},{256,27..., dimensions={0} | all-to-all | bytes 2162688 | tf_op jit(solution)/shard_map/all_to_all | solution.py:189
  118.0 0.1 shard_map.115
  118.2 13.4 %all_to_all.34.got_ref = bf16[8,80,256]{2,1,0:T(8,128)(2,1)S(1)} all-to-all(bf16[8,80,256]{2,1,0:T(8,128)(2,1)S(1)} %shard_map.115), channel_id=1, replica_groups={{0,64,128,192,256,320,384,448},{16,80,144,208,272,336,400,464},{32,96,1..., dimensions={0} | all-to-all | bytes 655360 | tf_op jit(solution)/shard_map/all_to_all | solution.py:189
  131.6 0.6 shard_map.116
  132.2 9.9 %all_to_all.35.terms_ref = bf16[8,64,256]{2,1,0:T(8,128)(2,1)S(1)} all-to-all(bf16[8,64,256]{2,1,0:T(8,128)(2,1)S(1)} %get-tuple-element.14), channel_id=1, replica_groups=mesh['dp'=64,'expert'=8] {'expert'}, dimensions={0} | all-to-all | bytes 524288 | tf_op jit(solution)/shard_map/all_to_all | solution.py:189
  142.1 1.4 shard_map.117
  (14 shorter events, 0.0 us)
Async XLA Ops:
  0.6 0.8 copy-start.2
  1.5 0.8 copy-start.3
  2.3 0.7 copy-start.4
  41.0 39.8 %copy-start.7 = (s32[32]{0:T(128)S(1)}, s32[32]{0:T(128)}, u32[]{:S(2)}) copy-start(s32[32]{0:T(128)} %constant.31.clone) | copy-start | bytes 388
  41.0 39.8 %copy-start.8 = (s32[32]{0:T(128)S(1)}, s32[32]{0:T(128)}, u32[]{:S(2)}) copy-start(s32[32]{0:T(128)} %constant.30.clone) | copy-start | bytes 388
  41.0 44.3 %copy-start = (bf16[1,4096,128]{2,1,0:T(8,128)(2,1)S(1)}, bf16[1,4096,128]{2,1,0:T(8,128)(2,1)}, u32[]{:S(2)}) copy-start(bf16[1,4096,128]{2,1,0:T(8,128)(2,1)} %param.10) | copy-start | bytes 3145732
  41.0 44.3 %copy-start.1 = (bf16[1,128,4096]{2,1,0:T(8,128)(2,1)S(1)}, bf16[1,128,4096]{2,1,0:T(8,128)(2,1)}, u32[]{:S(2)}) copy-start(bf16[1,128,4096]{2,1,0:T(8,128)(2,1)} %param.11) | copy-start | bytes 3145732
  41.0 44.2 %copy-start.6 = (f32[1,256]{1,0:T(1,128)S(1)}, f32[1,256]{1,0:T(1,128)}, u32[]{:S(2)}) copy-start(f32[1,256]{1,0:T(1,128)} %score_ref.1) | copy-start | bytes 3076
  78.9 6.4 %collective-permute-start = (bf16[4,8,128,256]{3,2,1,0:T(8,128)(2,1)}, bf16[4,8,128,256]{3,2,1,0:T(8,128)(2,1)}, u32[]{:S(2)}, u32[]{:S(2)}) collective-permute-start(bf16[4,8,128,256]{3,2,1,0:T(8,128)(2,1)} %all_to_all.32.own_ref), channel_id=1, source_target_pairs={{0,8},{8,0},{16,24},{24,16},{32,40},{40,32},{48,56},{56,48},{64,72... | collective-permute-start | bytes 6291464 | tf_op jit(solution)/shard_map/ppermute | solution.py:211
  91.8 4.6 %collective-permute-start.1 = (bf16[2064,256]{1,0:T(8,128)(2,1)S(1)}, bf16[2064,256]{1,0:T(8,128)(2,1)S(1)}, u32[]{:S(2)}, u32[]{:S(2)}) collective-permute-start(bf16[2064,256]{1,0:T(8,128)(2,1)S(1)} %get-tuple-element.13), channel_id=1, source_target_pairs={{0,8},{8,0},{16,24},{24,16},{32,40},{40,32},{48,56},{56,48},{64,72... | collective-permute-start | bytes 3170312 | tf_op jit(solution)/shard_map/ppermute | solution.py:225
  118.2 23.9 %copy-start.5 = (s32[8,256]{1,0:T(8,128)S(1)}, s32[8,256]{1,0:T(8,128)}, u32[]{:S(2)}) copy-start(s32[8,256]{1,0:T(8,128)} %chosen_ref.3) | copy-start | bytes 24580

commit v2 on v1

v2 whole, which is shorter than its diff:
```python
import jax
import jax.numpy as jnp
from jax import lax
from jax.experimental import pallas as pl
from jax.experimental.pallas import tpu as pltpu
from jax.sharding import PartitionSpec as P

GELU_SCALE = 0.7978845608
CUBIC_COEF = 0.044715

NY, NZ = 8, 4
MIB = 1024 * 1024
BF, F32 = jnp.bfloat16, jnp.float32


def dp_index(y, z, core):
    return (y * NZ + z) * 2 + core


INNER = [[dp_index(y, z, 0) for y in range(NY)] for z in range(NZ)] + [
    [dp_index(4 * h + q, z, 1) for h in range(2) for z in range(NZ)] for q in range(4)
]
OUTER = [[dp_index(y, z, 0) for z in range(NZ)] for y in range(NY)] + [
    [dp_index(4 * h + q, z, 1) for q in range(4)] for h in range(2) for z in range(NZ)
]
SHIFTS = [
    [(g[j], g[(j + k) % 4]) for g in OUTER for j in range(4)] for k in range(4)
]
SWAP = [(d, d ^ 1) for d in range(NY * NZ * 2)]


def gelu_parts(preact):
    inner = GELU_SCALE * (preact + CUBIC_COEF * preact * preact * preact)
    tanh_part = jnp.tanh(inner)
    gelu_val = 0.5 * preact * (1.0 + tanh_part)
    gelu_slope = 0.5 * (1.0 + tanh_part) + 0.5 * preact * (
        1.0 - tanh_part * tanh_part
    ) * GELU_SCALE * (1.0 + 3.0 * CUBIC_COEF * preact * preact)
    return gelu_val, gelu_slope


def contract(left, right, left_axis, right_axis):
    return lax.dot_general(
        left, right, (((left_axis,), (right_axis,)), ((), ())), preferred_element_type=F32
    )


def onehot(base, chosen_row, tokens):
    rows = chosen_row.shape[1]
    ids = base + lax.broadcasted_iota(jnp.int32, (tokens, rows), 0)
    return jnp.where(ids == chosen_row, 1.0, 0.0).astype(BF)


def hi_lo(value):
    high = value.astype(BF)
    low = (value - high.astype(F32)).astype(BF)
    return high, low


def pick_kernel(
    base_ref, act_hbm, grad_hbm, chosen_hbm, out_ref, sel_ref, both_ref, chosen_ref, sems
):
    feats = act_hbm.shape[0]
    copies = [
        pltpu.make_async_copy(act_hbm, both_ref.at[pl.ds(0, feats)], sems.at[0]),
        pltpu.make_async_copy(grad_hbm, both_ref.at[pl.ds(feats, feats)], sems.at[1]),
        pltpu.make_async_copy(chosen_hbm, chosen_ref, sems.at[2]),
    ]
    for copy in copies:
        copy.start()
    for copy in copies:
        copy.wait()
    both = both_ref[...]
    for e in range(out_ref.shape[0]):
        sel = onehot(base_ref[0], chosen_ref[e : e + 1, :], both.shape[1])
        sel_ref[e] = sel
        out_ref[e] = contract(both, sel, 1, 0).astype(BF)


def merge_kernel(parts_ref, out_ref):
    total = parts_ref[0].astype(F32)
    for k in range(1, parts_ref.shape[0]):
        total = total + parts_ref[k].astype(F32)
    total = total.astype(BF)
    for k in range(out_ref.shape[0]):
        out_ref[k] = total


def gate_tile(pairs):
    rows = [half.astype(F32) for pair in pairs for half in pair]
    rows.append(jnp.zeros((16 - len(rows), rows[0].shape[1]), F32))
    return jnp.concatenate(rows, axis=0).astype(BF)


def block_rows(slots_ref, slot, feats):
    return pl.ds(pl.multiple_of(slots_ref[slot] * feats, feats), feats)


def main_kernel(slots_ref, *refs):
    parts, (w_in_ref, w_out_ref, score_ref) = refs[:8], refs[8:11]
    x_ref, u_ref, back_ref, scaled_ref, gate_ref, send_ref = refs[11:17]
    w_out_held, x_sem, u_sem, w_sem = refs[17:]
    weights = pltpu.make_async_copy(w_out_ref, w_out_held, w_sem)
    inner, feats = parts[0].shape[0], parts[0].shape[1] // 2
    for k, ref in enumerate(parts):
        for i in range(inner):
            at = block_rows(slots_ref, k * inner + i, feats)
            pltpu.make_async_copy(ref.at[i, pl.ds(0, feats)], x_ref.at[at], x_sem).start()
            pltpu.make_async_copy(ref.at[i, pl.ds(feats, feats)], u_ref.at[at], u_sem).start()
    weights.start()
    pltpu.make_async_copy(x_ref, x_ref, x_sem).wait()
    preact = contract(w_in_ref[...], x_ref[...], 0, 0)
    pltpu.make_async_copy(u_ref, u_ref, u_sem).wait()
    weights.wait()
    raw = contract(w_out_held[...], u_ref[...], 1, 0)
    val, slope = gelu_parts(preact)
    hidden = val.astype(BF).astype(F32)
    score = score_ref[...]
    gate = jnp.sum(hidden * raw, axis=0, keepdims=True)
    back = (score * raw * slope).astype(BF)
    back_ref[...] = back
    scaled_ref[...] = (score * hidden).astype(BF)
    gate_ref[...] = gate
    count = send_ref.shape[0] // feats
    for s in range(count):
        at = block_rows(slots_ref, 8 * inner + s, feats)
        send_ref[pl.ds(s * feats, feats), :] = contract(w_in_ref[at, :], back, 1, 0).astype(BF)
    send_ref[pl.ds(count * feats, 16), :] = gate_tile([hi_lo(gate)])


def weight_kernel(x_ref, u_ref, back_ref, scaled_ref, gin_ref, gout_ref):
    gin_ref[...] = contract(x_ref[...], back_ref[...], 1, 1).astype(BF)
    gout_ref[...] = contract(scaled_ref[...], u_ref[...], 1, 1).astype(BF)


def pair_kernel(slots_ref, w_in_ref, back_ref, gate_ref, got_ref, *outs):
    rows = outs[0].shape[0] - 16
    feats = rows // 8
    tile = got_ref[pl.ds(len(outs) * rows, 16), :].astype(F32)
    high, low = hi_lo(gate_ref[...])
    gate = (high.astype(F32) + low.astype(F32)) + (tile[0:1] + tile[1:2])
    packed = gate_tile([hi_lo(gate)])
    back = back_ref[...]
    for k, ref in enumerate(outs):
        for i in range(8):
            s = k * 8 + i
            mine = contract(w_in_ref[block_rows(slots_ref, s, feats), :], back, 1, 0)
            other = got_ref[pl.ds(s * feats, feats), :].astype(F32)
            ref[pl.ds(i * feats, feats), :] = (mine + other).astype(BF)
        ref[pl.ds(rows, 16), :] = packed


def outer_kernel(place_ref, *refs):
    parts, out_ref = refs[:4], refs[4]
    count, rows = out_ref.shape[0], out_ref.shape[1] - 16
    base = count * rows
    tiles = [ref[pl.ds(base, 16), :].astype(F32) for ref in parts]
    pairs = []
    for o in range(4):
        source = (place_ref[0] + 4 - o) % 4
        pair = tiles[0]
        for k in range(1, 4):
            pair = jnp.where(source == k, tiles[k], pair)
        pairs.append((pair[0:1], pair[1:2]))
    packed = gate_tile(pairs)
    for i in range(count):
        at = pl.ds(i * rows, rows)
        total = parts[0][at, :].astype(F32)
        for k in range(1, 4):
            total = total + parts[k][at, :].astype(F32)
        out_ref[i, :rows, :] = total.astype(BF)
        out_ref[i, rows:, :] = packed


def inner_kernel(core_ref, got_ref, out_ref, gate_ref):
    rows = out_ref.shape[1]
    sources = got_ref.shape[0]
    total = got_ref[0, :rows, :].astype(F32)
    for i in range(1, sources):
        total = total + got_ref[i, :rows, :].astype(F32)
    total = total.astype(BF)
    for k in range(out_ref.shape[0]):
        out_ref[k] = total
    tiles = [got_ref[i, rows:, :].astype(F32) for i in range(sources)]
    gates = [[t[2 * o : 2 * o + 1] + t[2 * o + 1 : 2 * o + 2] for o in range(4)] for t in tiles]
    first = core_ref[0] == 0
    gate = jnp.zeros((1, got_ref.shape[2]), F32)
    for y in range(NY):
        for z in range(NZ):
            gate = gate + jnp.where(first, gates[y][z], gates[(y // 4) * NZ + z][y % 4])
    gate_ref[...] = gate


def scatter_kernel(terms_ref, sel_ref, out_ref):
    total = jnp.zeros(out_ref.shape, F32)
    for e in range(terms_ref.shape[0]):
        total = total + contract(terms_ref[e], sel_ref[e], 1, 1)
    out_ref[...] = total.astype(BF)


SMEM = pl.BlockSpec(memory_space=pltpu.SMEM)
VMEM = pl.BlockSpec(memory_space=pltpu.VMEM)
HBM = pl.BlockSpec(memory_space=pltpu.HBM)


def call(kernel, specs, outs, *args, scratch=(), mib=16, flops=0, moved=0):
    shapes = [jax.ShapeDtypeStruct(s, t) for s, t in outs]
    single = len(shapes) == 1
    return pl.pallas_call(
        kernel,
        out_shape=shapes[0] if single else shapes,
        in_specs=specs,
        out_specs=VMEM if single else [VMEM] * len(shapes),
        scratch_shapes=scratch,
        cost_estimate=pl.CostEstimate(flops=flops, bytes_accessed=moved, transcendentals=0),
        compiler_params=pltpu.CompilerParams(vmem_limit_bytes=mib * MIB),
    )(*args)


def in_hbm(value):
    return pltpu.with_memory_space_constraint(value, pltpu.HBM)


def exchange(parts, axis, groups=None):
    return lax.all_to_all(parts, axis, 0, 0, axis_index_groups=groups)


def block_table(core, place):
    o = place[:, None]
    i = jnp.arange(8, dtype=jnp.int32)[None, :]
    zero = dp_index(i, o, 0)
    one = dp_index(4 * (i // NZ) + o, i % NZ, 1)
    return jnp.where(core == 0, zero, one).reshape(-1)


def per_device(activations, out_grad, w_in, w_out, chosen, gate_scores):
    tokens, feats = activations.shape
    experts, rows = chosen.shape
    depth, units = w_in.shape[1], w_in.shape[2]
    base = (lax.axis_index("expert") * tokens).astype(jnp.int32).reshape(1)
    index = lax.axis_index("dp").astype(jnp.int32)
    core, z, y = index & 1, (index >> 1) & (NZ - 1), index >> 3
    place = jnp.where(core == 0, z, y & 3)
    other_place = jnp.where(core == 0, y & 3, z)
    steps = jnp.arange(4, dtype=jnp.int32)
    gathered = jnp.concatenate(
        [
            block_table(core, (place - steps) & 3),
            block_table(1 - core, (other_place - steps) & 3),
            block_table(1 - core, (other_place + steps) & 3),
        ]
    )
    summed = block_table(core, (place + steps) & 3)
    count = summed.shape[0]

    picked, sel = call(
        pick_kernel,
        [SMEM, HBM, HBM, HBM],
        [((experts, 2 * feats, rows), BF), ((experts, tokens, rows), BF)],
        base, in_hbm(activations.T), in_hbm(out_grad.T), in_hbm(chosen),
        scratch=[
            pltpu.VMEM((2 * feats, tokens), BF),
            pltpu.VMEM((experts, rows), jnp.int32),
            pltpu.SemaphoreType.DMA((3,)),
        ],
    )
    picked = exchange(picked, "expert")
    mine = call(merge_kernel, [VMEM], [((8, 2 * feats, rows), BF)], picked)
    own = exchange(mine, "dp", INNER)
    blocks = [own] + [lax.ppermute(own, "dp", SHIFTS[k]) for k in (1, 2, 3)]
    blocks += [lax.ppermute(block, "dp", SWAP) for block in blocks]

    x, u, back, scaled, gate, send = call(
        main_kernel,
        [SMEM] + [HBM] * 8 + [VMEM, HBM, VMEM],
        [
            ((depth, rows), BF),
            ((depth, rows), BF),
            ((units, rows), BF),
            ((units, rows), BF),
            ((1, rows), F32),
            ((count * feats + 16, rows), BF),
        ],
        gathered, *blocks, w_in[0], in_hbm(w_out[0]), gate_scores, mib=24,
        scratch=[pltpu.VMEM((units, depth), BF)] + [pltpu.SemaphoreType.DMA] * 3,
    )
    got = lax.ppermute(send, "dp", SWAP)
    weight_in_grad, weight_out_grad = call(
        weight_kernel,
        [VMEM] * 4,
        [((depth, units), BF), ((units, depth), BF)],
        x, u, back, scaled, flops=4 * depth * units * rows, moved=6 * depth * rows,
    )
    parts = call(
        pair_kernel,
        [SMEM] + [VMEM] * 4,
        [((8 * feats + 16, rows), BF)] * 4,
        summed, w_in[0], back, gate, got,
    )
    parts = [parts[0]] + [lax.ppermute(parts[k], "dp", SHIFTS[k]) for k in (1, 2, 3)]
    part = call(
        outer_kernel, [SMEM] + [VMEM] * 4, [((8, feats + 16, rows), BF)],
        place.reshape(1), *parts,
    )
    part = exchange(part, "dp", INNER)
    term, gate_grad = call(
        inner_kernel, [SMEM, VMEM], [((experts, feats, rows), BF), ((1, rows), F32)],
        core.reshape(1), part,
    )
    terms = exchange(term, "expert")
    act_grad = call(scatter_kernel, [VMEM, VMEM], [((feats, tokens), BF)], terms, sel)
    return weight_in_grad[None], weight_out_grad[None], act_grad.T, gate_grad


def solution(mesh):
    return jax.shard_map(
        per_device,
        mesh=mesh,
        in_specs=(
            P("expert", "dp"),
            P("expert", "dp"),
            P("expert", None, "dp"),
            P("expert", "dp", None),
            P(),
            P("expert", None),
        ),
        out_specs=(
            P("expert", None, "dp"),
            P("expert", "dp", None),
            P("expert", "dp"),
            P("expert", None),
        ),
        check_vma=False,
    )
```

time: 144 us -> 153 us (1.062); the launches traced: 144 us -> 150 us
  blocking collectives: 120 us -> 49.8 us
  starting transfers between devices: 3.94 us -> 47.6 us
  waiting for transfers between devices: 6.86 us -> 32.2 us
  Pallas kernels: 9.38 us -> 13.7 us
  local copies, waits for them, and re-layouts: 2.65 us -> 6.13 us
    all_to_all x6 -> x3, blocking collectives: 120 us -> 49.8 us  [exchange(): return lax.all_to_all(parts, axis, 0, 0, axis_index_groups=groups)]
    ppermute x1 -> x10, starting transfers between devices: 1.91 us -> 42.2 us  [the longest x3 20.1 us: per_device(): blocks = [own] + [lax.ppermute(own, 'dp', SHIFTS[k]) for k in (1, 2, 3)]]
    ppermute x1 -> x10, waiting for transfers between devices: 4.35 us -> 27.9 us  [the longest x3 15.7 us: per_device(): blocks = [own] + [lax.ppermute(own, 'dp', SHIFTS[k]) for k in (1, 2, 3)]]
    pallas_call x7 -> x8, Pallas kernels: 9.38 us -> 13.7 us  [call(): pl.pallas_call(kernel, out_shape=shapes[0] if single else shapes, in_spec...]
    all_to_all x0 -> x1, starting transfers between devices: none -> 3.41 us  [exchange(): return lax.all_to_all(parts, axis, 0, 0, axis_index_groups=groups)]
    unnamed x18 -> x12, local copies, waits for them, and re-layouts: 2.41 us -> 5.8 us
  transfers between devices with their start and end apart: 2 -> 12, of which waited for: 2 -> 6; matrix products, arithmetic and copies ran while one was open for 0% -> 0% of each run, Pallas kernels for 0% -> 2%
where the time goes in v2:
time: 153 us; the launch traced here: 150 us
  blocking collectives  49.8 us (33%)
  starting transfers between devices  47.6 us (31%)
  waiting for transfers between devices  32.2 us (21%)
  Pallas kernels  13.7 us (9%)
  local copies, waits for them, and re-layouts  6.13 us (4%)
    all_to_all x3, blocking collectives, exchange(): return lax.all_to_all(parts, axis, 0, 0, axis_index_groups=groups)  49.8 us
    ppermute x3, starting transfers between devices, per_device(): blocks = [own] + [lax.ppermute(own, 'dp', SHIFTS[k]) for k in (1, 2, 3)]  20.1 us
    ppermute x3, waiting for transfers between devices, per_device(): blocks = [own] + [lax.ppermute(own, 'dp', SHIFTS[k]) for k in (1, 2, 3)]  15.7 us
    ppermute x3, starting transfers between devices, per_device(): lax.ppermute(parts[k], 'dp', SHIFTS[k])  13.9 us
    pallas_call x8, Pallas kernels, call(): pl.pallas_call(kernel, out_shape=shapes[0] if single else shapes, in_spec...  13.7 us
    ppermute x3, waiting for transfers between devices, per_device(): lax.ppermute(parts[k], 'dp', SHIFTS[k])  10.4 us
    ppermute x4, starting transfers between devices, per_device(): blocks += [lax.ppermute(block, 'dp', SWAP) for block in blocks]  8.16 us
    unnamed x12, local copies, waits for them, and re-layouts  5.8 us
  transfers between devices with their start and end apart: 12, of which 6 were waited for; matrix products, arithmetic and copies ran while one was open for 0% of the time, Pallas kernels for 2%

profile of v2, /device:TPU:8, one launch (start us, length us, event | category | flops | bytes accessed | tf_op | source)
XLA Modules:
  0.0 150.5 jit_solution(7202185830221414906)
XLA Ops:
  2.2 16.0 %all_to_all.20.parts_ref = bf16[8,128,256]{2,1,0:T(8,128)(2,1)S(1)} all-to-all(bf16[8,128,256]{2,1,0:T(8,128)(2,1)S(1)} %get-tuple-element.20), channel_id=1, replica_groups=mesh['dp'=64,'expert'=8] {'expert'}, dimensions={0} | all-to-all | bytes 1048576 | tf_op jit(solution)/shard_map/all_to_all | solution.py:225
  18.3 20.6 %all_to_all.21.refs_0_ = bf16[8,128,256]{2,1,0:T(8,128)(2,1)} all-to-all(bf16[8,128,256]{2,1,0:T(8,128)(2,1)S(1)} %shard_map.94), channel_id=1, replica_groups={{0,64,128,192,256,320,384,448},{16,80,144,208,272,336,400,464},{32,96,1..., dimensions={0} | all-to-all | bytes 1048576 | tf_op jit(solution)/shard_map/all_to_all | solution.py:225
  38.9 13.9 %collective-permute-start.2 = (bf16[8,128,256]{2,1,0:T(8,128)(2,1)}, bf16[8,128,256]{2,1,0:T(8,128)(2,1)}, u32[]{:S(2)}, u32[]{:S(2)}) collective-permute-start(bf16[8,128,256]{2,1,0:T(8,128)(2,1)} %all_to_all.21.refs_0_), channel_id=1, source_target_pairs={{0,48},{16,0},{32,16},{48,32},{64,112},{80,64},{96,80},{112,96},{1... | collective-permute-start | bytes 1572872 | tf_op jit(solution)/shard_map/ppermute | solution.py:270
  52.8 1.9 %collective-permute-start.1 = (bf16[8,128,256]{2,1,0:T(8,128)(2,1)}, bf16[8,128,256]{2,1,0:T(8,128)(2,1)}, u32[]{:S(2)}, u32[]{:S(2)}) collective-permute-start(bf16[8,128,256]{2,1,0:T(8,128)(2,1)} %all_to_all.21.refs_0_), channel_id=1, source_target_pairs={{0,32},{16,48},{32,0},{48,16},{64,96},{80,112},{96,64},{112,80},{1... | collective-permute-start | bytes 1572872 | tf_op jit(solution)/shard_map/ppermute | solution.py:270
  54.8 4.3 %collective-permute-start = (bf16[8,128,256]{2,1,0:T(8,128)(2,1)}, bf16[8,128,256]{2,1,0:T(8,128)(2,1)}, u32[]{:S(2)}, u32[]{:S(2)}) collective-permute-start(bf16[8,128,256]{2,1,0:T(8,128)(2,1)} %all_to_all.21.refs_0_), channel_id=1, source_target_pairs={{0,16},{16,32},{32,48},{48,0},{64,80},{80,96},{96,112},{112,64},{1... | collective-permute-start | bytes 1572872 | tf_op jit(solution)/shard_map/ppermute | solution.py:270
  59.1 1.9 %collective-permute-start.3 = (bf16[8,128,256]{2,1,0:T(8,128)(2,1)}, bf16[8,128,256]{2,1,0:T(8,128)(2,1)}, u32[]{:S(2)}, u32[]{:S(2)}) collective-permute-start(bf16[8,128,256]{2,1,0:T(8,128)(2,1)} %all_to_all.21.refs_0_), channel_id=1, source_target_pairs={{0,8},{8,0},{16,24},{24,16},{32,40},{40,32},{48,56},{56,48},{64,72... | collective-permute-start | bytes 1572872 | tf_op jit(solution)/shard_map/ppermute | solution.py:271
  61.0 15.7 %collective-permute-done.2.refs_3_ = bf16[8,128,256]{2,1,0:T(8,128)(2,1)} collective-permute-done((bf16[8,128,256]{2,1,0:T(8,128)(2,1)}, bf16[8,128,256]{2,1,0:T(8,128)(2,1)}, u32[]{:S(2)}, u32[]{:S(2)}) %collective-permute-start.2) | collective-permute-done | bytes 524320 | tf_op jit(solution)/shard_map/ppermute | solution.py:270
  76.7 1.9 %collective-permute-start.6 = (bf16[8,128,256]{2,1,0:T(8,128)(2,1)}, bf16[8,128,256]{2,1,0:T(8,128)(2,1)}, u32[]{:S(2)}, u32[]{:S(2)}) collective-permute-start(bf16[8,128,256]{2,1,0:T(8,128)(2,1)} %collective-permute-done.2.refs_3_), channel_id=1, source_target_pairs={{0,8},{8,0},{16,24},{24,16},{32,40},{40,32},{48,56},{56,48},{64,72... | collective-permute-start | bytes 1572872 | tf_op jit(solution)/shard_map/ppermute | solution.py:271
  78.6 2.4 %collective-permute-start.5 = (bf16[8,128,256]{2,1,0:T(8,128)(2,1)}, bf16[8,128,256]{2,1,0:T(8,128)(2,1)}, u32[]{:S(2)}, u32[]{:S(2)}) collective-permute-start(bf16[8,128,256]{2,1,0:T(8,128)(2,1)} %collective-permute-done.1.refs_2_), channel_id=1, source_target_pairs={{0,8},{8,0},{16,24},{24,16},{32,40},{40,32},{48,56},{56,48},{64,72... | collective-permute-start | bytes 1572872 | tf_op jit(solution)/shard_map/ppermute | solution.py:271
  81.1 1.9 %collective-permute-start.4 = (bf16[8,128,256]{2,1,0:T(8,128)(2,1)}, bf16[8,128,256]{2,1,0:T(8,128)(2,1)}, u32[]{:S(2)}, u32[]{:S(2)}) collective-permute-start(bf16[8,128,256]{2,1,0:T(8,128)(2,1)} %collective-permute-done.refs_1_), channel_id=1, source_target_pairs={{0,8},{8,0},{16,24},{24,16},{32,40},{40,32},{48,56},{56,48},{64,72... | collective-permute-start | bytes 1572872 | tf_op jit(solution)/shard_map/ppermute | solution.py:271
  83.5 1.8 %collective-permute-done.4.refs_5_ = bf16[8,128,256]{2,1,0:T(8,128)(2,1)} collective-permute-done((bf16[8,128,256]{2,1,0:T(8,128)(2,1)}, bf16[8,128,256]{2,1,0:T(8,128)(2,1)}, u32[]{:S(2)}, u32[]{:S(2)}) %collective-permute-start.4) | collective-permute-done | bytes 524320 | tf_op jit(solution)/shard_map/ppermute | solution.py:271
  85.2 5.5 %shard_map.95 = (bf16[4096,256]{1,0:T(8,128)(2,1)S(1)}, bf16[4096,256]{1,0:T(8,128)(2,1)S(1)}, bf16[128,256]{1,0:T(8,128)(2,1)S(1)}, bf16[128,256]{1,0:T(8,128)(...) custom-call(s32[96]{0:T(128)S(1)} %pad_add_fusion.slots_ref, bf16[8,128,256]{2,1,0:T(8,128)(2,1)} %all_to_all.21.refs_0_, ...), custom_call_target="tpu_custom_call" | custom-call | tf_op jit(solution)/shard_map/pallas_call | solution.py:209
  93.4 2.0 %collective-permute-start.7 = (bf16[2064,256]{1,0:T(8,128)(2,1)}, bf16[2064,256]{1,0:T(8,128)(2,1)}, u32[]{:S(2)}, u32[]{:S(2)}) collective-permute-start(bf16[2064,256]{1,0:T(8,128)(2,1)} %get-tuple-element.28), channel_id=1, source_target_pairs={{0,8},{8,0},{16,24},{24,16},{32,40},{40,32},{48,56},{56,48},{64,72... | collective-permute-start | bytes 3170312 | tf_op jit(solution)/shard_map/ppermute | solution.py:287
  95.5 2.8 %collective-permute-done.7.got_ref = bf16[2064,256]{1,0:T(8,128)(2,1)} collective-permute-done((bf16[2064,256]{1,0:T(8,128)(2,1)}, bf16[2064,256]{1,0:T(8,128)(2,1)}, u32[]{:S(2)}, u32[]{:S(2)}) %collective-permute-start.7) | collective-permute-done | bytes 1056800 | tf_op jit(solution)/shard_map/ppermute | solution.py:287
  98.3 1.7 %shard_map.97 = (bf16[528,256]{1,0:T(8,128)(2,1)S(1)}, bf16[528,256]{1,0:T(8,128)(2,1)S(1)}, bf16[528,256]{1,0:T(8,128)(2,1)S(1)}, bf16[528,256]{1,0:T(8,128)(2,1)S(1)}) custom-call(s32[32]{0:T(128)S(1)} %reshape.174.slots_ref, bf16[4096,128]{1,0:T(8,128)(2,1)S(1)} %bitcast.11, bf16[128,256]{1,0:T(8,128)(2,1)S(1)} %get-tuple-element.23.back_ref, ...), custom_call_target="tpu_custom_call" | custom-call | tf_op jit(solution)/shard_map/pallas_call | solution.py:209
  100.0 1.9 %collective-permute-start.8 = (bf16[528,256]{1,0:T(8,128)(2,1)S(1)}, bf16[528,256]{1,0:T(8,128)(2,1)S(1)}, u32[]{:S(2)}, u32[]{:S(2)}) collective-permute-start(bf16[528,256]{1,0:T(8,128)(2,1)S(1)} %get-tuple-element.30), channel_id=1, source_target_pairs={{0,16},{16,32},{32,48},{48,0},{64,80},{80,96},{96,112},{112,64},{1... | collective-permute-start | bytes 811016 | tf_op jit(solution)/shard_map/ppermute | solution.py:300
  101.9 8.8 %collective-permute-start.9 = (bf16[528,256]{1,0:T(8,128)(2,1)S(1)}, bf16[528,256]{1,0:T(8,128)(2,1)S(1)}, u32[]{:S(2)}, u32[]{:S(2)}) collective-permute-start(bf16[528,256]{1,0:T(8,128)(2,1)S(1)} %get-tuple-element.31), channel_id=1, source_target_pairs={{0,32},{16,48},{32,0},{48,16},{64,96},{80,112},{96,64},{112,80},{1... | collective-permute-start | bytes 811016 | tf_op jit(solution)/shard_map/ppermute | solution.py:300
  110.7 3.2 %collective-permute-start.10 = (bf16[528,256]{1,0:T(8,128)(2,1)S(1)}, bf16[528,256]{1,0:T(8,128)(2,1)S(1)}, u32[]{:S(2)}, u32[]{:S(2)}) collective-permute-start(bf16[528,256]{1,0:T(8,128)(2,1)S(1)} %get-tuple-element.32), channel_id=1, source_target_pairs={{0,48},{16,0},{32,16},{48,32},{64,112},{80,64},{96,80},{112,96},{1... | collective-permute-start | bytes 811016 | tf_op jit(solution)/shard_map/ppermute | solution.py:300
  113.9 8.0 %collective-permute-done.9.refs_2_ = bf16[528,256]{1,0:T(8,128)(2,1)S(1)} collective-permute-done((bf16[528,256]{1,0:T(8,128)(2,1)S(1)}, bf16[528,256]{1,0:T(8,128)(2,1)S(1)}, u32[]{:S(2)}, u32[]{:S(2)}) %collective-permute-start.9) | collective-permute-done | bytes 270368 | tf_op jit(solution)/shard_map/ppermute | solution.py:300
  121.9 2.4 %collective-permute-done.10.refs_3_ = bf16[528,256]{1,0:T(8,128)(2,1)S(1)} collective-permute-done((bf16[528,256]{1,0:T(8,128)(2,1)S(1)}, bf16[528,256]{1,0:T(8,128)(2,1)S(1)}, u32[]{:S(2)}, u32[]{:S(2)}) %collective-permute-start.10) | collective-permute-done | bytes 270368 | tf_op jit(solution)/shard_map/ppermute | solution.py:300
  124.5 13.2 %all_to_all.22.got_ref = bf16[8,80,256]{2,1,0:T(8,128)(2,1)S(1)} all-to-all(bf16[8,80,256]{2,1,0:T(8,128)(2,1)S(1)} %shard_map.98), channel_id=1, replica_groups={{0,64,128,192,256,320,384,448},{16,80,144,208,272,336,400,464},{32,96,1..., dimensions={0} | all-to-all | bytes 655360 | tf_op jit(solution)/shard_map/all_to_all | solution.py:225
  138.4 3.4 %all-to-all-start.3 = ((bf16[8,64,256]{2,1,0:T(8,128)(2,1)}), bf16[8,64,256]{2,1,0:T(8,128)(2,1)S(1)}, u32[]{:S(2)}, u32[]{:S(2)}) async-start(bf16[8,64,256]{2,1,0:T(8,128)(2,1)} %get-tuple-element.33), calls=%async_computation.3 | async-start | bytes 524288 | tf_op jit(solution)/shard_map/all_to_all | solution.py:225
  143.4 1.6 %copy-done.4 = bf16[4096,256]{1,0:T(8,128)(2,1)S(1)} copy-done((bf16[4096,256]{1,0:T(8,128)(2,1)S(1)}, bf16[4096,256]{1,0:T(8,128)(2,1)}, u32[]{:S(2)}) %copy-start.4) | copy-done | bytes 2097176
  145.0 2.6 %shard_map.96 = (bf16[4096,128]{1,0:T(8,128)(2,1)}, bf16[128,4096]{1,0:T(8,128)(2,1)}) custom-call(bf16[4096,256]{1,0:T(8,128)(2,1)S(1)} %copy-done.2, bf16[4096,256]{1,0:T(8,128)(2,1)S(1)} %copy-done.4, bf16[128,256]{1,0:T(8,128)(2,1)S(1)} %get-tuple-element.23.back_ref, bf16[128,256]{1,0:T(8,128)(2,1)S(1)} %get-tuple-element.24.scaled_ref), custom_call_target="tpu_custom_call" | custom-call | flops 536870912 | bytes 6291456 | tf_op jit(solution)/shard_map/pallas_call | solution.py:209
  (33 shorter events, 10.2 us)
Async XLA Ops:
  0.6 84.6 %copy-start.5 = (f32[1,256]{1,0:T(1,128)S(1)}, f32[1,256]{1,0:T(1,128)}, u32[]{:S(2)}) copy-start(f32[1,256]{1,0:T(1,128)} %refs_10_.1) | copy-start | bytes 3076
  0.6 84.6 %copy-start = (bf16[1,4096,128]{2,1,0:T(8,128)(2,1)S(1)}, bf16[1,4096,128]{2,1,0:T(8,128)(2,1)}, u32[]{:S(2)}) copy-start(bf16[1,4096,128]{2,1,0:T(8,128)(2,1)} %param.8) | copy-start | bytes 3145732
  38.9 37.8 %collective-permute-start.2 = (bf16[8,128,256]{2,1,0:T(8,128)(2,1)}, bf16[8,128,256]{2,1,0:T(8,128)(2,1)}, u32[]{:S(2)}, u32[]{:S(2)}) collective-permute-start(bf16[8,128,256]{2,1,0:T(8,128)(2,1)} %all_to_all.21.refs_0_), channel_id=1, source_target_pairs={{0,48},{16,0},{32,16},{48,32},{64,112},{80,64},{96,80},{112,96},{1... | collective-permute-start | bytes 1572872 | tf_op jit(solution)/shard_map/ppermute | solution.py:270
  52.8 25.8 %collective-permute-start.1 = (bf16[8,128,256]{2,1,0:T(8,128)(2,1)}, bf16[8,128,256]{2,1,0:T(8,128)(2,1)}, u32[]{:S(2)}, u32[]{:S(2)}) collective-permute-start(bf16[8,128,256]{2,1,0:T(8,128)(2,1)} %all_to_all.21.refs_0_), channel_id=1, source_target_pairs={{0,32},{16,48},{32,0},{48,16},{64,96},{80,112},{96,64},{112,80},{1... | collective-permute-start | bytes 1572872 | tf_op jit(solution)/shard_map/ppermute | solution.py:270
  54.8 26.3 %collective-permute-start = (bf16[8,128,256]{2,1,0:T(8,128)(2,1)}, bf16[8,128,256]{2,1,0:T(8,128)(2,1)}, u32[]{:S(2)}, u32[]{:S(2)}) collective-permute-start(bf16[8,128,256]{2,1,0:T(8,128)(2,1)} %all_to_all.21.refs_0_), channel_id=1, source_target_pairs={{0,16},{16,32},{32,48},{48,0},{64,80},{80,96},{96,112},{112,64},{1... | collective-permute-start | bytes 1572872 | tf_op jit(solution)/shard_map/ppermute | solution.py:270
  59.1 24.3 %collective-permute-start.3 = (bf16[8,128,256]{2,1,0:T(8,128)(2,1)}, bf16[8,128,256]{2,1,0:T(8,128)(2,1)}, u32[]{:S(2)}, u32[]{:S(2)}) collective-permute-start(bf16[8,128,256]{2,1,0:T(8,128)(2,1)} %all_to_all.21.refs_0_), channel_id=1, source_target_pairs={{0,8},{8,0},{16,24},{24,16},{32,40},{40,32},{48,56},{56,48},{64,72... | collective-permute-start | bytes 1572872 | tf_op jit(solution)/shard_map/ppermute | solution.py:271
  76.7 6.7 %collective-permute-start.6 = (bf16[8,128,256]{2,1,0:T(8,128)(2,1)}, bf16[8,128,256]{2,1,0:T(8,128)(2,1)}, u32[]{:S(2)}, u32[]{:S(2)}) collective-permute-start(bf16[8,128,256]{2,1,0:T(8,128)(2,1)} %collective-permute-done.2.refs_3_), channel_id=1, source_target_pairs={{0,8},{8,0},{16,24},{24,16},{32,40},{40,32},{48,56},{56,48},{64,72... | collective-permute-start | bytes 1572872 | tf_op jit(solution)/shard_map/ppermute | solution.py:271
  78.6 4.8 %collective-permute-start.5 = (bf16[8,128,256]{2,1,0:T(8,128)(2,1)}, bf16[8,128,256]{2,1,0:T(8,128)(2,1)}, u32[]{:S(2)}, u32[]{:S(2)}) collective-permute-start(bf16[8,128,256]{2,1,0:T(8,128)(2,1)} %collective-permute-done.1.refs_2_), channel_id=1, source_target_pairs={{0,8},{8,0},{16,24},{24,16},{32,40},{40,32},{48,56},{56,48},{64,72... | collective-permute-start | bytes 1572872 | tf_op jit(solution)/shard_map/ppermute | solution.py:271
  81.1 4.1 %collective-permute-start.4 = (bf16[8,128,256]{2,1,0:T(8,128)(2,1)}, bf16[8,128,256]{2,1,0:T(8,128)(2,1)}, u32[]{:S(2)}, u32[]{:S(2)}) collective-permute-start(bf16[8,128,256]{2,1,0:T(8,128)(2,1)} %collective-permute-done.refs_1_), channel_id=1, source_target_pairs={{0,8},{8,0},{16,24},{24,16},{32,40},{40,32},{48,56},{56,48},{64,72... | collective-permute-start | bytes 1572872 | tf_op jit(solution)/shard_map/ppermute | solution.py:271
  90.8 1.3 copy-start.1
  92.1 1.3 copy-start.3
  93.4 4.9 %collective-permute-start.7 = (bf16[2064,256]{1,0:T(8,128)(2,1)}, bf16[2064,256]{1,0:T(8,128)(2,1)}, u32[]{:S(2)}, u32[]{:S(2)}) collective-permute-start(bf16[2064,256]{1,0:T(8,128)(2,1)} %get-tuple-element.28), channel_id=1, source_target_pairs={{0,8},{8,0},{16,24},{24,16},{32,40},{40,32},{48,56},{56,48},{64,72... | collective-permute-start | bytes 3170312 | tf_op jit(solution)/shard_map/ppermute | solution.py:287
  100.0 13.9 %collective-permute-start.8 = (bf16[528,256]{1,0:T(8,128)(2,1)S(1)}, bf16[528,256]{1,0:T(8,128)(2,1)S(1)}, u32[]{:S(2)}, u32[]{:S(2)}) collective-permute-start(bf16[528,256]{1,0:T(8,128)(2,1)S(1)} %get-tuple-element.30), channel_id=1, source_target_pairs={{0,16},{16,32},{32,48},{48,0},{64,80},{80,96},{96,112},{112,64},{1... | collective-permute-start | bytes 811016 | tf_op jit(solution)/shard_map/ppermute | solution.py:300
  101.9 20.0 %collective-permute-start.9 = (bf16[528,256]{1,0:T(8,128)(2,1)S(1)}, bf16[528,256]{1,0:T(8,128)(2,1)S(1)}, u32[]{:S(2)}, u32[]{:S(2)}) collective-permute-start(bf16[528,256]{1,0:T(8,128)(2,1)S(1)} %get-tuple-element.31), channel_id=1, source_target_pairs={{0,32},{16,48},{32,0},{48,16},{64,96},{80,112},{96,64},{112,80},{1... | collective-permute-start | bytes 811016 | tf_op jit(solution)/shard_map/ppermute | solution.py:300
  110.7 13.6 %collective-permute-start.10 = (bf16[528,256]{1,0:T(8,128)(2,1)S(1)}, bf16[528,256]{1,0:T(8,128)(2,1)S(1)}, u32[]{:S(2)}, u32[]{:S(2)}) collective-permute-start(bf16[528,256]{1,0:T(8,128)(2,1)S(1)} %get-tuple-element.32), channel_id=1, source_target_pairs={{0,48},{16,0},{32,16},{48,32},{64,112},{80,64},{96,80},{112,96},{1... | collective-permute-start | bytes 811016 | tf_op jit(solution)/shard_map/ppermute | solution.py:300
  138.4 10.7 %all-to-all-start.3 = ((bf16[8,64,256]{2,1,0:T(8,128)(2,1)}), bf16[8,64,256]{2,1,0:T(8,128)(2,1)S(1)}, u32[]{:S(2)}, u32[]{:S(2)}) async-start(bf16[8,64,256]{2,1,0:T(8,128)(2,1)} %get-tuple-element.33), calls=%async_computation.3 | async-start | bytes 524288 | tf_op jit(solution)/shard_map/all_to_all | solution.py:225
  141.9 1.6 %copy-start.2 = (bf16[4096,256]{1,0:T(8,128)(2,1)S(1)}, bf16[4096,256]{1,0:T(8,128)(2,1)}, u32[]{:S(2)}) copy-start(bf16[4096,256]{1,0:T(8,128)(2,1)} %copy-done.1) | copy-start | bytes 6291460
  143.4 1.6 %copy-start.4 = (bf16[4096,256]{1,0:T(8,128)(2,1)S(1)}, bf16[4096,256]{1,0:T(8,128)(2,1)}, u32[]{:S(2)}) copy-start(bf16[4096,256]{1,0:T(8,128)(2,1)} %copy-done.3) | copy-start | bytes 6291460

commit v3 on v2

--- a/solution.py
+++ b/solution.py
@@ -22,9 +22,6 @@
 ]
 OUTER = [[dp_index(y, z, 0) for z in range(NZ)] for y in range(NY)] + [
     [dp_index(4 * h + q, z, 1) for q in range(4)] for h in range(2) for z in range(NZ)
-]
-SHIFTS = [
-    [(g[j], g[(j + k) % 4]) for g in OUTER for j in range(4)] for k in range(4)
 ]
 SWAP = [(d, d ^ 1) for d in range(NY * NZ * 2)]
 
@@ -96,23 +93,43 @@
     return pl.ds(pl.multiple_of(slots_ref[slot] * feats, feats), feats)
 
 
-def main_kernel(slots_ref, *refs):
-    parts, (w_in_ref, w_out_ref, score_ref) = refs[:8], refs[8:11]
-    x_ref, u_ref, back_ref, scaled_ref, gate_ref, send_ref = refs[11:17]
-    w_out_held, x_sem, u_sem, w_sem = refs[17:]
-    weights = pltpu.make_async_copy(w_out_ref, w_out_held, w_sem)
-    inner, feats = parts[0].shape[0], parts[0].shape[1] // 2
-    for k, ref in enumerate(parts):
+def load_blocks(slots_ref, first, blocks_ref, x_ref, u_ref, x_sem, u_sem):
+    outer, inner, both = blocks_ref.shape[:3]
+    feats = both // 2
+    for o in range(outer):
         for i in range(inner):
-            at = block_rows(slots_ref, k * inner + i, feats)
-            pltpu.make_async_copy(ref.at[i, pl.ds(0, feats)], x_ref.at[at], x_sem).start()
-            pltpu.make_async_copy(ref.at[i, pl.ds(feats, feats)], u_ref.at[at], u_sem).start()
+            at = block_rows(slots_ref, first + o * inner + i, feats)
+            act, grad = (blocks_ref.at[o, i, pl.ds(h * feats, feats)] for h in range(2))
+            pltpu.make_async_copy(act, x_ref.at[at], x_sem).start()
+            pltpu.make_async_copy(grad, u_ref.at[at], u_sem).start()
+    half = pl.ds(0, outer * inner * feats)
+    return (
+        pltpu.make_async_copy(x_ref.at[half], x_ref.at[half], x_sem),
+        pltpu.make_async_copy(u_ref.at[half], u_ref.at[half], u_sem),
+    )
+
+
+def ready_kernel(slots_ref, own_ref, w_in_ref, x_ref, u_ref, turned_ref, x_sem, u_sem):
+    arrived = load_blocks(slots_ref, 0, own_ref, x_ref, u_ref, x_sem, u_sem)
+    turned_ref[...] = w_in_ref[...].T
+    for copy in arrived:
+        copy.wait()
+
+
+def main_kernel(
+    slots_ref, oth_ref, x_in, u_in, turned_ref, w_in_ref, w_out_ref, score_ref,
+    x_ref, u_ref, back_ref, scaled_ref, gate_ref, send_ref, held_ref, x_sem, u_sem, w_sem,
+):
+    weights = pltpu.make_async_copy(w_out_ref, held_ref, w_sem)
     weights.start()
-    pltpu.make_async_copy(x_ref, x_ref, x_sem).wait()
-    preact = contract(w_in_ref[...], x_ref[...], 0, 0)
-    pltpu.make_async_copy(u_ref, u_ref, u_sem).wait()
+    slots = oth_ref.shape[0] * oth_ref.shape[1]
+    feats = oth_ref.shape[2] // 2
+    x_done, u_done = load_blocks(slots_ref, slots, oth_ref, x_ref, u_ref, x_sem, u_sem)
+    x_done.wait()
+    preact = contract(turned_ref[...], x_ref[...], 1, 0)
+    u_done.wait()
     weights.wait()
-    raw = contract(w_out_held[...], u_ref[...], 1, 0)
+    raw = contract(held_ref[...], u_ref[...], 1, 0)
     val, slope = gelu_parts(preact)
     hidden = val.astype(BF).astype(F32)
     score = score_ref[...]
@@ -121,11 +138,10 @@
     back_ref[...] = back
     scaled_ref[...] = (score * hidden).astype(BF)
     gate_ref[...] = gate
-    count = send_ref.shape[0] // feats
-    for s in range(count):
-        at = block_rows(slots_ref, 8 * inner + s, feats)
+    for s in range(slots):
+        at = block_rows(slots_ref, slots + s, feats)
         send_ref[pl.ds(s * feats, feats), :] = contract(w_in_ref[at, :], back, 1, 0).astype(BF)
-    send_ref[pl.ds(count * feats, 16), :] = gate_tile([hi_lo(gate)])
+    send_ref[pl.ds(slots * feats, 16), :] = gate_tile([hi_lo(gate)])
 
 
 def weight_kernel(x_ref, u_ref, back_ref, scaled_ref, gin_ref, gout_ref):
@@ -133,41 +149,33 @@
     gout_ref[...] = contract(scaled_ref[...], u_ref[...], 1, 1).astype(BF)
 
 
-def pair_kernel(slots_ref, w_in_ref, back_ref, gate_ref, got_ref, *outs):
-    rows = outs[0].shape[0] - 16
+def pair_kernel(slots_ref, w_in_ref, back_ref, gate_ref, got_ref, out_ref):
+    parts, rows = out_ref.shape[0], out_ref.shape[1] - 16
     feats = rows // 8
-    tile = got_ref[pl.ds(len(outs) * rows, 16), :].astype(F32)
+    back = back_ref[...]
+    tile = got_ref[pl.ds(parts * rows, 16), :].astype(F32)
     high, low = hi_lo(gate_ref[...])
     gate = (high.astype(F32) + low.astype(F32)) + (tile[0:1] + tile[1:2])
     packed = gate_tile([hi_lo(gate)])
-    back = back_ref[...]
-    for k, ref in enumerate(outs):
+    for k in range(parts):
         for i in range(8):
             s = k * 8 + i
             mine = contract(w_in_ref[block_rows(slots_ref, s, feats), :], back, 1, 0)
             other = got_ref[pl.ds(s * feats, feats), :].astype(F32)
-            ref[pl.ds(i * feats, feats), :] = (mine + other).astype(BF)
-        ref[pl.ds(rows, 16), :] = packed
-
-
-def outer_kernel(place_ref, *refs):
-    parts, out_ref = refs[:4], refs[4]
+            out_ref[k, pl.ds(i * feats, feats), :] = (mine + other).astype(BF)
+        out_ref[k, rows:, :] = packed
+
+
+def outer_kernel(got_ref, out_ref):
     count, rows = out_ref.shape[0], out_ref.shape[1] - 16
     base = count * rows
-    tiles = [ref[pl.ds(base, 16), :].astype(F32) for ref in parts]
-    pairs = []
-    for o in range(4):
-        source = (place_ref[0] + 4 - o) % 4
-        pair = tiles[0]
-        for k in range(1, 4):
-            pair = jnp.where(source == k, tiles[k], pair)
-        pairs.append((pair[0:1], pair[1:2]))
-    packed = gate_tile(pairs)
+    tiles = [got_ref[o, pl.ds(base, 16), :].astype(F32) for o in range(4)]
+    packed = gate_tile([(t[0:1], t[1:2]) for t in tiles])
     for i in range(count):
         at = pl.ds(i * rows, rows)
-        total = parts[0][at, :].astype(F32)
-        for k in range(1, 4):
-            total = total + parts[k][at, :].astype(F32)
+        total = got_ref[0, at, :].astype(F32)
+        for o in range(1, 4):
+            total = total + got_ref[o, at, :].astype(F32)
         out_ref[i, :rows, :] = total.astype(BF)
         out_ref[i, rows:, :] = packed
 
@@ -201,9 +209,10 @@
 SMEM = pl.BlockSpec(memory_space=pltpu.SMEM)
 VMEM = pl.BlockSpec(memory_space=pltpu.VMEM)
 HBM = pl.BlockSpec(memory_space=pltpu.HBM)
-
-
-def call(kernel, specs, outs, *args, scratch=(), mib=16, flops=0, moved=0):
+ANY = pl.BlockSpec(memory_space=pl.ANY)
+
+
+def call(kernel, specs, outs, *args, scratch=(), alias=None, mib=16, flops=0, moved=0):
     shapes = [jax.ShapeDtypeStruct(s, t) for s, t in outs]
     single = len(shapes) == 1
     return pl.pallas_call(
@@ -212,6 +221,7 @@
         in_specs=specs,
         out_specs=VMEM if single else [VMEM] * len(shapes),
         scratch_shapes=scratch,
+        input_output_aliases=alias or {},
         cost_estimate=pl.CostEstimate(flops=flops, bytes_accessed=moved, transcendentals=0),
         compiler_params=pltpu.CompilerParams(vmem_limit_bytes=mib * MIB),
     )(*args)
@@ -225,8 +235,8 @@
     return lax.all_to_all(parts, axis, 0, 0, axis_index_groups=groups)
 
 
-def block_table(core, place):
-    o = place[:, None]
+def block_table(core):
+    o = jnp.arange(4, dtype=jnp.int32)[:, None]
     i = jnp.arange(8, dtype=jnp.int32)[None, :]
     zero = dp_index(i, o, 0)
     one = dp_index(4 * (i // NZ) + o, i % NZ, 1)
@@ -238,20 +248,9 @@
     experts, rows = chosen.shape
     depth, units = w_in.shape[1], w_in.shape[2]
     base = (lax.axis_index("expert") * tokens).astype(jnp.int32).reshape(1)
-    index = lax.axis_index("dp").astype(jnp.int32)
-    core, z, y = index & 1, (index >> 1) & (NZ - 1), index >> 3
-    place = jnp.where(core == 0, z, y & 3)
-    other_place = jnp.where(core == 0, y & 3, z)
-    steps = jnp.arange(4, dtype=jnp.int32)
-    gathered = jnp.concatenate(
-        [
-            block_table(core, (place - steps) & 3),
-            block_table(1 - core, (other_place - steps) & 3),
-            block_table(1 - core, (other_place + steps) & 3),
-        ]
-    )
-    summed = block_table(core, (place + steps) & 3)
-    count = summed.shape[0]
+    core = lax.axis_index("dp").astype(jnp.int32) & 1
+    slots = jnp.concatenate([block_table(core), block_table(1 - core)])
+    count = slots.shape[0] // 2
 
     picked, sel = call(
         pick_kernel,
@@ -266,42 +265,44 @@
     )
     picked = exchange(picked, "expert")
     mine = call(merge_kernel, [VMEM], [((8, 2 * feats, rows), BF)], picked)
-    own = exchange(mine, "dp", INNER)
-    blocks = [own] + [lax.ppermute(own, "dp", SHIFTS[k]) for k in (1, 2, 3)]
-    blocks += [lax.ppermute(block, "dp", SWAP) for block in blocks]
-
+    inner = exchange(mine, "dp", INNER)
+    own = exchange(jnp.broadcast_to(inner[None], (4,) + inner.shape), "dp", OUTER)
+    other = lax.ppermute(own, "dp", SWAP)
+    sems = [pltpu.SemaphoreType.DMA] * 2
+    held = [((depth, rows), BF), ((depth, rows), BF)]
+    x, u, turned = call(
+        ready_kernel, [SMEM, ANY, VMEM], held + [((units, depth), BF)], slots, own, w_in[0],
+        scratch=sems, flops=2 * MIB, moved=6 * MIB,
+    )
     x, u, back, scaled, gate, send = call(
         main_kernel,
-        [SMEM] + [HBM] * 8 + [VMEM, HBM, VMEM],
-        [
-            ((depth, rows), BF),
-            ((depth, rows), BF),
+        [SMEM, ANY] + [VMEM] * 4 + [HBM, VMEM],
+        held
+        + [
             ((units, rows), BF),
             ((units, rows), BF),
             ((1, rows), F32),
             ((count * feats + 16, rows), BF),
         ],
-        gathered, *blocks, w_in[0], in_hbm(w_out[0]), gate_scores, mib=24,
-        scratch=[pltpu.VMEM((units, depth), BF)] + [pltpu.SemaphoreType.DMA] * 3,
+        slots, other, x, u, turned, w_in[0], in_hbm(w_out[0]), gate_scores,
+        scratch=[pltpu.VMEM((units, depth), BF)] + [pltpu.SemaphoreType.DMA] * 3, alias={2: 0, 3: 1},
     )
     got = lax.ppermute(send, "dp", SWAP)
-    weight_in_grad, weight_out_grad = call(
+    weight_grads = call(
         weight_kernel,
         [VMEM] * 4,
         [((depth, units), BF), ((units, depth), BF)],
         x, u, back, scaled, flops=4 * depth * units * rows, moved=6 * depth * rows,
     )
-    parts = call(
+    got, weight_in_grad, weight_out_grad = lax.optimization_barrier((got, *weight_grads))
+    part = call(
         pair_kernel,
         [SMEM] + [VMEM] * 4,
-        [((8 * feats + 16, rows), BF)] * 4,
-        summed, w_in[0], back, gate, got,
-    )
-    parts = [parts[0]] + [lax.ppermute(parts[k], "dp", SHIFTS[k]) for k in (1, 2, 3)]
-    part = call(
-        outer_kernel, [SMEM] + [VMEM] * 4, [((8, feats + 16, rows), BF)],
-        place.reshape(1), *parts,
-    )
+        [((4, 8 * feats + 16, rows), BF)],
+        slots, w_in[0], back, gate, got,
+    )
+    part = exchange(part, "dp", OUTER)
+    part = call(outer_kernel, [VMEM], [((8, feats + 16, rows), BF)], part)
     part = exchange(part, "dp", INNER)
     term, gate_grad = call(
         inner_kernel, [SMEM, VMEM], [((experts, feats, rows), BF), ((1, rows), F32)],

time: 153 us -> 150 us (0.980)
  the two profiles are of different devices: /device:TPU:8 before, /device:TPU:1 now
where the time goes in v3:
time: 150 us; the launch traced here: 149 us
  blocking collectives  124 us (83%)
  Pallas kernels  15.2 us (10%)
  starting transfers between devices  7.54 us (5%)
  local copies, waits for them, and re-layouts  1.75 us (1%)
    all_to_all x6, blocking collectives, exchange(): return lax.all_to_all(parts, axis, 0, 0, axis_index_groups=groups)  124 us
    pallas_call x9, Pallas kernels, call(): pl.pallas_call(kernel, out_shape=shapes[0] if single else shapes, in_spec...  15.2 us
    ppermute x1, starting transfers between devices, per_device(): other = lax.ppermute(own, 'dp', SWAP)  5.41 us
  transfers between devices with their start and end apart: 2, of which 0 were waited for; matrix products, arithmetic and copies ran while one was open for 0% of the time, Pallas kernels for 4%

profile of v3, /device:TPU:1, one launch (start us, length us, event | category | flops | bytes accessed | tf_op | source)
XLA Modules:
  0.0 149.4 jit_solution(13466692478260234058)
XLA Ops:
  0.6 1.5 shard_map.93
  2.1 1.3 copy-done.1
  3.5 14.0 %all_to_all.30.parts_ref = bf16[8,128,256]{2,1,0:T(8,128)(2,1)S(1)} all-to-all(bf16[8,128,256]{2,1,0:T(8,128)(2,1)S(1)} %get-tuple-element.22), channel_id=1, replica_groups=mesh['dp'=64,'expert'=8] {'expert'}, dimensions={0} | all-to-all | bytes 1048576 | tf_op jit(solution)/shard_map/all_to_all | solution.py:235
  17.5 0.1 shard_map.94
  17.6 34.2 %all_to_all.31 = bf16[8,128,256]{2,1,0:T(8,128)(2,1)S(1)} all-to-all(bf16[8,128,256]{2,1,0:T(8,128)(2,1)S(1)} %shard_map.94), channel_id=1, replica_groups={{0,64,128,192,256,320,384,448},{16,80,144,208,272,336,400,464},{32,96,1..., dimensions={0} | all-to-all | bytes 1048576 | tf_op jit(solution)/shard_map/all_to_all | solution.py:235
  51.7 0.2 broadcast_in_dim.6
  52.0 0.0 copy-start
  52.0 29.6 %all_to_all.32.own_ref = bf16[4,8,128,256]{3,2,1,0:T(8,128)(2,1)S(1)} all-to-all(bf16[4,8,128,256]{3,2,1,0:T(8,128)(2,1)S(1)} %broadcast_in_dim.6), channel_id=1, replica_groups={{0,16,32,48},{64,80,96,112},{128,144,160,176},{192,208,224,240},{256,27..., dimensions={0} | all-to-all | bytes 4194304 | tf_op jit(solution)/shard_map/all_to_all | solution.py:235
  81.6 5.4 %collective-permute-start = (bf16[4,8,128,256]{3,2,1,0:T(8,128)(2,1)S(1)}, bf16[4,8,128,256]{3,2,1,0:T(8,128)(2,1)}, u32[]{:S(2)}, u32[]{:S(2)}) collective-permute-start(bf16[4,8,128,256]{3,2,1,0:T(8,128)(2,1)S(1)} %all_to_all.32.own_ref), channel_id=1, source_target_pairs={{0,8},{8,0},{16,24},{24,16},{32,40},{40,32},{48,56},{56,48},{64,72... | collective-permute-start | bytes 6291464 | tf_op jit(solution)/shard_map/ppermute | solution.py:270
  87.0 0.1 reshape.100
  87.1 0.1 reshape.102
  87.2 0.1 pad_add_fusion.slots_ref
  87.3 3.7 %shard_map.95 = (bf16[4096,256]{1,0:T(8,128)(2,1)S(1)}, bf16[4096,256]{1,0:T(8,128)(2,1)S(1)}, bf16[128,4096]{1,0:T(8,128)(2,1)S(1)}) custom-call(s32[64]{0:T(128)S(1)} %pad_add_fusion.slots_ref, bf16[4,8,128,256]{3,2,1,0:T(8,128)(2,1)S(1)} %all_to_all.32.own_ref, bf16[4096,128]{1,0:T(8,128)(2,1)S(1)} %bitcast.9), custom_call_target="tpu_custom_call" | custom-call | flops 2097152 | bytes 6291456 | tf_op jit(solution)/shard_map/pallas_call | solution.py:218
  91.0 0.0 collective-permute-done.oth_ref
  91.0 4.2 %shard_map.96 = (bf16[4096,256]{1,0:T(8,128)(2,1)S(1)}, bf16[4096,256]{1,0:T(8,128)(2,1)S(1)}, bf16[128,256]{1,0:T(8,128)(2,1)S(1)}, bf16[128,256]{1,0:T(8,128)(...) custom-call(s32[64]{0:T(128)S(1)} %pad_add_fusion.slots_ref, ...), custom_call_target="tpu_custom_call", output_to_operand_aliasing={{0}: (2, {}), {1}: (3, {})} | custom-call | tf_op jit(solution)/shard_map/pallas_call | solution.py:218
  95.2 2.1 %collective-permute-start.1 = (bf16[2064,256]{1,0:T(8,128)(2,1)S(1)}, bf16[2064,256]{1,0:T(8,128)(2,1)S(1)}, u32[]{:S(2)}, u32[]{:S(2)}) collective-permute-start(bf16[2064,256]{1,0:T(8,128)(2,1)S(1)} %get-tuple-element.26), channel_id=1, source_target_pairs={{0,8},{8,0},{16,24},{24,16},{32,40},{40,32},{48,56},{56,48},{64,72... | collective-permute-start | bytes 3170312 | tf_op jit(solution)/shard_map/ppermute | solution.py:290
  97.3 2.6 %shard_map.97 = (bf16[4096,128]{1,0:T(8,128)(2,1)}, bf16[128,4096]{1,0:T(8,128)(2,1)}) custom-call(bf16[4096,256]{1,0:T(8,128)(2,1)S(1)} %get-tuple-element.27.x_ref, bf16[4096,256]{1,0:T(8,128)(2,1)S(1)} %get-tuple-element.28.u_ref, bf16[128,256]{1,0:T(8,128)(2,1)S(1)} %get-tuple-element.29.back_ref, bf16[128,256]{1,0:T(8,128)(2,1)S(1)} %get-tuple-element.30.scaled_ref), custom_call_target="tpu_custom_call" | custom-call | flops 536870912 | bytes 6291456 | tf_op jit(solution)/shard_map/pallas_call | solution.py:218
  100.0 1.0 shard_map.98
  101.0 17.6 %all_to_all.33.got_ref = bf16[4,528,256]{2,1,0:T(8,128)(2,1)S(1)} all-to-all(bf16[4,528,256]{2,1,0:T(8,128)(2,1)S(1)} %shard_map.98), channel_id=1, replica_groups={{0,16,32,48},{64,80,96,112},{128,144,160,176},{192,208,224,240},{256,27..., dimensions={0} | all-to-all | bytes 2162688 | tf_op jit(solution)/shard_map/all_to_all | solution.py:235
  118.6 0.1 shard_map.99
  118.7 19.9 %all_to_all.34.got_ref = bf16[8,80,256]{2,1,0:T(8,128)(2,1)S(1)} all-to-all(bf16[8,80,256]{2,1,0:T(8,128)(2,1)S(1)} %shard_map.99), channel_id=1, replica_groups={{0,64,128,192,256,320,384,448},{16,80,144,208,272,336,400,464},{32,96,1..., dimensions={0} | all-to-all | bytes 655360 | tf_op jit(solution)/shard_map/all_to_all | solution.py:235
  138.7 0.6 shard_map.100
  139.3 8.8 %all_to_all.35.terms_ref = bf16[8,64,256]{2,1,0:T(8,128)(2,1)S(1)} all-to-all(bf16[8,64,256]{2,1,0:T(8,128)(2,1)S(1)} %get-tuple-element.37), channel_id=1, replica_groups=mesh['dp'=64,'expert'=8] {'expert'}, dimensions={0} | all-to-all | bytes 524288 | tf_op jit(solution)/shard_map/all_to_all | solution.py:235
  148.0 1.4 shard_map.101
  (10 shorter events, 0.0 us)
Async XLA Ops:
  2.1 1.3 copy-start.1
  52.0 35.3 %copy-start = (bf16[1,4096,128]{2,1,0:T(8,128)(2,1)S(1)}, bf16[1,4096,128]{2,1,0:T(8,128)(2,1)}, u32[]{:S(2)}) copy-start(bf16[1,4096,128]{2,1,0:T(8,128)(2,1)} %param.8) | copy-start | bytes 3145732
  81.6 9.5 %copy-start.3 = (f32[1,256]{1,0:T(1,128)S(1)}, f32[1,256]{1,0:T(1,128)}, u32[]{:S(2)}) copy-start(f32[1,256]{1,0:T(1,128)} %score_ref.1) | copy-start | bytes 3076
  81.6 9.4 %collective-permute-start = (bf16[4,8,128,256]{3,2,1,0:T(8,128)(2,1)S(1)}, bf16[4,8,128,256]{3,2,1,0:T(8,128)(2,1)}, u32[]{:S(2)}, u32[]{:S(2)}) collective-permute-start(bf16[4,8,128,256]{3,2,1,0:T(8,128)(2,1)S(1)} %all_to_all.32.own_ref), channel_id=1, source_target_pairs={{0,8},{8,0},{16,24},{24,16},{32,40},{40,32},{48,56},{56,48},{64,72... | collective-permute-start | bytes 6291464 | tf_op jit(solution)/shard_map/ppermute | solution.py:270
  95.2 4.8 %collective-permute-start.1 = (bf16[2064,256]{1,0:T(8,128)(2,1)S(1)}, bf16[2064,256]{1,0:T(8,128)(2,1)S(1)}, u32[]{:S(2)}, u32[]{:S(2)}) collective-permute-start(bf16[2064,256]{1,0:T(8,128)(2,1)S(1)} %get-tuple-element.26), channel_id=1, source_target_pairs={{0,8},{8,0},{16,24},{24,16},{32,40},{40,32},{48,56},{56,48},{64,72... | collective-permute-start | bytes 3170312 | tf_op jit(solution)/shard_map/ppermute | solution.py:290
  100.9 47.1 %copy-start.2 = (bf16[8,512,256]{2,1,0:T(8,128)(2,1)S(1)}, bf16[8,512,256]{2,1,0:T(8,128)(2,1)}, u32[]{:S(2)}) copy-start(bf16[8,512,256]{2,1,0:T(8,128)(2,1)} %copy-done.1) | copy-start | bytes 6291460

commit v4 on v3

--- a/solution.py
+++ b/solution.py
@@ -18,10 +18,10 @@
 
 
 INNER = [[dp_index(y, z, 0) for y in range(NY)] for z in range(NZ)] + [
-    [dp_index(4 * h + q, z, 1) for h in range(2) for z in range(NZ)] for q in range(4)
+    [dp_index(2 * q + p, z, 1) for p in range(2) for z in range(NZ)] for q in range(4)
 ]
 OUTER = [[dp_index(y, z, 0) for z in range(NZ)] for y in range(NY)] + [
-    [dp_index(4 * h + q, z, 1) for q in range(4)] for h in range(2) for z in range(NZ)
+    [dp_index(2 * q + p, z, 1) for q in range(4)] for p in range(2) for z in range(NZ)
 ]
 SWAP = [(d, d ^ 1) for d in range(NY * NZ * 2)]
 
@@ -55,7 +55,7 @@
 
 
 def pick_kernel(
-    base_ref, act_hbm, grad_hbm, chosen_hbm, out_ref, sel_ref, both_ref, chosen_ref, sems
+    base_ref, act_hbm, grad_hbm, chosen_hbm, out_ref, both_ref, chosen_ref, sems
 ):
     feats = act_hbm.shape[0]
     copies = [
@@ -70,7 +70,6 @@
     both = both_ref[...]
     for e in range(out_ref.shape[0]):
         sel = onehot(base_ref[0], chosen_ref[e : e + 1, :], both.shape[1])
-        sel_ref[e] = sel
         out_ref[e] = contract(both, sel, 1, 0).astype(BF)
 
 
@@ -195,14 +194,16 @@
     gate = jnp.zeros((1, got_ref.shape[2]), F32)
     for y in range(NY):
         for z in range(NZ):
-            gate = gate + jnp.where(first, gates[y][z], gates[(y // 4) * NZ + z][y % 4])
+            gate = gate + jnp.where(first, gates[y][z], gates[(y % 2) * NZ + z][y // 2])
     gate_ref[...] = gate
 
 
-def scatter_kernel(terms_ref, sel_ref, out_ref):
+def scatter_kernel(base_ref, terms_ref, chosen_ref, out_ref):
+    tokens = out_ref.shape[1]
     total = jnp.zeros(out_ref.shape, F32)
     for e in range(terms_ref.shape[0]):
-        total = total + contract(terms_ref[e], sel_ref[e], 1, 1)
+        sel = onehot(base_ref[0], chosen_ref[e : e + 1, :], tokens)
+        total = total + contract(terms_ref[e], sel, 1, 1)
     out_ref[...] = total.astype(BF)
 
 
@@ -239,7 +240,7 @@
     o = jnp.arange(4, dtype=jnp.int32)[:, None]
     i = jnp.arange(8, dtype=jnp.int32)[None, :]
     zero = dp_index(i, o, 0)
-    one = dp_index(4 * (i // NZ) + o, i % NZ, 1)
+    one = dp_index(2 * o + i // NZ, i % NZ, 1)
     return jnp.where(core == 0, zero, one).reshape(-1)
 
 
@@ -252,10 +253,10 @@
     slots = jnp.concatenate([block_table(core), block_table(1 - core)])
     count = slots.shape[0] // 2
 
-    picked, sel = call(
+    picked = call(
         pick_kernel,
         [SMEM, HBM, HBM, HBM],
-        [((experts, 2 * feats, rows), BF), ((experts, tokens, rows), BF)],
+        [((experts, 2 * feats, rows), BF)],
         base, in_hbm(activations.T), in_hbm(out_grad.T), in_hbm(chosen),
         scratch=[
             pltpu.VMEM((2 * feats, tokens), BF),
@@ -309,7 +310,9 @@
         core.reshape(1), part,
     )
     terms = exchange(term, "expert")
-    act_grad = call(scatter_kernel, [VMEM, VMEM], [((feats, tokens), BF)], terms, sel)
+    act_grad = call(
+        scatter_kernel, [SMEM, VMEM, VMEM], [((feats, tokens), BF)], base, terms, chosen
+    )
     return weight_in_grad[None], weight_out_grad[None], act_grad.T, gate_grad
 
 

time: 150 us -> 141 us (0.940)
  the two profiles are of different devices: /device:TPU:1 before, /device:TPU:8 now
where the time goes in v4:
time: 141 us
  blocking collectives  120 us (85%)
  Pallas kernels  15 us (11%)
  starting transfers between devices  4.31 us (3%)
    all_to_all x6, blocking collectives, exchange(): return lax.all_to_all(parts, axis, 0, 0, axis_index_groups=groups)  120 us
    pallas_call x9, Pallas kernels, call(): pl.pallas_call(kernel, out_shape=shapes[0] if single else shapes, in_spec...  15 us
  transfers between devices with their start and end apart: 2, of which 1 were waited for; matrix products, arithmetic and copies ran while one was open for 0% of the time, Pallas kernels for 5%

profile of v4, /device:TPU:8, one launch (start us, length us, event | category | flops | bytes accessed | tf_op | source)
XLA Modules:
  0.0 140.5 jit_solution(12123891144263642068)
XLA Ops:
  0.6 1.4 shard_map.93
  2.0 16.0 %all_to_all.30.parts_ref = bf16[8,128,256]{2,1,0:T(8,128)(2,1)S(1)} all-to-all(bf16[8,128,256]{2,1,0:T(8,128)(2,1)S(1)} %shard_map.93), channel_id=1, replica_groups=mesh['dp'=64,'expert'=8] {'expert'}, dimensions={0} | all-to-all | bytes 1048576 | tf_op jit(solution)/shard_map/all_to_all | solution.py:236
  18.0 0.1 shard_map.94
  18.1 21.2 %all_to_all.31 = bf16[8,128,256]{2,1,0:T(8,128)(2,1)S(1)} all-to-all(bf16[8,128,256]{2,1,0:T(8,128)(2,1)S(1)} %shard_map.94), channel_id=1, replica_groups={{0,64,128,192,256,320,384,448},{16,80,144,208,272,336,400,464},{32,96,1..., dimensions={0} | all-to-all | bytes 1048576 | tf_op jit(solution)/shard_map/all_to_all | solution.py:236
  39.3 0.2 broadcast_in_dim.6
  39.5 0.0 copy-start
  39.5 37.7 %all_to_all.32.own_ref = bf16[4,8,128,256]{3,2,1,0:T(8,128)(2,1)S(1)} all-to-all(bf16[4,8,128,256]{3,2,1,0:T(8,128)(2,1)S(1)} %broadcast_in_dim.6), channel_id=1, replica_groups={{0,16,32,48},{64,80,96,112},{128,144,160,176},{192,208,224,240},{256,27..., dimensions={0} | all-to-all | bytes 4194304 | tf_op jit(solution)/shard_map/all_to_all | solution.py:236
  77.3 2.0 %collective-permute-start = (bf16[4,8,128,256]{3,2,1,0:T(8,128)(2,1)S(1)}, bf16[4,8,128,256]{3,2,1,0:T(8,128)(2,1)}, u32[]{:S(2)}, u32[]{:S(2)}) collective-permute-start(bf16[4,8,128,256]{3,2,1,0:T(8,128)(2,1)S(1)} %all_to_all.32.own_ref), channel_id=1, source_target_pairs={{0,8},{8,0},{16,24},{24,16},{32,40},{40,32},{48,56},{56,48},{64,72... | collective-permute-start | bytes 6291464 | tf_op jit(solution)/shard_map/ppermute | solution.py:271
  79.4 0.1 fusion
  79.4 0.1 reshape.103
  79.5 0.1 reshape.105
  79.6 0.1 pad_add_fusion.slots_ref
  79.7 3.7 %shard_map.95 = (bf16[4096,256]{1,0:T(8,128)(2,1)S(1)}, bf16[4096,256]{1,0:T(8,128)(2,1)S(1)}, bf16[128,4096]{1,0:T(8,128)(2,1)S(1)}) custom-call(s32[64]{0:T(128)S(1)} %pad_add_fusion.slots_ref, bf16[4,8,128,256]{3,2,1,0:T(8,128)(2,1)S(1)} %all_to_all.32.own_ref, bf16[4096,128]{1,0:T(8,128)(2,1)S(1)} %bitcast.9), custom_call_target="tpu_custom_call" | custom-call | flops 2097152 | bytes 6291456 | tf_op jit(solution)/shard_map/pallas_call | solution.py:219
  83.4 0.2 collective-permute-done.oth_ref
  83.6 4.2 %shard_map.96 = (bf16[4096,256]{1,0:T(8,128)(2,1)S(1)}, bf16[4096,256]{1,0:T(8,128)(2,1)S(1)}, bf16[128,256]{1,0:T(8,128)(2,1)S(1)}, bf16[128,256]{1,0:T(8,128)(...) custom-call(s32[64]{0:T(128)S(1)} %pad_add_fusion.slots_ref, ...), custom_call_target="tpu_custom_call", output_to_operand_aliasing={{0}: (2, {}), {1}: (3, {})} | custom-call | tf_op jit(solution)/shard_map/pallas_call | solution.py:219
  87.7 2.3 %collective-permute-start.1 = (bf16[2064,256]{1,0:T(8,128)(2,1)S(1)}, bf16[2064,256]{1,0:T(8,128)(2,1)S(1)}, u32[]{:S(2)}, u32[]{:S(2)}) collective-permute-start(bf16[2064,256]{1,0:T(8,128)(2,1)S(1)} %get-tuple-element.23), channel_id=1, source_target_pairs={{0,8},{8,0},{16,24},{24,16},{32,40},{40,32},{48,56},{56,48},{64,72... | collective-permute-start | bytes 3170312 | tf_op jit(solution)/shard_map/ppermute | solution.py:291
  90.0 2.6 %shard_map.97 = (bf16[4096,128]{1,0:T(8,128)(2,1)}, bf16[128,4096]{1,0:T(8,128)(2,1)}) custom-call(bf16[4096,256]{1,0:T(8,128)(2,1)S(1)} %get-tuple-element.24.x_ref, bf16[4096,256]{1,0:T(8,128)(2,1)S(1)} %get-tuple-element.25.u_ref, bf16[128,256]{1,0:T(8,128)(2,1)S(1)} %get-tuple-element.26.back_ref, bf16[128,256]{1,0:T(8,128)(2,1)S(1)} %get-tuple-element.27.scaled_ref), custom_call_target="tpu_custom_call" | custom-call | flops 536870912 | bytes 6291456 | tf_op jit(solution)/shard_map/pallas_call | solution.py:219
  92.6 1.0 shard_map.98
  93.6 21.5 %all_to_all.33.got_ref = bf16[4,528,256]{2,1,0:T(8,128)(2,1)S(1)} all-to-all(bf16[4,528,256]{2,1,0:T(8,128)(2,1)S(1)} %shard_map.98), channel_id=1, replica_groups={{0,16,32,48},{64,80,96,112},{128,144,160,176},{192,208,224,240},{256,27..., dimensions={0} | all-to-all | bytes 2162688 | tf_op jit(solution)/shard_map/all_to_all | solution.py:236
  115.1 0.1 shard_map.99
  115.2 13.4 %all_to_all.34.got_ref = bf16[8,80,256]{2,1,0:T(8,128)(2,1)S(1)} all-to-all(bf16[8,80,256]{2,1,0:T(8,128)(2,1)S(1)} %shard_map.99), channel_id=1, replica_groups={{0,64,128,192,256,320,384,448},{16,80,144,208,272,336,400,464},{32,96,1..., dimensions={0} | all-to-all | bytes 655360 | tf_op jit(solution)/shard_map/all_to_all | solution.py:236
  128.7 0.6 shard_map.100
  129.3 9.9 %all_to_all.35.terms_ref = bf16[8,64,256]{2,1,0:T(8,128)(2,1)S(1)} all-to-all(bf16[8,64,256]{2,1,0:T(8,128)(2,1)S(1)} %get-tuple-element.34), channel_id=1, replica_groups=mesh['dp'=64,'expert'=8] {'expert'}, dimensions={0} | all-to-all | bytes 524288 | tf_op jit(solution)/shard_map/all_to_all | solution.py:236
  139.2 1.4 shard_map.101
  (9 shorter events, 0.0 us)
Async XLA Ops:
  39.5 40.2 %copy-start = (bf16[1,4096,128]{2,1,0:T(8,128)(2,1)S(1)}, bf16[1,4096,128]{2,1,0:T(8,128)(2,1)}, u32[]{:S(2)}) copy-start(bf16[1,4096,128]{2,1,0:T(8,128)(2,1)} %param.8) | copy-start | bytes 3145732
  77.3 6.3 %copy-start.2 = (f32[1,256]{1,0:T(1,128)S(1)}, f32[1,256]{1,0:T(1,128)}, u32[]{:S(2)}) copy-start(f32[1,256]{1,0:T(1,128)} %score_ref.1) | copy-start | bytes 3076
  77.3 6.3 %collective-permute-start = (bf16[4,8,128,256]{3,2,1,0:T(8,128)(2,1)S(1)}, bf16[4,8,128,256]{3,2,1,0:T(8,128)(2,1)}, u32[]{:S(2)}, u32[]{:S(2)}) collective-permute-start(bf16[4,8,128,256]{3,2,1,0:T(8,128)(2,1)S(1)} %all_to_all.32.own_ref), channel_id=1, source_target_pairs={{0,8},{8,0},{16,24},{24,16},{32,40},{40,32},{48,56},{56,48},{64,72... | collective-permute-start | bytes 6291464 | tf_op jit(solution)/shard_map/ppermute | solution.py:271
  87.7 4.9 %collective-permute-start.1 = (bf16[2064,256]{1,0:T(8,128)(2,1)S(1)}, bf16[2064,256]{1,0:T(8,128)(2,1)S(1)}, u32[]{:S(2)}, u32[]{:S(2)}) collective-permute-start(bf16[2064,256]{1,0:T(8,128)(2,1)S(1)} %get-tuple-element.23), channel_id=1, source_target_pairs={{0,8},{8,0},{16,24},{24,16},{32,40},{40,32},{48,56},{56,48},{64,72... | collective-permute-start | bytes 3170312 | tf_op jit(solution)/shard_map/ppermute | solution.py:291
  93.6 45.5 %copy-start.1 = (s32[8,256]{1,0:T(8,128)S(1)}, s32[8,256]{1,0:T(8,128)}, u32[]{:S(2)}) copy-start(s32[8,256]{1,0:T(8,128)} %chosen_ref.1) | copy-start | bytes 24580

commit v5 on v4

--- a/solution.py
+++ b/solution.py
@@ -22,6 +22,19 @@
 ]
 OUTER = [[dp_index(y, z, 0) for z in range(NZ)] for y in range(NY)] + [
     [dp_index(2 * q + p, z, 1) for q in range(4)] for p in range(2) for z in range(NZ)
+]
+EVERY_OTHER_Y = [
+    [[dp_index(2 * q + p, z, c) for q in range(4)] for p in range(2) for z in range(NZ)]
+    for c in range(2)
+]
+ALL_Z = [[[dp_index(y, z, c) for z in range(NZ)] for y in range(NY)] for c in range(2)]
+FIRST = EVERY_OTHER_Y[0] + ALL_Z[1]
+SECOND = ALL_Z[0] + EVERY_OTHER_Y[1]
+NEIGHBOUR = [
+    (dp_index(y, z, c), dp_index((y + (1 if y % 2 == c else NY - 1)) % NY, z, c))
+    for y in range(NY)
+    for z in range(NZ)
+    for c in range(2)
 ]
 SWAP = [(d, d ^ 1) for d in range(NY * NZ * 2)]
 
@@ -108,10 +121,20 @@
     )
 
 
-def ready_kernel(slots_ref, own_ref, w_in_ref, x_ref, u_ref, turned_ref, x_sem, u_sem):
-    arrived = load_blocks(slots_ref, 0, own_ref, x_ref, u_ref, x_sem, u_sem)
+def ready_kernel(
+    slots_ref, own_ref, oth_ref, w_in_ref, x_ref, u_ref, turned_ref, x_sem, u_sem
+):
+    count = own_ref.shape[0] * own_ref.shape[1]
+    arrived = load_blocks(slots_ref, 0, own_ref, x_ref, u_ref, x_sem.at[0], u_sem.at[0])
+    arrived += load_blocks(slots_ref, count, oth_ref, x_ref, u_ref, x_sem.at[1], u_sem.at[1])
     turned_ref[...] = w_in_ref[...].T
     for copy in arrived:
+        copy.wait()
+
+
+def more_kernel(slots_ref, pair_ref, x_in, u_in, x_ref, u_ref, x_sem, u_sem):
+    count = pair_ref.shape[0] * pair_ref.shape[1]
+    for copy in load_blocks(slots_ref, 2 * count, pair_ref, x_ref, u_ref, x_sem, u_sem):
         copy.wait()
 
 
@@ -121,9 +144,9 @@
 ):
     weights = pltpu.make_async_copy(w_out_ref, held_ref, w_sem)
     weights.start()
-    slots = oth_ref.shape[0] * oth_ref.shape[1]
+    count = oth_ref.shape[0] * oth_ref.shape[1]
     feats = oth_ref.shape[2] // 2
-    x_done, u_done = load_blocks(slots_ref, slots, oth_ref, x_ref, u_ref, x_sem, u_sem)
+    x_done, u_done = load_blocks(slots_ref, 3 * count, oth_ref, x_ref, u_ref, x_sem, u_sem)
     x_done.wait()
     preact = contract(turned_ref[...], x_ref[...], 1, 0)
     u_done.wait()
@@ -137,8 +160,9 @@
     back_ref[...] = back
     scaled_ref[...] = (score * hidden).astype(BF)
     gate_ref[...] = gate
+    slots = 2 * count
     for s in range(slots):
-        at = block_rows(slots_ref, slots + s, feats)
+        at = block_rows(slots_ref, 3 * slots + s, feats)
         send_ref[pl.ds(s * feats, feats), :] = contract(w_in_ref[at, :], back, 1, 0).astype(BF)
     send_ref[pl.ds(slots * feats, 16), :] = gate_tile([hi_lo(gate)])
 
@@ -159,7 +183,7 @@
     for k in range(parts):
         for i in range(8):
             s = k * 8 + i
-            mine = contract(w_in_ref[block_rows(slots_ref, s, feats), :], back, 1, 0)
+            mine = contract(w_in_ref[block_rows(slots_ref, 2 * 8 * parts + s, feats), :], back, 1, 0)
             other = got_ref[pl.ds(s * feats, feats), :].astype(F32)
             out_ref[k, pl.ds(i * feats, feats), :] = (mine + other).astype(BF)
         out_ref[k, rows:, :] = packed
@@ -244,14 +268,32 @@
     return jnp.where(core == 0, zero, one).reshape(-1)
 
 
+def half_table(core, parity):
+    o = jnp.arange(4, dtype=jnp.int32)[:, None]
+    i = jnp.arange(4, dtype=jnp.int32)[None, :]
+    zero = dp_index(2 * i + parity, o, 0)
+    one = dp_index(2 * o + parity, i, 1)
+    return jnp.where(core == 0, zero, one).reshape(-1)
+
+
 def per_device(activations, out_grad, w_in, w_out, chosen, gate_scores):
     tokens, feats = activations.shape
     experts, rows = chosen.shape
     depth, units = w_in.shape[1], w_in.shape[2]
     base = (lax.axis_index("expert") * tokens).astype(jnp.int32).reshape(1)
-    core = lax.axis_index("dp").astype(jnp.int32) & 1
-    slots = jnp.concatenate([block_table(core), block_table(1 - core)])
-    count = slots.shape[0] // 2
+    index = lax.axis_index("dp").astype(jnp.int32)
+    core, parity = index & 1, (index >> 3) & 1
+    slots = jnp.concatenate(
+        [
+            half_table(core, parity),
+            half_table(1 - core, parity),
+            half_table(core, 1 - parity),
+            half_table(1 - core, 1 - parity),
+            block_table(core),
+            block_table(1 - core),
+        ]
+    )
+    count = slots.shape[0] // 4
 
     picked = call(
         pick_kernel,
@@ -265,15 +307,23 @@
         ],
     )
     picked = exchange(picked, "expert")
-    mine = call(merge_kernel, [VMEM], [((8, 2 * feats, rows), BF)], picked)
-    inner = exchange(mine, "dp", INNER)
-    own = exchange(jnp.broadcast_to(inner[None], (4,) + inner.shape), "dp", OUTER)
+    mine = call(merge_kernel, [VMEM], [((4, 2 * feats, rows), BF)], picked)
+    first = exchange(mine, "dp", FIRST)
+    own = exchange(jnp.broadcast_to(first[None], (4,) + first.shape), "dp", SECOND)
+    pair = lax.ppermute(own, "dp", NEIGHBOUR)
     other = lax.ppermute(own, "dp", SWAP)
     sems = [pltpu.SemaphoreType.DMA] * 2
     held = [((depth, rows), BF), ((depth, rows), BF)]
     x, u, turned = call(
-        ready_kernel, [SMEM, ANY, VMEM], held + [((units, depth), BF)], slots, own, w_in[0],
-        scratch=sems, flops=2 * MIB, moved=6 * MIB,
+        ready_kernel, [SMEM, ANY, ANY, VMEM], held + [((units, depth), BF)],
+        slots, own, other, w_in[0],
+        scratch=[pltpu.SemaphoreType.DMA((2,))] * 2, flops=2 * MIB, moved=6 * MIB,
+    )
+    pair, x, u, turned = lax.optimization_barrier((pair, x, u, turned))
+    other = lax.ppermute(pair, "dp", SWAP)
+    x, u = call(
+        more_kernel, [SMEM, ANY, VMEM, VMEM], held, slots, pair, x, u,
+        scratch=sems, alias={2: 0, 3: 1}, flops=2 * MIB, moved=3 * MIB,
     )
     x, u, back, scaled, gate, send = call(
         main_kernel,

time: 141 us -> 143 us (1.014)
  blocking collectives: 120 us -> 105 us
  waiting for transfers between devices: 0.16 us -> 10.7 us
  starting transfers between devices: 4.31 us -> 8.63 us
    all_to_all x6, blocking collectives: 120 us -> 105 us  [exchange(): return lax.all_to_all(parts, axis, 0, 0, axis_index_groups=groups)]
    ppermute x0 -> x2, waiting for transfers between devices: none -> 10.7 us  [the longest x1 9.6 us: per_device(): pair = lax.ppermute(own, 'dp', NEIGHBOUR)]
    ppermute x0 -> x2, starting transfers between devices: none -> 4.68 us  [the longest x1 2.64 us: per_device(): pair = lax.ppermute(own, 'dp', NEIGHBOUR)]
    pallas_call x9 -> x10, Pallas kernels: 15 us -> 16.4 us  [call(): pl.pallas_call(kernel, out_shape=shapes[0] if single else shapes, in_spec...]
  transfers between devices with their start and end apart: 2 -> 4, of which waited for: 1 -> 2; matrix products, arithmetic and copies ran while one was open for 0% -> 1% of each run, Pallas kernels for 5% -> 6%
where the time goes in v5:
time: 143 us; the launch traced here: 142 us
  blocking collectives  105 us (73%)
  Pallas kernels  16.4 us (11%)
  waiting for transfers between devices  10.7 us (7%)
  starting transfers between devices  8.63 us (6%)
    all_to_all x6, blocking collectives, exchange(): return lax.all_to_all(parts, axis, 0, 0, axis_index_groups=groups)  105 us
    pallas_call x10, Pallas kernels, call(): pl.pallas_call(kernel, out_shape=shapes[0] if single else shapes, in_spec...  16.4 us
    ppermute x1, waiting for transfers between devices, per_device(): pair = lax.ppermute(own, 'dp', NEIGHBOUR)  9.6 us
  transfers between devices with their start and end apart: 4, of which 2 were waited for; matrix products, arithmetic and copies ran while one was open for 1% of the time, Pallas kernels for 6%

profile of v5, /device:TPU:8, one launch (start us, length us, event | category | flops | bytes accessed | tf_op | source)
XLA Modules:
  0.0 142.1 jit_solution(301003259782707479)
XLA Ops:
  0.6 1.4 shard_map.93
  2.0 16.0 %all_to_all.30.parts_ref = bf16[8,128,256]{2,1,0:T(8,128)(2,1)S(1)} all-to-all(bf16[8,128,256]{2,1,0:T(8,128)(2,1)S(1)} %shard_map.93), channel_id=1, replica_groups=mesh['dp'=64,'expert'=8] {'expert'}, dimensions={0} | all-to-all | bytes 1048576 | tf_op jit(solution)/shard_map/all_to_all | solution.py:260
  18.1 16.6 %all_to_all.31 = bf16[4,128,256]{2,1,0:T(8,128)(2,1)S(1)} all-to-all(bf16[4,128,256]{2,1,0:T(8,128)(2,1)S(1)} %shard_map.94), channel_id=1, replica_groups={{0,128,256,384},{16,144,272,400},{32,160,288,416},{48,176,304,432},{64,..., dimensions={0} | all-to-all | bytes 524288 | tf_op jit(solution)/shard_map/all_to_all | solution.py:260
  34.7 0.1 broadcast_in_dim.6
  34.8 27.5 %all_to_all.32.own_ref = bf16[4,4,128,256]{3,2,1,0:T(8,128)(2,1)S(1)} all-to-all(bf16[4,4,128,256]{3,2,1,0:T(8,128)(2,1)S(1)} %broadcast_in_dim.6), channel_id=1, replica_groups={{0,16,32,48},{64,80,96,112},{128,144,160,176},{192,208,224,240},{256,27..., dimensions={0} | all-to-all | bytes 2097152 | tf_op jit(solution)/shard_map/all_to_all | solution.py:260
  62.3 1.9 %collective-permute-start.1 = (bf16[4,4,128,256]{3,2,1,0:T(8,128)(2,1)S(1)}, bf16[4,4,128,256]{3,2,1,0:T(8,128)(2,1)S(1)}, u32[]{:S(2)}, u32[]{:S(2)}) collective-permute-start(bf16[4,4,128,256]{3,2,1,0:T(8,128)(2,1)S(1)} %all_to_all.32.own_ref), channel_id=1, source_target_pairs={{0,8},{8,0},{16,24},{24,16},{32,40},{40,32},{48,56},{56,48},{64,72... | collective-permute-start | bytes 3145736 | tf_op jit(solution)/shard_map/ppermute | solution.py:314
  64.2 2.6 %collective-permute-start = (bf16[4,4,128,256]{3,2,1,0:T(8,128)(2,1)S(1)}, bf16[4,4,128,256]{3,2,1,0:T(8,128)(2,1)}, u32[]{:S(2)}, u32[]{:S(2)}) collective-permute-start(bf16[4,4,128,256]{3,2,1,0:T(8,128)(2,1)S(1)} %all_to_all.32.own_ref), channel_id=1, source_target_pairs={{0,64},{8,456},{16,80},{24,472},{32,96},{40,488},{48,112},{56,504}... | collective-permute-start | bytes 3145736 | tf_op jit(solution)/shard_map/ppermute | solution.py:313
  67.0 0.1 reshape.173
  67.2 0.1 select_n.92
  67.7 3.7 %shard_map.95 = (bf16[4096,256]{1,0:T(8,128)(2,1)S(1)}, bf16[4096,256]{1,0:T(8,128)(2,1)S(1)}, bf16[128,4096]{1,0:T(8,128)(2,1)S(1)}) custom-call(s32[128]{0:T(128)S(1)} %concatenate.3.slots_ref, bf16[4,4,128,256]{3,2,1,0:T(8,128)(2,1)S(1)} %all_to_all.32.own_ref, bf16[4,4,128,256]{3,2,1,0:T(8,128)(2,1)S(1)} %collective-permute-done.1.oth_ref, ...), custom_call_target="tpu_custom_call" | custom-call | flops 2097152 | bytes 6291456 | tf_op jit(solution)/shard_map/pallas_call | solution.py:243
  71.4 9.6 %collective-permute-done.pair_ref = bf16[4,4,128,256]{3,2,1,0:T(8,128)(2,1)} collective-permute-done((bf16[4,4,128,256]{3,2,1,0:T(8,128)(2,1)S(1)}, bf16[4,4,128,256]{3,2,1,0:T(8,128)(2,1)}, u32[]{:S(2)}, u32[]{:S(2)}) %collective-permute-start) | collective-permute-done | bytes 1048608 | tf_op jit(solution)/shard_map/ppermute | solution.py:313
  81.0 2.0 %collective-permute-start.2 = (bf16[4,4,128,256]{3,2,1,0:T(8,128)(2,1)}, bf16[4,4,128,256]{3,2,1,0:T(8,128)(2,1)S(1)}, u32[]{:S(2)}, u32[]{:S(2)}) collective-permute-start(bf16[4,4,128,256]{3,2,1,0:T(8,128)(2,1)} %collective-permute-done.pair_ref), channel_id=1, source_target_pairs={{0,8},{8,0},{16,24},{24,16},{32,40},{40,32},{48,56},{56,48},{64,72... | collective-permute-start | bytes 3145736 | tf_op jit(solution)/shard_map/ppermute | solution.py:323
  83.1 1.7 %shard_map.96 = (bf16[4096,256]{1,0:T(8,128)(2,1)S(1)}, bf16[4096,256]{1,0:T(8,128)(2,1)S(1)}) custom-call(s32[128]{0:T(128)S(1)} %concatenate.3.slots_ref, bf16[4,4,128,256]{3,2,1,0:T(8,128)(2,1)} %collective-permute-done.pair_ref, bf16[4096,256]{1,0:T(8,128)(2,1)S(1)} %get-tuple-element.30.x_in, ...), custom_call_target="tpu_custom_call", output_to_operand_aliasing={{0}: (2, {}), {1}: (3, {})} | custom-call | flops 2097152 | bytes 3145728 | tf_op jit(solution)/shard_map/pallas_call | solution.py:243
  84.8 1.1 collective-permute-done.2.oth_ref
  85.9 3.8 %shard_map.97 = (bf16[4096,256]{1,0:T(8,128)(2,1)S(1)}, bf16[4096,256]{1,0:T(8,128)(2,1)S(1)}, bf16[128,256]{1,0:T(8,128)(2,1)S(1)}, bf16[128,256]{1,0:T(8,128)(...) custom-call(s32[128]{0:T(128)S(1)} %concatenate.3.slots_ref, ...), custom_call_target="tpu_custom_call", output_to_operand_aliasing={{0}: (2, {}), {1}: (3, {})} | custom-call | tf_op jit(solution)/shard_map/pallas_call | solution.py:243
  89.7 2.0 %collective-permute-start.3 = (bf16[2064,256]{1,0:T(8,128)(2,1)S(1)}, bf16[2064,256]{1,0:T(8,128)(2,1)S(1)}, u32[]{:S(2)}, u32[]{:S(2)}) collective-permute-start(bf16[2064,256]{1,0:T(8,128)(2,1)S(1)} %get-tuple-element.35), channel_id=1, source_target_pairs={{0,8},{8,0},{16,24},{24,16},{32,40},{40,32},{48,56},{56,48},{64,72... | collective-permute-start | bytes 3170312 | tf_op jit(solution)/shard_map/ppermute | solution.py:341
  91.8 2.6 %shard_map.98 = (bf16[4096,128]{1,0:T(8,128)(2,1)}, bf16[128,4096]{1,0:T(8,128)(2,1)}) custom-call(bf16[4096,256]{1,0:T(8,128)(2,1)S(1)} %get-tuple-element.36.x_ref, bf16[4096,256]{1,0:T(8,128)(2,1)S(1)} %get-tuple-element.37.u_ref, bf16[128,256]{1,0:T(8,128)(2,1)S(1)} %get-tuple-element.38.back_ref, bf16[128,256]{1,0:T(8,128)(2,1)S(1)} %get-tuple-element.39.scaled_ref), custom_call_target="tpu_custom_call" | custom-call | flops 536870912 | bytes 6291456 | tf_op jit(solution)/shard_map/pallas_call | solution.py:243
  94.4 1.0 shard_map.99
  95.4 21.5 %all_to_all.33.got_ref = bf16[4,528,256]{2,1,0:T(8,128)(2,1)S(1)} all-to-all(bf16[4,528,256]{2,1,0:T(8,128)(2,1)S(1)} %shard_map.99), channel_id=1, replica_groups={{0,16,32,48},{64,80,96,112},{128,144,160,176},{192,208,224,240},{256,27..., dimensions={0} | all-to-all | bytes 2162688 | tf_op jit(solution)/shard_map/all_to_all | solution.py:260
  116.8 0.1 shard_map.100
  117.0 13.3 %all_to_all.34.got_ref = bf16[8,80,256]{2,1,0:T(8,128)(2,1)S(1)} all-to-all(bf16[8,80,256]{2,1,0:T(8,128)(2,1)S(1)} %shard_map.100), channel_id=1, replica_groups={{0,64,128,192,256,320,384,448},{16,80,144,208,272,336,400,464},{32,96,1..., dimensions={0} | all-to-all | bytes 655360 | tf_op jit(solution)/shard_map/all_to_all | solution.py:260
  130.2 0.6 shard_map.101
  130.8 9.8 %all_to_all.35.terms_ref = bf16[8,64,256]{2,1,0:T(8,128)(2,1)S(1)} all-to-all(bf16[8,64,256]{2,1,0:T(8,128)(2,1)S(1)} %get-tuple-element.46), channel_id=1, replica_groups=mesh['dp'=64,'expert'=8] {'expert'}, dimensions={0} | all-to-all | bytes 524288 | tf_op jit(solution)/shard_map/all_to_all | solution.py:260
  140.7 1.4 shard_map.102
  (21 shorter events, 0.7 us)
Async XLA Ops:
  18.1 49.6 %copy-start = (bf16[1,4096,128]{2,1,0:T(8,128)(2,1)S(1)}, bf16[1,4096,128]{2,1,0:T(8,128)(2,1)}, u32[]{:S(2)}) copy-start(bf16[1,4096,128]{2,1,0:T(8,128)(2,1)} %param.8) | copy-start | bytes 3145732
  62.3 5.4 %collective-permute-start.1 = (bf16[4,4,128,256]{3,2,1,0:T(8,128)(2,1)S(1)}, bf16[4,4,128,256]{3,2,1,0:T(8,128)(2,1)S(1)}, u32[]{:S(2)}, u32[]{:S(2)}) collective-permute-start(bf16[4,4,128,256]{3,2,1,0:T(8,128)(2,1)S(1)} %all_to_all.32.own_ref), channel_id=1, source_target_pairs={{0,8},{8,0},{16,24},{24,16},{32,40},{40,32},{48,56},{56,48},{64,72... | collective-permute-start | bytes 3145736 | tf_op jit(solution)/shard_map/ppermute | solution.py:314
  64.2 16.8 %collective-permute-start = (bf16[4,4,128,256]{3,2,1,0:T(8,128)(2,1)S(1)}, bf16[4,4,128,256]{3,2,1,0:T(8,128)(2,1)}, u32[]{:S(2)}, u32[]{:S(2)}) collective-permute-start(bf16[4,4,128,256]{3,2,1,0:T(8,128)(2,1)S(1)} %all_to_all.32.own_ref), channel_id=1, source_target_pairs={{0,64},{8,456},{16,80},{24,472},{32,96},{40,488},{48,112},{56,504}... | collective-permute-start | bytes 3145736 | tf_op jit(solution)/shard_map/ppermute | solution.py:313
  81.0 4.9 %copy-start.2 = (f32[1,256]{1,0:T(1,128)S(1)}, f32[1,256]{1,0:T(1,128)}, u32[]{:S(2)}) copy-start(f32[1,256]{1,0:T(1,128)} %score_ref.1) | copy-start | bytes 3076
  81.0 4.9 %collective-permute-start.2 = (bf16[4,4,128,256]{3,2,1,0:T(8,128)(2,1)}, bf16[4,4,128,256]{3,2,1,0:T(8,128)(2,1)S(1)}, u32[]{:S(2)}, u32[]{:S(2)}) collective-permute-start(bf16[4,4,128,256]{3,2,1,0:T(8,128)(2,1)} %collective-permute-done.pair_ref), channel_id=1, source_target_pairs={{0,8},{8,0},{16,24},{24,16},{32,40},{40,32},{48,56},{56,48},{64,72... | collective-permute-start | bytes 3145736 | tf_op jit(solution)/shard_map/ppermute | solution.py:323
  89.7 4.7 %collective-permute-start.3 = (bf16[2064,256]{1,0:T(8,128)(2,1)S(1)}, bf16[2064,256]{1,0:T(8,128)(2,1)S(1)}, u32[]{:S(2)}, u32[]{:S(2)}) collective-permute-start(bf16[2064,256]{1,0:T(8,128)(2,1)S(1)} %get-tuple-element.35), channel_id=1, source_target_pairs={{0,8},{8,0},{16,24},{24,16},{32,40},{40,32},{48,56},{56,48},{64,72... | collective-permute-start | bytes 3170312 | tf_op jit(solution)/shard_map/ppermute | solution.py:341
  95.3 45.3 %copy-start.1 = (s32[8,256]{1,0:T(8,128)S(1)}, s32[8,256]{1,0:T(8,128)}, u32[]{:S(2)}) copy-start(s32[8,256]{1,0:T(8,128)} %chosen_ref.1) | copy-start | bytes 24580

commit v6 on v4

--- a/solution.py
+++ b/solution.py
@@ -17,11 +17,11 @@
     return (y * NZ + z) * 2 + core
 
 
-INNER = [[dp_index(y, z, 0) for y in range(NY)] for z in range(NZ)] + [
-    [dp_index(2 * q + p, z, 1) for p in range(2) for z in range(NZ)] for q in range(4)
+INNER = [[dp_index(y, z, 1) for y in range(NY)] for z in range(NZ)] + [
+    [dp_index(2 * q + p, z, 0) for p in range(2) for z in range(NZ)] for q in range(4)
 ]
-OUTER = [[dp_index(y, z, 0) for z in range(NZ)] for y in range(NY)] + [
-    [dp_index(2 * q + p, z, 1) for q in range(4)] for p in range(2) for z in range(NZ)
+OUTER = [[dp_index(y, z, 1) for z in range(NZ)] for y in range(NY)] + [
+    [dp_index(2 * q + p, z, 0) for q in range(4)] for p in range(2) for z in range(NZ)
 ]
 SWAP = [(d, d ^ 1) for d in range(NY * NZ * 2)]
 
@@ -190,11 +190,11 @@
         out_ref[k] = total
     tiles = [got_ref[i, rows:, :].astype(F32) for i in range(sources)]
     gates = [[t[2 * o : 2 * o + 1] + t[2 * o + 1 : 2 * o + 2] for o in range(4)] for t in tiles]
-    first = core_ref[0] == 0
+    along_y = core_ref[0] == 1
     gate = jnp.zeros((1, got_ref.shape[2]), F32)
     for y in range(NY):
         for z in range(NZ):
-            gate = gate + jnp.where(first, gates[y][z], gates[(y % 2) * NZ + z][y // 2])
+            gate = gate + jnp.where(along_y, gates[y][z], gates[(y % 2) * NZ + z][y // 2])
     gate_ref[...] = gate
 
 
@@ -239,8 +239,8 @@
 def block_table(core):
     o = jnp.arange(4, dtype=jnp.int32)[:, None]
     i = jnp.arange(8, dtype=jnp.int32)[None, :]
-    zero = dp_index(i, o, 0)
-    one = dp_index(2 * o + i // NZ, i % NZ, 1)
+    zero = dp_index(2 * o + i // NZ, i % NZ, 0)
+    one = dp_index(i, o, 1)
     return jnp.where(core == 0, zero, one).reshape(-1)
 
 

time: 141 us -> 141 us (level)
  transfers between devices with their start and end apart: 2 -> 2, of which waited for: 1 -> 1; matrix products, arithmetic and copies ran while one was open for 0% -> 0% of each run, Pallas kernels for 5% -> 4%
where the time goes in v6:
time: 141 us
  blocking collectives  120 us (85%)
  Pallas kernels  15 us (11%)
  starting transfers between devices  4.31 us (3%)
    all_to_all x6, blocking collectives, exchange(): return lax.all_to_all(parts, axis, 0, 0, axis_index_groups=groups)  120 us
    pallas_call x9, Pallas kernels, call(): pl.pallas_call(kernel, out_shape=shapes[0] if single else shapes, in_spec...  15 us
  transfers between devices with their start and end apart: 2, of which 1 were waited for; matrix products, arithmetic and copies ran while one was open for 0% of the time, Pallas kernels for 4%

profile of v6, /device:TPU:8, one launch (start us, length us, event | category | flops | bytes accessed | tf_op | source)
XLA Modules:
  0.0 140.9 jit_solution(9591257409313987992)
XLA Ops:
  0.6 1.4 shard_map.93
  2.0 16.0 %all_to_all.30.parts_ref = bf16[8,128,256]{2,1,0:T(8,128)(2,1)S(1)} all-to-all(bf16[8,128,256]{2,1,0:T(8,128)(2,1)S(1)} %shard_map.93), channel_id=1, replica_groups=mesh['dp'=64,'expert'=8] {'expert'}, dimensions={0} | all-to-all | bytes 1048576 | tf_op jit(solution)/shard_map/all_to_all | solution.py:236
  18.0 0.1 shard_map.94
  18.1 22.4 %all_to_all.31 = bf16[8,128,256]{2,1,0:T(8,128)(2,1)S(1)} all-to-all(bf16[8,128,256]{2,1,0:T(8,128)(2,1)S(1)} %shard_map.94), channel_id=1, replica_groups={{8,72,136,200,264,328,392,456},{24,88,152,216,280,344,408,472},{40,104,..., dimensions={0} | all-to-all | bytes 1048576 | tf_op jit(solution)/shard_map/all_to_all | solution.py:236
  40.5 0.2 broadcast_in_dim.6
  40.8 0.0 copy-start
  40.8 36.8 %all_to_all.32.own_ref = bf16[4,8,128,256]{3,2,1,0:T(8,128)(2,1)S(1)} all-to-all(bf16[4,8,128,256]{3,2,1,0:T(8,128)(2,1)S(1)} %broadcast_in_dim.6), channel_id=1, replica_groups={{8,24,40,56},{72,88,104,120},{136,152,168,184},{200,216,232,248},{264,2..., dimensions={0} | all-to-all | bytes 4194304 | tf_op jit(solution)/shard_map/all_to_all | solution.py:236
  77.6 2.0 %collective-permute-start = (bf16[4,8,128,256]{3,2,1,0:T(8,128)(2,1)S(1)}, bf16[4,8,128,256]{3,2,1,0:T(8,128)(2,1)}, u32[]{:S(2)}, u32[]{:S(2)}) collective-permute-start(bf16[4,8,128,256]{3,2,1,0:T(8,128)(2,1)S(1)} %all_to_all.32.own_ref), channel_id=1, source_target_pairs={{0,8},{8,0},{16,24},{24,16},{32,40},{40,32},{48,56},{56,48},{64,72... | collective-permute-start | bytes 6291464 | tf_op jit(solution)/shard_map/ppermute | solution.py:271
  79.7 0.1 fusion
  79.7 0.1 reshape.103
  79.8 0.1 reshape.105
  79.9 0.1 pad_add_fusion.slots_ref
  80.0 3.7 %shard_map.95 = (bf16[4096,256]{1,0:T(8,128)(2,1)S(1)}, bf16[4096,256]{1,0:T(8,128)(2,1)S(1)}, bf16[128,4096]{1,0:T(8,128)(2,1)S(1)}) custom-call(s32[64]{0:T(128)S(1)} %pad_add_fusion.slots_ref, bf16[4,8,128,256]{3,2,1,0:T(8,128)(2,1)S(1)} %all_to_all.32.own_ref, bf16[4096,128]{1,0:T(8,128)(2,1)S(1)} %bitcast.9), custom_call_target="tpu_custom_call" | custom-call | flops 2097152 | bytes 6291456 | tf_op jit(solution)/shard_map/pallas_call | solution.py:219
  83.7 0.2 collective-permute-done.oth_ref
  83.9 4.2 %shard_map.96 = (bf16[4096,256]{1,0:T(8,128)(2,1)S(1)}, bf16[4096,256]{1,0:T(8,128)(2,1)S(1)}, bf16[128,256]{1,0:T(8,128)(2,1)S(1)}, bf16[128,256]{1,0:T(8,128)(...) custom-call(s32[64]{0:T(128)S(1)} %pad_add_fusion.slots_ref, ...), custom_call_target="tpu_custom_call", output_to_operand_aliasing={{0}: (2, {}), {1}: (3, {})} | custom-call | tf_op jit(solution)/shard_map/pallas_call | solution.py:219
  88.0 2.3 %collective-permute-start.1 = (bf16[2064,256]{1,0:T(8,128)(2,1)S(1)}, bf16[2064,256]{1,0:T(8,128)(2,1)S(1)}, u32[]{:S(2)}, u32[]{:S(2)}) collective-permute-start(bf16[2064,256]{1,0:T(8,128)(2,1)S(1)} %get-tuple-element.23), channel_id=1, source_target_pairs={{0,8},{8,0},{16,24},{24,16},{32,40},{40,32},{48,56},{56,48},{64,72... | collective-permute-start | bytes 3170312 | tf_op jit(solution)/shard_map/ppermute | solution.py:291
  90.3 2.6 %shard_map.97 = (bf16[4096,128]{1,0:T(8,128)(2,1)}, bf16[128,4096]{1,0:T(8,128)(2,1)}) custom-call(bf16[4096,256]{1,0:T(8,128)(2,1)S(1)} %get-tuple-element.24.x_ref, bf16[4096,256]{1,0:T(8,128)(2,1)S(1)} %get-tuple-element.25.u_ref, bf16[128,256]{1,0:T(8,128)(2,1)S(1)} %get-tuple-element.26.back_ref, bf16[128,256]{1,0:T(8,128)(2,1)S(1)} %get-tuple-element.27.scaled_ref), custom_call_target="tpu_custom_call" | custom-call | flops 536870912 | bytes 6291456 | tf_op jit(solution)/shard_map/pallas_call | solution.py:219
  92.9 1.0 shard_map.98
  93.9 21.2 %all_to_all.33.got_ref = bf16[4,528,256]{2,1,0:T(8,128)(2,1)S(1)} all-to-all(bf16[4,528,256]{2,1,0:T(8,128)(2,1)S(1)} %shard_map.98), channel_id=1, replica_groups={{8,24,40,56},{72,88,104,120},{136,152,168,184},{200,216,232,248},{264,2..., dimensions={0} | all-to-all | bytes 2162688 | tf_op jit(solution)/shard_map/all_to_all | solution.py:236
  115.2 0.1 shard_map.99
  115.3 13.8 %all_to_all.34.got_ref = bf16[8,80,256]{2,1,0:T(8,128)(2,1)S(1)} all-to-all(bf16[8,80,256]{2,1,0:T(8,128)(2,1)S(1)} %shard_map.99), channel_id=1, replica_groups={{8,72,136,200,264,328,392,456},{24,88,152,216,280,344,408,472},{40,104,..., dimensions={0} | all-to-all | bytes 655360 | tf_op jit(solution)/shard_map/all_to_all | solution.py:236
  129.1 0.6 shard_map.100
  129.7 9.9 %all_to_all.35.terms_ref = bf16[8,64,256]{2,1,0:T(8,128)(2,1)S(1)} all-to-all(bf16[8,64,256]{2,1,0:T(8,128)(2,1)S(1)} %get-tuple-element.34), channel_id=1, replica_groups=mesh['dp'=64,'expert'=8] {'expert'}, dimensions={0} | all-to-all | bytes 524288 | tf_op jit(solution)/shard_map/all_to_all | solution.py:236
  139.6 1.4 shard_map.101
  (9 shorter events, 0.0 us)
Async XLA Ops:
  40.8 39.2 %copy-start = (bf16[1,4096,128]{2,1,0:T(8,128)(2,1)S(1)}, bf16[1,4096,128]{2,1,0:T(8,128)(2,1)}, u32[]{:S(2)}) copy-start(bf16[1,4096,128]{2,1,0:T(8,128)(2,1)} %param.8) | copy-start | bytes 3145732
  77.6 6.3 %copy-start.2 = (f32[1,256]{1,0:T(1,128)S(1)}, f32[1,256]{1,0:T(1,128)}, u32[]{:S(2)}) copy-start(f32[1,256]{1,0:T(1,128)} %score_ref.1) | copy-start | bytes 3076
  77.6 6.3 %collective-permute-start = (bf16[4,8,128,256]{3,2,1,0:T(8,128)(2,1)S(1)}, bf16[4,8,128,256]{3,2,1,0:T(8,128)(2,1)}, u32[]{:S(2)}, u32[]{:S(2)}) collective-permute-start(bf16[4,8,128,256]{3,2,1,0:T(8,128)(2,1)S(1)} %all_to_all.32.own_ref), channel_id=1, source_target_pairs={{0,8},{8,0},{16,24},{24,16},{32,40},{40,32},{48,56},{56,48},{64,72... | collective-permute-start | bytes 6291464 | tf_op jit(solution)/shard_map/ppermute | solution.py:271
  88.0 4.9 %collective-permute-start.1 = (bf16[2064,256]{1,0:T(8,128)(2,1)S(1)}, bf16[2064,256]{1,0:T(8,128)(2,1)S(1)}, u32[]{:S(2)}, u32[]{:S(2)}) collective-permute-start(bf16[2064,256]{1,0:T(8,128)(2,1)S(1)} %get-tuple-element.23), channel_id=1, source_target_pairs={{0,8},{8,0},{16,24},{24,16},{32,40},{40,32},{48,56},{56,48},{64,72... | collective-permute-start | bytes 3170312 | tf_op jit(solution)/shard_map/ppermute | solution.py:291
  93.9 45.6 %copy-start.1 = (s32[8,256]{1,0:T(8,128)S(1)}, s32[8,256]{1,0:T(8,128)}, u32[]{:S(2)}) copy-start(s32[8,256]{1,0:T(8,128)} %chosen_ref.1) | copy-start | bytes 24580

commit v7 on v5

--- a/solution.py
+++ b/solution.py
@@ -121,20 +121,19 @@
     )
 
 
-def ready_kernel(
-    slots_ref, own_ref, oth_ref, w_in_ref, x_ref, u_ref, turned_ref, x_sem, u_sem
-):
-    count = own_ref.shape[0] * own_ref.shape[1]
-    arrived = load_blocks(slots_ref, 0, own_ref, x_ref, u_ref, x_sem.at[0], u_sem.at[0])
-    arrived += load_blocks(slots_ref, count, oth_ref, x_ref, u_ref, x_sem.at[1], u_sem.at[1])
+def ready_kernel(slots_ref, own_ref, w_in_ref, x_ref, u_ref, turned_ref, x_sem, u_sem):
+    arrived = load_blocks(slots_ref, 0, own_ref, x_ref, u_ref, x_sem, u_sem)
     turned_ref[...] = w_in_ref[...].T
     for copy in arrived:
         copy.wait()
 
 
-def more_kernel(slots_ref, pair_ref, x_in, u_in, x_ref, u_ref, x_sem, u_sem):
+def more_kernel(slots_ref, oth_ref, pair_ref, x_in, u_in, x_ref, u_ref, x_sem, u_sem):
     count = pair_ref.shape[0] * pair_ref.shape[1]
-    for copy in load_blocks(slots_ref, 2 * count, pair_ref, x_ref, u_ref, x_sem, u_sem):
+    copies = []
+    for k, ref in enumerate((oth_ref, pair_ref)):
+        copies += load_blocks(slots_ref, (k + 1) * count, ref, x_ref, u_ref, x_sem.at[k], u_sem.at[k])
+    for copy in copies:
         copy.wait()
 
 
@@ -311,19 +310,19 @@
     first = exchange(mine, "dp", FIRST)
     own = exchange(jnp.broadcast_to(first[None], (4,) + first.shape), "dp", SECOND)
     pair = lax.ppermute(own, "dp", NEIGHBOUR)
-    other = lax.ppermute(own, "dp", SWAP)
+    near = lax.ppermute(own, "dp", SWAP)
     sems = [pltpu.SemaphoreType.DMA] * 2
     held = [((depth, rows), BF), ((depth, rows), BF)]
     x, u, turned = call(
-        ready_kernel, [SMEM, ANY, ANY, VMEM], held + [((units, depth), BF)],
-        slots, own, other, w_in[0],
-        scratch=[pltpu.SemaphoreType.DMA((2,))] * 2, flops=2 * MIB, moved=6 * MIB,
-    )
-    pair, x, u, turned = lax.optimization_barrier((pair, x, u, turned))
+        ready_kernel, [SMEM, ANY, VMEM], held + [((units, depth), BF)], slots, own, w_in[0],
+        scratch=sems, flops=2 * MIB, moved=6 * MIB,
+    )
+    near, pair, x, u, turned = lax.optimization_barrier((near, pair, x, u, turned))
     other = lax.ppermute(pair, "dp", SWAP)
     x, u = call(
-        more_kernel, [SMEM, ANY, VMEM, VMEM], held, slots, pair, x, u,
-        scratch=sems, alias={2: 0, 3: 1}, flops=2 * MIB, moved=3 * MIB,
+        more_kernel, [SMEM, ANY, ANY, VMEM, VMEM], held, slots, near, pair, x, u,
+        scratch=[pltpu.SemaphoreType.DMA((2,))] * 2, alias={3: 0, 4: 1},
+        flops=2 * MIB, moved=3 * MIB,
     )
     x, u, back, scaled, gate, send = call(
         main_kernel,

time: 143 us -> 140 us (0.979)
  transfers between devices with their start and end apart: 4 -> 4, of which waited for: 2 -> 2; matrix products, arithmetic and copies ran while one was open for 1% -> 1% of each run, Pallas kernels for 6% -> 5%
where the time goes in v7:
time: 140 us; the launch traced here: 139 us
  blocking collectives  104 us (74%)
  Pallas kernels  15.3 us (11%)
  waiting for transfers between devices  9.58 us (7%)
  starting transfers between devices  8.63 us (6%)
    all_to_all x6, blocking collectives, exchange(): return lax.all_to_all(parts, axis, 0, 0, axis_index_groups=groups)  104 us
    pallas_call x10, Pallas kernels, call(): pl.pallas_call(kernel, out_shape=shapes[0] if single else shapes, in_spec...  15.3 us
    ppermute x1, waiting for transfers between devices, per_device(): pair = lax.ppermute(own, 'dp', NEIGHBOUR)  9 us
  transfers between devices with their start and end apart: 4, of which 2 were waited for; matrix products, arithmetic and copies ran while one was open for 1% of the time, Pallas kernels for 5%

profile of v7, /device:TPU:8, one launch (start us, length us, event | category | flops | bytes accessed | tf_op | source)
XLA Modules:
  0.0 139.4 jit_solution(8096884697088740488)
XLA Ops:
  0.6 1.4 shard_map.93
  2.0 16.0 %all_to_all.30.parts_ref = bf16[8,128,256]{2,1,0:T(8,128)(2,1)S(1)} all-to-all(bf16[8,128,256]{2,1,0:T(8,128)(2,1)S(1)} %shard_map.93), channel_id=1, replica_groups=mesh['dp'=64,'expert'=8] {'expert'}, dimensions={0} | all-to-all | bytes 1048576 | tf_op jit(solution)/shard_map/all_to_all | solution.py:259
  18.1 16.6 %all_to_all.31 = bf16[4,128,256]{2,1,0:T(8,128)(2,1)S(1)} all-to-all(bf16[4,128,256]{2,1,0:T(8,128)(2,1)S(1)} %shard_map.94), channel_id=1, replica_groups={{0,128,256,384},{16,144,272,400},{32,160,288,416},{48,176,304,432},{64,..., dimensions={0} | all-to-all | bytes 524288 | tf_op jit(solution)/shard_map/all_to_all | solution.py:259
  34.7 0.1 broadcast_in_dim.6
  34.8 27.5 %all_to_all.32.own_ref = bf16[4,4,128,256]{3,2,1,0:T(8,128)(2,1)S(1)} all-to-all(bf16[4,4,128,256]{3,2,1,0:T(8,128)(2,1)S(1)} %broadcast_in_dim.6), channel_id=1, replica_groups={{0,16,32,48},{64,80,96,112},{128,144,160,176},{192,208,224,240},{256,27..., dimensions={0} | all-to-all | bytes 2097152 | tf_op jit(solution)/shard_map/all_to_all | solution.py:259
  62.3 2.6 %collective-permute-start.1 = (bf16[4,4,128,256]{3,2,1,0:T(8,128)(2,1)S(1)}, bf16[4,4,128,256]{3,2,1,0:T(8,128)(2,1)S(1)}, u32[]{:S(2)}, u32[]{:S(2)}) collective-permute-start(bf16[4,4,128,256]{3,2,1,0:T(8,128)(2,1)S(1)} %all_to_all.32.own_ref), channel_id=1, source_target_pairs={{0,64},{8,456},{16,80},{24,472},{32,96},{40,488},{48,112},{56,504}... | collective-permute-start | bytes 3145736 | tf_op jit(solution)/shard_map/ppermute | solution.py:312
  64.9 1.9 %collective-permute-start = (bf16[4,4,128,256]{3,2,1,0:T(8,128)(2,1)S(1)}, bf16[4,4,128,256]{3,2,1,0:T(8,128)(2,1)}, u32[]{:S(2)}, u32[]{:S(2)}) collective-permute-start(bf16[4,4,128,256]{3,2,1,0:T(8,128)(2,1)S(1)} %all_to_all.32.own_ref), channel_id=1, source_target_pairs={{0,8},{8,0},{16,24},{24,16},{32,40},{40,32},{48,56},{56,48},{64,72... | collective-permute-start | bytes 3145736 | tf_op jit(solution)/shard_map/ppermute | solution.py:313
  67.0 0.1 reshape.173
  67.2 0.1 select_n.92
  67.7 2.3 %shard_map.95 = (bf16[4096,256]{1,0:T(8,128)(2,1)S(1)}, bf16[4096,256]{1,0:T(8,128)(2,1)S(1)}, bf16[128,4096]{1,0:T(8,128)(2,1)S(1)}) custom-call(s32[128]{0:T(128)S(1)} %concatenate.3.slots_ref, bf16[4,4,128,256]{3,2,1,0:T(8,128)(2,1)S(1)} %all_to_all.32.own_ref, bf16[4096,128]{1,0:T(8,128)(2,1)S(1)} %bitcast.9), custom_call_target="tpu_custom_call" | custom-call | flops 2097152 | bytes 6291456 | tf_op jit(solution)/shard_map/pallas_call | solution.py:242
  70.0 9.0 %collective-permute-done.1.pair_ref = bf16[4,4,128,256]{3,2,1,0:T(8,128)(2,1)S(1)} collective-permute-done((bf16[4,4,128,256]{3,2,1,0:T(8,128)(2,1)S(1)}, bf16[4,4,128,256]{3,2,1,0:T(8,128)(2,1)S(1)}, u32[]{:S(2)}, u32[]{:S(2)}) %collective-permute-start.1) | collective-permute-done | bytes 1048608 | tf_op jit(solution)/shard_map/ppermute | solution.py:312
  79.0 2.0 %collective-permute-start.2 = (bf16[4,4,128,256]{3,2,1,0:T(8,128)(2,1)S(1)}, bf16[4,4,128,256]{3,2,1,0:T(8,128)(2,1)S(1)}, u32[]{:S(2)}, u32[]{:S(2)}) collective-permute-start(bf16[4,4,128,256]{3,2,1,0:T(8,128)(2,1)S(1)} %collective-permute-done.1.pair_ref), channel_id=1, source_target_pairs={{0,8},{8,0},{16,24},{24,16},{32,40},{40,32},{48,56},{56,48},{64,72... | collective-permute-start | bytes 3145736 | tf_op jit(solution)/shard_map/ppermute | solution.py:321
  81.0 2.0 %shard_map.96 = (bf16[4096,256]{1,0:T(8,128)(2,1)S(1)}, bf16[4096,256]{1,0:T(8,128)(2,1)S(1)}) custom-call(s32[128]{0:T(128)S(1)} %concatenate.3.slots_ref, bf16[4,4,128,256]{3,2,1,0:T(8,128)(2,1)} %collective-permute-done.oth_ref, bf16[4,4,128,256]{3,2,1,0:T(8,128)(2,1)S(1)} %collective-permute-done.1.pair_ref, ...), custom_call_target="tpu_custom_call", output_to_operand_aliasing={{0}: (3, {}), {1}: (4, {})} | custom-call | flops 2097152 | bytes 3145728 | tf_op jit(solution)/shard_map/pallas_call | solution.py:242
  83.1 0.6 collective-permute-done.2.oth_ref
  83.7 3.8 %shard_map.97 = (bf16[4096,256]{1,0:T(8,128)(2,1)S(1)}, bf16[4096,256]{1,0:T(8,128)(2,1)S(1)}, bf16[128,256]{1,0:T(8,128)(2,1)S(1)}, bf16[128,256]{1,0:T(8,128)(...) custom-call(s32[128]{0:T(128)S(1)} %concatenate.3.slots_ref, ...), custom_call_target="tpu_custom_call", output_to_operand_aliasing={{0}: (2, {}), {1}: (3, {})} | custom-call | tf_op jit(solution)/shard_map/pallas_call | solution.py:242
  87.5 2.0 %collective-permute-start.3 = (bf16[2064,256]{1,0:T(8,128)(2,1)S(1)}, bf16[2064,256]{1,0:T(8,128)(2,1)S(1)}, u32[]{:S(2)}, u32[]{:S(2)}) collective-permute-start(bf16[2064,256]{1,0:T(8,128)(2,1)S(1)} %get-tuple-element.37), channel_id=1, source_target_pairs={{0,8},{8,0},{16,24},{24,16},{32,40},{40,32},{48,56},{56,48},{64,72... | collective-permute-start | bytes 3170312 | tf_op jit(solution)/shard_map/ppermute | solution.py:340
  89.5 2.6 %shard_map.98 = (bf16[4096,128]{1,0:T(8,128)(2,1)}, bf16[128,4096]{1,0:T(8,128)(2,1)}) custom-call(bf16[4096,256]{1,0:T(8,128)(2,1)S(1)} %get-tuple-element.38.x_ref, bf16[4096,256]{1,0:T(8,128)(2,1)S(1)} %get-tuple-element.39.u_ref, bf16[128,256]{1,0:T(8,128)(2,1)S(1)} %get-tuple-element.40.back_ref, bf16[128,256]{1,0:T(8,128)(2,1)S(1)} %get-tuple-element.41.scaled_ref), custom_call_target="tpu_custom_call" | custom-call | flops 536870912 | bytes 6291456 | tf_op jit(solution)/shard_map/pallas_call | solution.py:242
  92.1 1.0 shard_map.99
  93.1 21.5 %all_to_all.33.got_ref = bf16[4,528,256]{2,1,0:T(8,128)(2,1)S(1)} all-to-all(bf16[4,528,256]{2,1,0:T(8,128)(2,1)S(1)} %shard_map.99), channel_id=1, replica_groups={{0,16,32,48},{64,80,96,112},{128,144,160,176},{192,208,224,240},{256,27..., dimensions={0} | all-to-all | bytes 2162688 | tf_op jit(solution)/shard_map/all_to_all | solution.py:259
  114.6 0.1 shard_map.100
  114.7 12.8 %all_to_all.34.got_ref = bf16[8,80,256]{2,1,0:T(8,128)(2,1)S(1)} all-to-all(bf16[8,80,256]{2,1,0:T(8,128)(2,1)S(1)} %shard_map.100), channel_id=1, replica_groups={{0,64,128,192,256,320,384,448},{16,80,144,208,272,336,400,464},{32,96,1..., dimensions={0} | all-to-all | bytes 655360 | tf_op jit(solution)/shard_map/all_to_all | solution.py:259
  127.6 0.6 shard_map.101
  128.2 9.8 %all_to_all.35.terms_ref = bf16[8,64,256]{2,1,0:T(8,128)(2,1)S(1)} all-to-all(bf16[8,64,256]{2,1,0:T(8,128)(2,1)S(1)} %get-tuple-element.48), channel_id=1, replica_groups=mesh['dp'=64,'expert'=8] {'expert'}, dimensions={0} | all-to-all | bytes 524288 | tf_op jit(solution)/shard_map/all_to_all | solution.py:259
  138.0 1.4 shard_map.102
  (21 shorter events, 0.7 us)
Async XLA Ops:
  18.1 49.6 %copy-start = (bf16[1,4096,128]{2,1,0:T(8,128)(2,1)S(1)}, bf16[1,4096,128]{2,1,0:T(8,128)(2,1)}, u32[]{:S(2)}) copy-start(bf16[1,4096,128]{2,1,0:T(8,128)(2,1)} %param.8) | copy-start | bytes 3145732
  62.3 16.7 %collective-permute-start.1 = (bf16[4,4,128,256]{3,2,1,0:T(8,128)(2,1)S(1)}, bf16[4,4,128,256]{3,2,1,0:T(8,128)(2,1)S(1)}, u32[]{:S(2)}, u32[]{:S(2)}) collective-permute-start(bf16[4,4,128,256]{3,2,1,0:T(8,128)(2,1)S(1)} %all_to_all.32.own_ref), channel_id=1, source_target_pairs={{0,64},{8,456},{16,80},{24,472},{32,96},{40,488},{48,112},{56,504}... | collective-permute-start | bytes 3145736 | tf_op jit(solution)/shard_map/ppermute | solution.py:312
  64.9 14.1 %collective-permute-start = (bf16[4,4,128,256]{3,2,1,0:T(8,128)(2,1)S(1)}, bf16[4,4,128,256]{3,2,1,0:T(8,128)(2,1)}, u32[]{:S(2)}, u32[]{:S(2)}) collective-permute-start(bf16[4,4,128,256]{3,2,1,0:T(8,128)(2,1)S(1)} %all_to_all.32.own_ref), channel_id=1, source_target_pairs={{0,8},{8,0},{16,24},{24,16},{32,40},{40,32},{48,56},{56,48},{64,72... | collective-permute-start | bytes 3145736 | tf_op jit(solution)/shard_map/ppermute | solution.py:313
  79.0 4.7 %copy-start.2 = (f32[1,256]{1,0:T(1,128)S(1)}, f32[1,256]{1,0:T(1,128)}, u32[]{:S(2)}) copy-start(f32[1,256]{1,0:T(1,128)} %score_ref.1) | copy-start | bytes 3076
  79.0 4.7 %collective-permute-start.2 = (bf16[4,4,128,256]{3,2,1,0:T(8,128)(2,1)S(1)}, bf16[4,4,128,256]{3,2,1,0:T(8,128)(2,1)S(1)}, u32[]{:S(2)}, u32[]{:S(2)}) collective-permute-start(bf16[4,4,128,256]{3,2,1,0:T(8,128)(2,1)S(1)} %collective-permute-done.1.pair_ref), channel_id=1, source_target_pairs={{0,8},{8,0},{16,24},{24,16},{32,40},{40,32},{48,56},{56,48},{64,72... | collective-permute-start | bytes 3145736 | tf_op jit(solution)/shard_map/ppermute | solution.py:321
  87.5 4.7 %collective-permute-start.3 = (bf16[2064,256]{1,0:T(8,128)(2,1)S(1)}, bf16[2064,256]{1,0:T(8,128)(2,1)S(1)}, u32[]{:S(2)}, u32[]{:S(2)}) collective-permute-start(bf16[2064,256]{1,0:T(8,128)(2,1)S(1)} %get-tuple-element.37), channel_id=1, source_target_pairs={{0,8},{8,0},{16,24},{24,16},{32,40},{40,32},{48,56},{56,48},{64,72... | collective-permute-start | bytes 3170312 | tf_op jit(solution)/shard_map/ppermute | solution.py:340
  93.1 44.9 %copy-start.1 = (s32[8,256]{1,0:T(8,128)S(1)}, s32[8,256]{1,0:T(8,128)}, u32[]{:S(2)}) copy-start(s32[8,256]{1,0:T(8,128)} %chosen_ref.1) | copy-start | bytes 24580

commit v8 on v7

--- a/solution.py
+++ b/solution.py
@@ -17,12 +17,6 @@
     return (y * NZ + z) * 2 + core
 
 
-INNER = [[dp_index(y, z, 0) for y in range(NY)] for z in range(NZ)] + [
-    [dp_index(2 * q + p, z, 1) for p in range(2) for z in range(NZ)] for q in range(4)
-]
-OUTER = [[dp_index(y, z, 0) for z in range(NZ)] for y in range(NY)] + [
-    [dp_index(2 * q + p, z, 1) for q in range(4)] for p in range(2) for z in range(NZ)
-]
 EVERY_OTHER_Y = [
     [[dp_index(2 * q + p, z, c) for q in range(4)] for p in range(2) for z in range(NZ)]
     for c in range(2)
@@ -161,7 +155,7 @@
     gate_ref[...] = gate
     slots = 2 * count
     for s in range(slots):
-        at = block_rows(slots_ref, 3 * slots + s, feats)
+        at = block_rows(slots_ref, s + count * (1 + s // count), feats)
         send_ref[pl.ds(s * feats, feats), :] = contract(w_in_ref[at, :], back, 1, 0).astype(BF)
     send_ref[pl.ds(slots * feats, 16), :] = gate_tile([hi_lo(gate)])
 
@@ -171,20 +165,34 @@
     gout_ref[...] = contract(scaled_ref[...], u_ref[...], 1, 1).astype(BF)
 
 
-def pair_kernel(slots_ref, w_in_ref, back_ref, gate_ref, got_ref, out_ref):
-    parts, rows = out_ref.shape[0], out_ref.shape[1] - 16
-    feats = rows // 8
-    back = back_ref[...]
-    tile = got_ref[pl.ds(parts * rows, 16), :].astype(F32)
+def add_blocks(slots_ref, first, w_in_ref, back, got_ref, base, out_ref):
+    feats = 64
+    for s in range(16):
+        mine = contract(w_in_ref[block_rows(slots_ref, first + s, feats), :], back, 1, 0)
+        other = got_ref[pl.ds(base + s * feats, feats), :].astype(F32)
+        out_ref[pl.ds(s * feats, feats), :] = (mine + other).astype(out_ref.dtype)
+
+
+def far_kernel(slots_ref, w_in_ref, back_ref, gate_ref, got_ref, far_ref):
+    rows = far_ref.shape[0] - 16
+    add_blocks(slots_ref, 32, w_in_ref, back_ref[...], got_ref, rows, far_ref)
+    tile = got_ref[pl.ds(2 * rows, 16), :].astype(F32)
     high, low = hi_lo(gate_ref[...])
     gate = (high.astype(F32) + low.astype(F32)) + (tile[0:1] + tile[1:2])
-    packed = gate_tile([hi_lo(gate)])
+    far_ref[pl.ds(rows, 16), :] = gate_tile([hi_lo(gate)])
+
+
+def near_kernel(slots_ref, w_in_ref, back_ref, got_ref, near_ref):
+    add_blocks(slots_ref, 0, w_in_ref, back_ref[...], got_ref, 0, near_ref)
+
+
+def join_kernel(near_ref, far_ref, got_ref, out_ref):
+    parts, rows = out_ref.shape[0], out_ref.shape[1] - 16
+    tiles = [ref[pl.ds(parts * rows, 16), :].astype(F32) for ref in (far_ref, got_ref)]
+    packed = gate_tile([(t[0:1], t[1:2]) for t in tiles])
     for k in range(parts):
-        for i in range(8):
-            s = k * 8 + i
-            mine = contract(w_in_ref[block_rows(slots_ref, 2 * 8 * parts + s, feats), :], back, 1, 0)
-            other = got_ref[pl.ds(s * feats, feats), :].astype(F32)
-            out_ref[k, pl.ds(i * feats, feats), :] = (mine + other).astype(BF)
+        at = pl.ds(k * rows, rows)
+        out_ref[k, :rows, :] = (near_ref[at, :] + got_ref[at, :].astype(F32)).astype(BF)
         out_ref[k, rows:, :] = packed
 
 
@@ -192,7 +200,7 @@
     count, rows = out_ref.shape[0], out_ref.shape[1] - 16
     base = count * rows
     tiles = [got_ref[o, pl.ds(base, 16), :].astype(F32) for o in range(4)]
-    packed = gate_tile([(t[0:1], t[1:2]) for t in tiles])
+    packed = jnp.concatenate([t[0:4] for t in tiles], axis=0).astype(BF)
     for i in range(count):
         at = pl.ds(i * rows, rows)
         total = got_ref[0, at, :].astype(F32)
@@ -202,7 +210,16 @@
         out_ref[i, rows:, :] = packed
 
 
-def inner_kernel(core_ref, got_ref, out_ref, gate_ref):
+def gate_source(core, parity, y, z):
+    odd = y % 2
+    if core == 0:
+        return y // 2, z, odd ^ parity
+    if odd == parity:
+        return z, y // 2, 0
+    return z, ((y + 1) // 2 if parity == 0 else (y + 6) // 2) % 4, 1
+
+
+def inner_kernel(place_ref, got_ref, out_ref, gate_ref):
     rows = out_ref.shape[1]
     sources = got_ref.shape[0]
     total = got_ref[0, :rows, :].astype(F32)
@@ -212,12 +229,19 @@
     for k in range(out_ref.shape[0]):
         out_ref[k] = total
     tiles = [got_ref[i, rows:, :].astype(F32) for i in range(sources)]
-    gates = [[t[2 * o : 2 * o + 1] + t[2 * o + 1 : 2 * o + 2] for o in range(4)] for t in tiles]
-    first = core_ref[0] == 0
+    gates = [[t[2 * j : 2 * j + 1] + t[2 * j + 1 : 2 * j + 2] for j in range(8)] for t in tiles]
+    place = place_ref[0]
     gate = jnp.zeros((1, got_ref.shape[2]), F32)
     for y in range(NY):
         for z in range(NZ):
-            gate = gate + jnp.where(first, gates[y][z], gates[(y % 2) * NZ + z][y // 2])
+            term = None
+            for core in range(2):
+                for parity in range(2):
+                    i, o, n = gate_source(core, parity, y, z)
+                    value = gates[i][2 * o + n]
+                    here = place == 2 * core + parity
+                    term = value if term is None else jnp.where(here, value, term)
+            gate = gate + term
     gate_ref[...] = gate
 
 
@@ -259,14 +283,6 @@
     return lax.all_to_all(parts, axis, 0, 0, axis_index_groups=groups)
 
 
-def block_table(core):
-    o = jnp.arange(4, dtype=jnp.int32)[:, None]
-    i = jnp.arange(8, dtype=jnp.int32)[None, :]
-    zero = dp_index(i, o, 0)
-    one = dp_index(2 * o + i // NZ, i % NZ, 1)
-    return jnp.where(core == 0, zero, one).reshape(-1)
-
-
 def half_table(core, parity):
     o = jnp.arange(4, dtype=jnp.int32)[:, None]
     i = jnp.arange(4, dtype=jnp.int32)[None, :]
@@ -288,11 +304,9 @@
             half_table(1 - core, parity),
             half_table(core, 1 - parity),
             half_table(1 - core, 1 - parity),
-            block_table(core),
-            block_table(1 - core),
         ]
     )
-    count = slots.shape[0] // 4
+    count = slots.shape[0] // 2
 
     picked = call(
         pick_kernel,
@@ -345,18 +359,24 @@
         x, u, back, scaled, flops=4 * depth * units * rows, moved=6 * depth * rows,
     )
     got, weight_in_grad, weight_out_grad = lax.optimization_barrier((got, *weight_grads))
-    part = call(
-        pair_kernel,
-        [SMEM] + [VMEM] * 4,
-        [((4, 8 * feats + 16, rows), BF)],
+    half = count * feats // 2
+    far = call(
+        far_kernel, [SMEM] + [VMEM] * 4, [((half + 16, rows), BF)],
         slots, w_in[0], back, gate, got,
     )
-    part = exchange(part, "dp", OUTER)
-    part = call(outer_kernel, [VMEM], [((8, feats + 16, rows), BF)], part)
-    part = exchange(part, "dp", INNER)
+    come = lax.ppermute(far, "dp", NEIGHBOUR)
+    near = call(
+        near_kernel, [SMEM] + [VMEM] * 3, [((half, rows), F32)], slots, w_in[0], back, got,
+        flops=depth * units * rows // 2, moved=4 * MIB,
+    )
+    near, come = lax.optimization_barrier((near, come))
+    part = call(join_kernel, [VMEM] * 3, [((4, 4 * feats + 16, rows), BF)], near, far, come)
+    part = exchange(part, "dp", SECOND)
+    part = call(outer_kernel, [VMEM], [((4, feats + 16, rows), BF)], part)
+    part = exchange(part, "dp", FIRST)
     term, gate_grad = call(
         inner_kernel, [SMEM, VMEM], [((experts, feats, rows), BF), ((1, rows), F32)],
-        core.reshape(1), part,
+        (2 * core + parity).reshape(1), part,
     )
     terms = exchange(term, "expert")
     act_grad = call(

time: 140 us -> 145 us (1.036)
  blocking collectives: 104 us -> 85.8 us
  waiting for transfers between devices: 9.58 us -> 26.1 us
  starting transfers between devices: 8.63 us -> 14.6 us
    all_to_all x6 -> x5, blocking collectives: 104 us -> 85.8 us  [exchange(): return lax.all_to_all(parts, axis, 0, 0, axis_index_groups=groups)]
    all_to_all x0 -> x1, waiting for transfers between devices: none -> 8.52 us  [exchange(): return lax.all_to_all(parts, axis, 0, 0, axis_index_groups=groups)]
    ppermute x0 -> x1, waiting for transfers between devices: none -> 7.68 us  [per_device(): come = lax.ppermute(far, 'dp', NEIGHBOUR)]
    all_to_all x0 -> x1, starting transfers between devices: none -> 3.34 us  [exchange(): return lax.all_to_all(parts, axis, 0, 0, axis_index_groups=groups)]
    ppermute x0 -> x1, starting transfers between devices: none -> 2.63 us  [per_device(): come = lax.ppermute(far, 'dp', NEIGHBOUR)]
    pallas_call x10 -> x12, Pallas kernels: 15.3 us -> 16.7 us  [call(): pl.pallas_call(kernel, out_shape=shapes[0] if single else shapes, in_spec...]
  transfers between devices with their start and end apart: 4 -> 6, of which waited for: 2 -> 4; matrix products, arithmetic and copies ran while one was open for 1% -> 0% of each run, Pallas kernels for 5% -> 5%
where the time goes in v8:
time: 145 us
  blocking collectives  85.8 us (59%)
  waiting for transfers between devices  26.1 us (18%)
  Pallas kernels  16.7 us (12%)
  starting transfers between devices  14.6 us (10%)
    all_to_all x5, blocking collectives, exchange(): return lax.all_to_all(parts, axis, 0, 0, axis_index_groups=groups)  85.8 us
    pallas_call x12, Pallas kernels, call(): pl.pallas_call(kernel, out_shape=shapes[0] if single else shapes, in_spec...  16.7 us
    ppermute x1, waiting for transfers between devices, per_device(): pair = lax.ppermute(own, 'dp', NEIGHBOUR)  9.27 us
    all_to_all x1, waiting for transfers between devices, exchange(): return lax.all_to_all(parts, axis, 0, 0, axis_index_groups=groups)  8.52 us
    ppermute x1, waiting for transfers between devices, per_device(): come = lax.ppermute(far, 'dp', NEIGHBOUR)  7.68 us
    all_to_all x1, starting transfers between devices, exchange(): return lax.all_to_all(parts, axis, 0, 0, axis_index_groups=groups)  3.34 us
  transfers between devices with their start and end apart: 6, of which 4 were waited for; matrix products, arithmetic and copies ran while one was open for 0% of the time, Pallas kernels for 5%

profile of v8, /device:TPU:8, one launch (start us, length us, event | category | flops | bytes accessed | tf_op | source)
XLA Modules:
  0.0 144.6 jit_solution(8273071506843208314)
XLA Ops:
  0.6 1.4 shard_map.93
  2.0 16.0 %all_to_all.30.parts_ref = bf16[8,128,256]{2,1,0:T(8,128)(2,1)S(1)} all-to-all(bf16[8,128,256]{2,1,0:T(8,128)(2,1)S(1)} %shard_map.93), channel_id=1, replica_groups=mesh['dp'=64,'expert'=8] {'expert'}, dimensions={0} | all-to-all | bytes 1048576 | tf_op jit(solution)/shard_map/all_to_all | solution.py:283
  18.1 16.6 %all_to_all.31 = bf16[4,128,256]{2,1,0:T(8,128)(2,1)S(1)} all-to-all(bf16[4,128,256]{2,1,0:T(8,128)(2,1)S(1)} %shard_map.94), channel_id=1, replica_groups={{0,128,256,384},{16,144,272,400},{32,160,288,416},{48,176,304,432},{64,..., dimensions={0} | all-to-all | bytes 524288 | tf_op jit(solution)/shard_map/all_to_all | solution.py:283
  34.8 27.5 %all_to_all.32.own_ref = bf16[4,4,128,256]{3,2,1,0:T(8,128)(2,1)S(1)} all-to-all(bf16[4,4,128,256]{3,2,1,0:T(8,128)(2,1)S(1)} %broadcast_in_dim.6), channel_id=1, replica_groups={{0,16,32,48},{64,80,96,112},{128,144,160,176},{192,208,224,240},{256,27..., dimensions={0} | all-to-all | bytes 2097152 | tf_op jit(solution)/shard_map/all_to_all | solution.py:283
  62.3 2.6 %collective-permute-start.1 = (bf16[4,4,128,256]{3,2,1,0:T(8,128)(2,1)S(1)}, bf16[4,4,128,256]{3,2,1,0:T(8,128)(2,1)S(1)}, u32[]{:S(2)}, u32[]{:S(2)}) collective-permute-start(bf16[4,4,128,256]{3,2,1,0:T(8,128)(2,1)S(1)} %all_to_all.32.own_ref), channel_id=1, source_target_pairs={{0,64},{8,456},{16,80},{24,472},{32,96},{40,488},{48,112},{56,504}... | collective-permute-start | bytes 3145736 | tf_op jit(solution)/shard_map/ppermute | solution.py:326
  64.9 1.9 %collective-permute-start = (bf16[4,4,128,256]{3,2,1,0:T(8,128)(2,1)S(1)}, bf16[4,4,128,256]{3,2,1,0:T(8,128)(2,1)}, u32[]{:S(2)}, u32[]{:S(2)}) collective-permute-start(bf16[4,4,128,256]{3,2,1,0:T(8,128)(2,1)S(1)} %all_to_all.32.own_ref), channel_id=1, source_target_pairs={{0,8},{8,0},{16,24},{24,16},{32,40},{40,32},{48,56},{56,48},{64,72... | collective-permute-start | bytes 3145736 | tf_op jit(solution)/shard_map/ppermute | solution.py:327
  67.4 2.3 %shard_map.95 = (bf16[4096,256]{1,0:T(8,128)(2,1)S(1)}, bf16[4096,256]{1,0:T(8,128)(2,1)S(1)}, bf16[128,4096]{1,0:T(8,128)(2,1)S(1)}) custom-call(s32[64]{0:T(128)S(1)} %pad_add_fusion.slots_ref, bf16[4,4,128,256]{3,2,1,0:T(8,128)(2,1)S(1)} %all_to_all.32.own_ref, bf16[4096,128]{1,0:T(8,128)(2,1)S(1)} %bitcast.9), custom_call_target="tpu_custom_call" | custom-call | flops 2097152 | bytes 6291456 | tf_op jit(solution)/shard_map/pallas_call | solution.py:266
  69.7 9.3 %collective-permute-done.1.pair_ref = bf16[4,4,128,256]{3,2,1,0:T(8,128)(2,1)S(1)} collective-permute-done((bf16[4,4,128,256]{3,2,1,0:T(8,128)(2,1)S(1)}, bf16[4,4,128,256]{3,2,1,0:T(8,128)(2,1)S(1)}, u32[]{:S(2)}, u32[]{:S(2)}) %collective-permute-start.1) | collective-permute-done | bytes 1048608 | tf_op jit(solution)/shard_map/ppermute | solution.py:326
  79.0 2.0 %collective-permute-start.2 = (bf16[4,4,128,256]{3,2,1,0:T(8,128)(2,1)S(1)}, bf16[4,4,128,256]{3,2,1,0:T(8,128)(2,1)S(1)}, u32[]{:S(2)}, u32[]{:S(2)}) collective-permute-start(bf16[4,4,128,256]{3,2,1,0:T(8,128)(2,1)S(1)} %collective-permute-done.1.pair_ref), channel_id=1, source_target_pairs={{0,8},{8,0},{16,24},{24,16},{32,40},{40,32},{48,56},{56,48},{64,72... | collective-permute-start | bytes 3145736 | tf_op jit(solution)/shard_map/ppermute | solution.py:335
  81.0 2.0 %shard_map.96 = (bf16[4096,256]{1,0:T(8,128)(2,1)S(1)}, bf16[4096,256]{1,0:T(8,128)(2,1)S(1)}) custom-call(s32[64]{0:T(128)S(1)} %pad_add_fusion.slots_ref, bf16[4,4,128,256]{3,2,1,0:T(8,128)(2,1)} %collective-permute-done.oth_ref, bf16[4,4,128,256]{3,2,1,0:T(8,128)(2,1)S(1)} %collective-permute-done.1.pair_ref, ...), custom_call_target="tpu_custom_call", output_to_operand_aliasing={{0}: (3, {}), {1}: (4, {})} | custom-call | flops 2097152 | bytes 3145728 | tf_op jit(solution)/shard_map/pallas_call | solution.py:266
  83.7 3.8 %shard_map.97 = (bf16[4096,256]{1,0:T(8,128)(2,1)S(1)}, bf16[4096,256]{1,0:T(8,128)(2,1)S(1)}, bf16[128,256]{1,0:T(8,128)(2,1)S(1)}, bf16[128,256]{1,0:T(8,128)(...) custom-call(s32[64]{0:T(128)S(1)} %pad_add_fusion.slots_ref, ...), custom_call_target="tpu_custom_call", output_to_operand_aliasing={{0}: (2, {}), {1}: (3, {})} | custom-call | tf_op jit(solution)/shard_map/pallas_call | solution.py:266
  87.5 2.0 %collective-permute-start.3 = (bf16[2064,256]{1,0:T(8,128)(2,1)S(1)}, bf16[2064,256]{1,0:T(8,128)(2,1)S(1)}, u32[]{:S(2)}, u32[]{:S(2)}) collective-permute-start(bf16[2064,256]{1,0:T(8,128)(2,1)S(1)} %get-tuple-element.39), channel_id=1, source_target_pairs={{0,8},{8,0},{16,24},{24,16},{32,40},{40,32},{48,56},{56,48},{64,72... | collective-permute-start | bytes 3170312 | tf_op jit(solution)/shard_map/ppermute | solution.py:354
  89.5 2.6 %shard_map.98 = (bf16[4096,128]{1,0:T(8,128)(2,1)}, bf16[128,4096]{1,0:T(8,128)(2,1)}) custom-call(bf16[4096,256]{1,0:T(8,128)(2,1)S(1)} %get-tuple-element.40.x_ref, bf16[4096,256]{1,0:T(8,128)(2,1)S(1)} %get-tuple-element.41.u_ref, bf16[128,256]{1,0:T(8,128)(2,1)S(1)} %get-tuple-element.42.back_ref, bf16[128,256]{1,0:T(8,128)(2,1)S(1)} %get-tuple-element.43.scaled_ref), custom_call_target="tpu_custom_call" | custom-call | flops 536870912 | bytes 6291456 | tf_op jit(solution)/shard_map/pallas_call | solution.py:266
  92.1 0.8 shard_map.100.far_ref
  93.0 2.6 %collective-permute-start.4 = (bf16[1040,256]{1,0:T(8,128)(2,1)S(1)}, bf16[1040,256]{1,0:T(8,128)(2,1)S(1)}, u32[]{:S(2)}, u32[]{:S(2)}) collective-permute-start(bf16[1040,256]{1,0:T(8,128)(2,1)S(1)} %shard_map.100.far_ref), channel_id=1, source_target_pairs={{0,64},{8,456},{16,80},{24,472},{32,96},{40,488},{48,112},{56,504}... | collective-permute-start | bytes 1597448 | tf_op jit(solution)/shard_map/ppermute | solution.py:367
  95.6 0.8 shard_map.99.near_ref
  96.4 7.7 %collective-permute-done.4.got_ref = bf16[1040,256]{1,0:T(8,128)(2,1)S(1)} collective-permute-done((bf16[1040,256]{1,0:T(8,128)(2,1)S(1)}, bf16[1040,256]{1,0:T(8,128)(2,1)S(1)}, u32[]{:S(2)}, u32[]{:S(2)}) %collective-permute-start.4) | collective-permute-done | bytes 532512 | tf_op jit(solution)/shard_map/ppermute | solution.py:367
  104.3 15.8 %all_to_all.33.got_ref = bf16[4,272,256]{2,1,0:T(8,128)(2,1)S(1)} all-to-all(bf16[4,272,256]{2,1,0:T(8,128)(2,1)S(1)} %shard_map.101), channel_id=1, replica_groups={{0,16,32,48},{64,80,96,112},{128,144,160,176},{192,208,224,240},{256,27..., dimensions={0} | all-to-all | bytes 1114112 | tf_op jit(solution)/shard_map/all_to_all | solution.py:283
  120.1 0.7 shard_map.102
  120.8 3.3 %all-to-all-start.4 = ((bf16[4,80,256]{2,1,0:T(8,128)(2,1)}), bf16[4,80,256]{2,1,0:T(8,128)(2,1)S(1)}, u32[]{:S(2)}, u32[]{:S(2)}) async-start(bf16[4,80,256]{2,1,0:T(8,128)(2,1)} %shard_map.102), calls=%async_computation.4 | async-start | bytes 327680 | tf_op jit(solution)/shard_map/all_to_all | solution.py:283
  124.2 8.5 %all-to-all-done.4.got_ref = bf16[4,80,256]{2,1,0:T(8,128)(2,1)S(1)} async-done(((bf16[4,80,256]{2,1,0:T(8,128)(2,1)}), bf16[4,80,256]{2,1,0:T(8,128)(2,1)S(1)}, u32[]{:S(2)}, u32[]{:S(2)}) %all-to-all-start.4) | async-done | bytes 163872 | tf_op jit(solution)/shard_map/all_to_all | solution.py:283
  132.7 0.6 shard_map.103
  133.3 9.8 %all_to_all.34.terms_ref = bf16[8,64,256]{2,1,0:T(8,128)(2,1)S(1)} all-to-all(bf16[8,64,256]{2,1,0:T(8,128)(2,1)S(1)} %get-tuple-element.52), channel_id=1, replica_groups=mesh['dp'=64,'expert'=8] {'expert'}, dimensions={0} | all-to-all | bytes 524288 | tf_op jit(solution)/shard_map/all_to_all | solution.py:283
  143.2 1.4 shard_map.104
  (20 shorter events, 1.4 us)
Async XLA Ops:
  18.1 49.3 %copy-start = (bf16[1,4096,128]{2,1,0:T(8,128)(2,1)S(1)}, bf16[1,4096,128]{2,1,0:T(8,128)(2,1)}, u32[]{:S(2)}) copy-start(bf16[1,4096,128]{2,1,0:T(8,128)(2,1)} %param.8) | copy-start | bytes 3145732
  62.3 16.7 %collective-permute-start.1 = (bf16[4,4,128,256]{3,2,1,0:T(8,128)(2,1)S(1)}, bf16[4,4,128,256]{3,2,1,0:T(8,128)(2,1)S(1)}, u32[]{:S(2)}, u32[]{:S(2)}) collective-permute-start(bf16[4,4,128,256]{3,2,1,0:T(8,128)(2,1)S(1)} %all_to_all.32.own_ref), channel_id=1, source_target_pairs={{0,64},{8,456},{16,80},{24,472},{32,96},{40,488},{48,112},{56,504}... | collective-permute-start | bytes 3145736 | tf_op jit(solution)/shard_map/ppermute | solution.py:326
  64.9 14.1 %collective-permute-start = (bf16[4,4,128,256]{3,2,1,0:T(8,128)(2,1)S(1)}, bf16[4,4,128,256]{3,2,1,0:T(8,128)(2,1)}, u32[]{:S(2)}, u32[]{:S(2)}) collective-permute-start(bf16[4,4,128,256]{3,2,1,0:T(8,128)(2,1)S(1)} %all_to_all.32.own_ref), channel_id=1, source_target_pairs={{0,8},{8,0},{16,24},{24,16},{32,40},{40,32},{48,56},{56,48},{64,72... | collective-permute-start | bytes 3145736 | tf_op jit(solution)/shard_map/ppermute | solution.py:327
  79.0 4.7 %copy-start.2 = (f32[1,256]{1,0:T(1,128)S(1)}, f32[1,256]{1,0:T(1,128)}, u32[]{:S(2)}) copy-start(f32[1,256]{1,0:T(1,128)} %score_ref.1) | copy-start | bytes 3076
  79.0 4.7 %collective-permute-start.2 = (bf16[4,4,128,256]{3,2,1,0:T(8,128)(2,1)S(1)}, bf16[4,4,128,256]{3,2,1,0:T(8,128)(2,1)S(1)}, u32[]{:S(2)}, u32[]{:S(2)}) collective-permute-start(bf16[4,4,128,256]{3,2,1,0:T(8,128)(2,1)S(1)} %collective-permute-done.1.pair_ref), channel_id=1, source_target_pairs={{0,8},{8,0},{16,24},{24,16},{32,40},{40,32},{48,56},{56,48},{64,72... | collective-permute-start | bytes 3145736 | tf_op jit(solution)/shard_map/ppermute | solution.py:335
  87.5 4.7 %collective-permute-start.3 = (bf16[2064,256]{1,0:T(8,128)(2,1)S(1)}, bf16[2064,256]{1,0:T(8,128)(2,1)S(1)}, u32[]{:S(2)}, u32[]{:S(2)}) collective-permute-start(bf16[2064,256]{1,0:T(8,128)(2,1)S(1)} %get-tuple-element.39), channel_id=1, source_target_pairs={{0,8},{8,0},{16,24},{24,16},{32,40},{40,32},{48,56},{56,48},{64,72... | collective-permute-start | bytes 3170312 | tf_op jit(solution)/shard_map/ppermute | solution.py:354
  93.0 11.2 %collective-permute-start.4 = (bf16[1040,256]{1,0:T(8,128)(2,1)S(1)}, bf16[1040,256]{1,0:T(8,128)(2,1)S(1)}, u32[]{:S(2)}, u32[]{:S(2)}) collective-permute-start(bf16[1040,256]{1,0:T(8,128)(2,1)S(1)} %shard_map.100.far_ref), channel_id=1, source_target_pairs={{0,64},{8,456},{16,80},{24,472},{32,96},{40,488},{48,112},{56,504}... | collective-permute-start | bytes 1597448 | tf_op jit(solution)/shard_map/ppermute | solution.py:367
  104.2 38.9 %copy-start.1 = (s32[8,256]{1,0:T(8,128)S(1)}, s32[8,256]{1,0:T(8,128)}, u32[]{:S(2)}) copy-start(s32[8,256]{1,0:T(8,128)} %chosen_ref.1) | copy-start | bytes 24580
  120.8 11.9 %all-to-all-start.4 = ((bf16[4,80,256]{2,1,0:T(8,128)(2,1)}), bf16[4,80,256]{2,1,0:T(8,128)(2,1)S(1)}, u32[]{:S(2)}, u32[]{:S(2)}) async-start(bf16[4,80,256]{2,1,0:T(8,128)(2,1)} %shard_map.102), calls=%async_computation.4 | async-start | bytes 327680 | tf_op jit(solution)/shard_map/all_to_all | solution.py:283

commit v9 on v7

--- a/solution.py
+++ b/solution.py
@@ -121,9 +121,18 @@
     )
 
 
-def ready_kernel(slots_ref, own_ref, w_in_ref, x_ref, u_ref, turned_ref, x_sem, u_sem):
-    arrived = load_blocks(slots_ref, 0, own_ref, x_ref, u_ref, x_sem, u_sem)
+def ready_kernel(
+    slots_ref, own_ref, w_in_ref, w_out_ref,
+    x_ref, u_ref, turned_ref, order_ref, held_ref, x_sem, u_sem, w_sem,
+):
+    weights = pltpu.make_async_copy(w_out_ref, held_ref, w_sem)
+    weights.start()
+    arrived = load_blocks(slots_ref, 0, own_ref, x_ref, u_ref, x_sem, u_sem) + (weights,)
     turned_ref[...] = w_in_ref[...].T
+    count, feats = slots_ref.shape[0] // 2, own_ref.shape[2] // 2
+    for s in range(count):
+        at = block_rows(slots_ref, count + s, feats)
+        order_ref[pl.ds(s * feats, feats), :] = w_in_ref[at, :]
     for copy in arrived:
         copy.wait()
 
@@ -138,19 +147,15 @@
 
 
 def main_kernel(
-    slots_ref, oth_ref, x_in, u_in, turned_ref, w_in_ref, w_out_ref, score_ref,
-    x_ref, u_ref, back_ref, scaled_ref, gate_ref, send_ref, held_ref, x_sem, u_sem, w_sem,
+    slots_ref, oth_ref, x_in, u_in, turned_ref, order_ref, w_out_ref, score_ref,
+    x_ref, u_ref, back_ref, scaled_ref, gate_ref, send_ref, x_sem, u_sem,
 ):
-    weights = pltpu.make_async_copy(w_out_ref, held_ref, w_sem)
-    weights.start()
     count = oth_ref.shape[0] * oth_ref.shape[1]
-    feats = oth_ref.shape[2] // 2
     x_done, u_done = load_blocks(slots_ref, 3 * count, oth_ref, x_ref, u_ref, x_sem, u_sem)
     x_done.wait()
     preact = contract(turned_ref[...], x_ref[...], 1, 0)
     u_done.wait()
-    weights.wait()
-    raw = contract(held_ref[...], u_ref[...], 1, 0)
+    raw = contract(w_out_ref[...], u_ref[...], 1, 0)
     val, slope = gelu_parts(preact)
     hidden = val.astype(BF).astype(F32)
     score = score_ref[...]
@@ -159,11 +164,10 @@
     back_ref[...] = back
     scaled_ref[...] = (score * hidden).astype(BF)
     gate_ref[...] = gate
-    slots = 2 * count
-    for s in range(slots):
-        at = block_rows(slots_ref, 3 * slots + s, feats)
-        send_ref[pl.ds(s * feats, feats), :] = contract(w_in_ref[at, :], back, 1, 0).astype(BF)
-    send_ref[pl.ds(slots * feats, 16), :] = gate_tile([hi_lo(gate)])
+    half = order_ref.shape[0] // 2
+    send = contract(order_ref[pl.ds(half, half), :], back, 1, 0)
+    send_ref[pl.ds(0, half), :] = send.astype(BF)
+    send_ref[pl.ds(half, 16), :] = gate_tile([hi_lo(gate)])
 
 
 def weight_kernel(x_ref, u_ref, back_ref, scaled_ref, gin_ref, gout_ref):
@@ -171,20 +175,17 @@
     gout_ref[...] = contract(scaled_ref[...], u_ref[...], 1, 1).astype(BF)
 
 
-def pair_kernel(slots_ref, w_in_ref, back_ref, gate_ref, got_ref, out_ref):
+def pair_kernel(order_ref, back_ref, gate_ref, got_ref, out_ref):
     parts, rows = out_ref.shape[0], out_ref.shape[1] - 16
-    feats = rows // 8
     back = back_ref[...]
     tile = got_ref[pl.ds(parts * rows, 16), :].astype(F32)
     high, low = hi_lo(gate_ref[...])
     gate = (high.astype(F32) + low.astype(F32)) + (tile[0:1] + tile[1:2])
     packed = gate_tile([hi_lo(gate)])
     for k in range(parts):
-        for i in range(8):
-            s = k * 8 + i
-            mine = contract(w_in_ref[block_rows(slots_ref, 2 * 8 * parts + s, feats), :], back, 1, 0)
-            other = got_ref[pl.ds(s * feats, feats), :].astype(F32)
-            out_ref[k, pl.ds(i * feats, feats), :] = (mine + other).astype(BF)
+        at = pl.ds(k * rows, rows)
+        mine = contract(order_ref[at, :], back, 1, 0)
+        out_ref[k, :rows, :] = (mine + got_ref[at, :].astype(F32)).astype(BF)
         out_ref[k, rows:, :] = packed
 
 
@@ -313,9 +314,11 @@
     near = lax.ppermute(own, "dp", SWAP)
     sems = [pltpu.SemaphoreType.DMA] * 2
     held = [((depth, rows), BF), ((depth, rows), BF)]
-    x, u, turned = call(
-        ready_kernel, [SMEM, ANY, VMEM], held + [((units, depth), BF)], slots, own, w_in[0],
-        scratch=sems, flops=2 * MIB, moved=6 * MIB,
+    weight = ((depth, units), BF)
+    x, u, turned, order, held_out = call(
+        ready_kernel, [SMEM, ANY, VMEM, HBM], held + [((units, depth), BF), weight, ((units, depth), BF)],
+        slots, own, w_in[0], in_hbm(w_out[0]),
+        scratch=sems + sems[:1], flops=2 * MIB, moved=6 * MIB,
     )
     near, pair, x, u, turned = lax.optimization_barrier((near, pair, x, u, turned))
     other = lax.ppermute(pair, "dp", SWAP)
@@ -326,7 +329,7 @@
     )
     x, u, back, scaled, gate, send = call(
         main_kernel,
-        [SMEM, ANY] + [VMEM] * 4 + [HBM, VMEM],
+        [SMEM, ANY] + [VMEM] * 6,
         held
         + [
             ((units, rows), BF),
@@ -334,8 +337,8 @@
             ((1, rows), F32),
             ((count * feats + 16, rows), BF),
         ],
-        slots, other, x, u, turned, w_in[0], in_hbm(w_out[0]), gate_scores,
-        scratch=[pltpu.VMEM((units, depth), BF)] + [pltpu.SemaphoreType.DMA] * 3, alias={2: 0, 3: 1},
+        slots, other, x, u, turned, order, held_out, gate_scores,
+        scratch=sems, alias={2: 0, 3: 1},
     )
     got = lax.ppermute(send, "dp", SWAP)
     weight_grads = call(
@@ -347,9 +350,9 @@
     got, weight_in_grad, weight_out_grad = lax.optimization_barrier((got, *weight_grads))
     part = call(
         pair_kernel,
-        [SMEM] + [VMEM] * 4,
+        [VMEM] * 4,
         [((4, 8 * feats + 16, rows), BF)],
-        slots, w_in[0], back, gate, got,
+        order, back, gate, got,
     )
     part = exchange(part, "dp", OUTER)
     part = call(outer_kernel, [VMEM], [((8, feats + 16, rows), BF)], part)

time: 140 us -> 140 us (level)
  waiting for transfers between devices: 9.58 us -> 7.76 us
  transfers between devices with their start and end apart: 4 -> 4, of which waited for: 2 -> 1; matrix products, arithmetic and copies ran while one was open for 1% -> 1% of each run, Pallas kernels for 5% -> 6%
where the time goes in v9:
time: 140 us
  blocking collectives  104 us (74%)
  Pallas kernels  16.1 us (12%)
  starting transfers between devices  9 us (6%)
  waiting for transfers between devices  7.76 us (6%)
  local copies, waits for them, and re-layouts  1.92 us (1%)
    all_to_all x6, blocking collectives, exchange(): return lax.all_to_all(parts, axis, 0, 0, axis_index_groups=groups)  104 us
    pallas_call x10, Pallas kernels, call(): pl.pallas_call(kernel, out_shape=shapes[0] if single else shapes, in_spec...  16.1 us
    ppermute x1, waiting for transfers between devices, per_device(): pair = lax.ppermute(own, 'dp', NEIGHBOUR)  7.76 us
  transfers between devices with their start and end apart: 4, of which 1 were waited for; matrix products, arithmetic and copies ran while one was open for 1% of the time, Pallas kernels for 6%

profile of v9, /device:TPU:8, one launch (start us, length us, event | category | flops | bytes accessed | tf_op | source)
XLA Modules:
  0.0 139.8 jit_solution(11558370757018621390)
XLA Ops:
  0.6 1.4 shard_map.93
  2.0 16.0 %all_to_all.30.parts_ref = bf16[8,128,256]{2,1,0:T(8,128)(2,1)S(1)} all-to-all(bf16[8,128,256]{2,1,0:T(8,128)(2,1)S(1)} %shard_map.93), channel_id=1, replica_groups=mesh['dp'=64,'expert'=8] {'expert'}, dimensions={0} | all-to-all | bytes 1048576 | tf_op jit(solution)/shard_map/all_to_all | solution.py:260
  18.1 16.4 %all_to_all.31 = bf16[4,128,256]{2,1,0:T(8,128)(2,1)S(1)} all-to-all(bf16[4,128,256]{2,1,0:T(8,128)(2,1)S(1)} %shard_map.94), channel_id=1, replica_groups={{0,128,256,384},{16,144,272,400},{32,160,288,416},{48,176,304,432},{64,..., dimensions={0} | all-to-all | bytes 524288 | tf_op jit(solution)/shard_map/all_to_all | solution.py:260
  34.5 0.1 broadcast_in_dim.6
  34.6 27.5 %all_to_all.32.own_ref = bf16[4,4,128,256]{3,2,1,0:T(8,128)(2,1)S(1)} all-to-all(bf16[4,4,128,256]{3,2,1,0:T(8,128)(2,1)S(1)} %broadcast_in_dim.6), channel_id=1, replica_groups={{0,16,32,48},{64,80,96,112},{128,144,160,176},{192,208,224,240},{256,27..., dimensions={0} | all-to-all | bytes 2097152 | tf_op jit(solution)/shard_map/all_to_all | solution.py:260
  62.2 2.6 %collective-permute-start.1 = (bf16[4,4,128,256]{3,2,1,0:T(8,128)(2,1)S(1)}, bf16[4,4,128,256]{3,2,1,0:T(8,128)(2,1)S(1)}, u32[]{:S(2)}, u32[]{:S(2)}) collective-permute-start(bf16[4,4,128,256]{3,2,1,0:T(8,128)(2,1)S(1)} %all_to_all.32.own_ref), channel_id=1, source_target_pairs={{0,64},{8,456},{16,80},{24,472},{32,96},{40,488},{48,112},{56,504}... | collective-permute-start | bytes 3145736 | tf_op jit(solution)/shard_map/ppermute | solution.py:313
  64.8 1.9 %collective-permute-start = (bf16[4,4,128,256]{3,2,1,0:T(8,128)(2,1)S(1)}, bf16[4,4,128,256]{3,2,1,0:T(8,128)(2,1)S(1)}, u32[]{:S(2)}, u32[]{:S(2)}) collective-permute-start(bf16[4,4,128,256]{3,2,1,0:T(8,128)(2,1)S(1)} %all_to_all.32.own_ref), channel_id=1, source_target_pairs={{0,8},{8,0},{16,24},{24,16},{32,40},{40,32},{48,56},{56,48},{64,72... | collective-permute-start | bytes 3145736 | tf_op jit(solution)/shard_map/ppermute | solution.py:314
  66.8 0.1 reshape.173
  67.1 0.1 select_n.92
  67.5 1.2 copy-done
  68.8 2.3 %shard_map.95 = (bf16[4096,256]{1,0:T(8,128)(2,1)S(1)}, bf16[4096,256]{1,0:T(8,128)(2,1)S(1)}, bf16[128,4096]{1,0:T(8,128)(2,1)S(1)}, bf16[4096,128]{1,0:T(8,128)(2,1)S(1)}, bf16[128,4096]{1,0:T(8,128)(2,1)S(1)}) custom-call(s32[128]{0:T(128)S(1)} %concatenate.3.slots_ref, bf16[4,4,128,256]{3,2,1,0:T(8,128)(2,1)S(1)} %all_to_all.32.own_ref, ...), custom_call_target="tpu_custom_call" | custom-call | flops 2097152 | bytes 6291456 | tf_op jit(solution)/shard_map/pallas_call | solution.py:243
  71.1 7.8 %collective-permute-done.1.pair_ref = bf16[4,4,128,256]{3,2,1,0:T(8,128)(2,1)S(1)} collective-permute-done((bf16[4,4,128,256]{3,2,1,0:T(8,128)(2,1)S(1)}, bf16[4,4,128,256]{3,2,1,0:T(8,128)(2,1)S(1)}, u32[]{:S(2)}, u32[]{:S(2)}) %collective-permute-start.1) | collective-permute-done | bytes 1048608 | tf_op jit(solution)/shard_map/ppermute | solution.py:313
  78.8 2.0 %collective-permute-start.2 = (bf16[4,4,128,256]{3,2,1,0:T(8,128)(2,1)S(1)}, bf16[4,4,128,256]{3,2,1,0:T(8,128)(2,1)S(1)}, u32[]{:S(2)}, u32[]{:S(2)}) collective-permute-start(bf16[4,4,128,256]{3,2,1,0:T(8,128)(2,1)S(1)} %collective-permute-done.1.pair_ref), channel_id=1, source_target_pairs={{0,8},{8,0},{16,24},{24,16},{32,40},{40,32},{48,56},{56,48},{64,72... | collective-permute-start | bytes 3145736 | tf_op jit(solution)/shard_map/ppermute | solution.py:324
  80.9 3.4 %shard_map.96 = (bf16[4096,256]{1,0:T(8,128)(2,1)S(1)}, bf16[4096,256]{1,0:T(8,128)(2,1)S(1)}) custom-call(s32[128]{0:T(128)S(1)} %concatenate.3.slots_ref, bf16[4,4,128,256]{3,2,1,0:T(8,128)(2,1)S(1)} %collective-permute-done.oth_ref, bf16[4,4,128,256]{3,2,1,0:T(8,128)(2,1)S(1)} %collective-permute-done.1.pair_ref, ...), custom_call_target="tpu_custom_call", output_to_operand_aliasing={{0}: (3, {}), {1}: (4, {})} | custom-call | flops 2097152 | bytes 3145728 | tf_op jit(solution)/shard_map/pallas_call | solution.py:243
  84.3 3.8 %shard_map.97 = (bf16[4096,256]{1,0:T(8,128)(2,1)S(1)}, bf16[4096,256]{1,0:T(8,128)(2,1)S(1)}, bf16[128,256]{1,0:T(8,128)(2,1)S(1)}, bf16[128,256]{1,0:T(8,128)(...) custom-call(s32[128]{0:T(128)S(1)} %concatenate.3.slots_ref, ...), custom_call_target="tpu_custom_call", output_to_operand_aliasing={{0}: (2, {}), {1}: (3, {})} | custom-call | tf_op jit(solution)/shard_map/pallas_call | solution.py:243
  88.1 2.4 %collective-permute-start.3 = (bf16[2064,256]{1,0:T(8,128)(2,1)S(1)}, bf16[2064,256]{1,0:T(8,128)(2,1)S(1)}, u32[]{:S(2)}, u32[]{:S(2)}) collective-permute-start(bf16[2064,256]{1,0:T(8,128)(2,1)S(1)} %get-tuple-element.41), channel_id=1, source_target_pairs={{0,8},{8,0},{16,24},{24,16},{32,40},{40,32},{48,56},{56,48},{64,72... | collective-permute-start | bytes 3170312 | tf_op jit(solution)/shard_map/ppermute | solution.py:343
  90.5 2.6 %shard_map.98 = (bf16[4096,128]{1,0:T(8,128)(2,1)}, bf16[128,4096]{1,0:T(8,128)(2,1)}) custom-call(bf16[4096,256]{1,0:T(8,128)(2,1)S(1)} %get-tuple-element.42.x_ref, bf16[4096,256]{1,0:T(8,128)(2,1)S(1)} %get-tuple-element.43.u_ref, bf16[128,256]{1,0:T(8,128)(2,1)S(1)} %get-tuple-element.44.back_ref, bf16[128,256]{1,0:T(8,128)(2,1)S(1)} %get-tuple-element.45.scaled_ref), custom_call_target="tpu_custom_call" | custom-call | flops 536870912 | bytes 6291456 | tf_op jit(solution)/shard_map/pallas_call | solution.py:243
  93.1 0.4 shard_map.99
  93.6 21.5 %all_to_all.33.got_ref = bf16[4,528,256]{2,1,0:T(8,128)(2,1)S(1)} all-to-all(bf16[4,528,256]{2,1,0:T(8,128)(2,1)S(1)} %shard_map.99), channel_id=1, replica_groups={{0,16,32,48},{64,80,96,112},{128,144,160,176},{192,208,224,240},{256,27..., dimensions={0} | all-to-all | bytes 2162688 | tf_op jit(solution)/shard_map/all_to_all | solution.py:260
  115.0 0.1 shard_map.100
  115.2 12.8 %all_to_all.34.got_ref = bf16[8,80,256]{2,1,0:T(8,128)(2,1)S(1)} all-to-all(bf16[8,80,256]{2,1,0:T(8,128)(2,1)S(1)} %shard_map.100), channel_id=1, replica_groups={{0,64,128,192,256,320,384,448},{16,80,144,208,272,336,400,464},{32,96,1..., dimensions={0} | all-to-all | bytes 655360 | tf_op jit(solution)/shard_map/all_to_all | solution.py:260
  128.0 0.6 shard_map.101
  128.6 9.8 %all_to_all.35.terms_ref = bf16[8,64,256]{2,1,0:T(8,128)(2,1)S(1)} all-to-all(bf16[8,64,256]{2,1,0:T(8,128)(2,1)S(1)} %get-tuple-element.52), channel_id=1, replica_groups=mesh['dp'=64,'expert'=8] {'expert'}, dimensions={0} | all-to-all | bytes 524288 | tf_op jit(solution)/shard_map/all_to_all | solution.py:260
  138.5 1.4 shard_map.102
  (21 shorter events, 0.7 us)
Async XLA Ops:
  62.2 16.7 %collective-permute-start.1 = (bf16[4,4,128,256]{3,2,1,0:T(8,128)(2,1)S(1)}, bf16[4,4,128,256]{3,2,1,0:T(8,128)(2,1)S(1)}, u32[]{:S(2)}, u32[]{:S(2)}) collective-permute-start(bf16[4,4,128,256]{3,2,1,0:T(8,128)(2,1)S(1)} %all_to_all.32.own_ref), channel_id=1, source_target_pairs={{0,64},{8,456},{16,80},{24,472},{32,96},{40,488},{48,112},{56,504}... | collective-permute-start | bytes 3145736 | tf_op jit(solution)/shard_map/ppermute | solution.py:313
  64.8 14.1 %collective-permute-start = (bf16[4,4,128,256]{3,2,1,0:T(8,128)(2,1)S(1)}, bf16[4,4,128,256]{3,2,1,0:T(8,128)(2,1)S(1)}, u32[]{:S(2)}, u32[]{:S(2)}) collective-permute-start(bf16[4,4,128,256]{3,2,1,0:T(8,128)(2,1)S(1)} %all_to_all.32.own_ref), channel_id=1, source_target_pairs={{0,8},{8,0},{16,24},{24,16},{32,40},{40,32},{48,56},{56,48},{64,72... | collective-permute-start | bytes 3145736 | tf_op jit(solution)/shard_map/ppermute | solution.py:314
  67.5 1.2 copy-start
  78.8 5.5 %copy-start.2 = (f32[1,256]{1,0:T(1,128)S(1)}, f32[1,256]{1,0:T(1,128)}, u32[]{:S(2)}) copy-start(f32[1,256]{1,0:T(1,128)} %score_ref.1) | copy-start | bytes 3076
  78.8 5.5 %collective-permute-start.2 = (bf16[4,4,128,256]{3,2,1,0:T(8,128)(2,1)S(1)}, bf16[4,4,128,256]{3,2,1,0:T(8,128)(2,1)S(1)}, u32[]{:S(2)}, u32[]{:S(2)}) collective-permute-start(bf16[4,4,128,256]{3,2,1,0:T(8,128)(2,1)S(1)} %collective-permute-done.1.pair_ref), channel_id=1, source_target_pairs={{0,8},{8,0},{16,24},{24,16},{32,40},{40,32},{48,56},{56,48},{64,72... | collective-permute-start | bytes 3145736 | tf_op jit(solution)/shard_map/ppermute | solution.py:324
  88.1 5.0 %collective-permute-start.3 = (bf16[2064,256]{1,0:T(8,128)(2,1)S(1)}, bf16[2064,256]{1,0:T(8,128)(2,1)S(1)}, u32[]{:S(2)}, u32[]{:S(2)}) collective-permute-start(bf16[2064,256]{1,0:T(8,128)(2,1)S(1)} %get-tuple-element.41), channel_id=1, source_target_pairs={{0,8},{8,0},{16,24},{24,16},{32,40},{40,32},{48,56},{56,48},{64,72... | collective-permute-start | bytes 3170312 | tf_op jit(solution)/shard_map/ppermute | solution.py:343
  93.6 44.9 %copy-start.1 = (s32[8,256]{1,0:T(8,128)S(1)}, s32[8,256]{1,0:T(8,128)}, u32[]{:S(2)}) copy-start(s32[8,256]{1,0:T(8,128)} %chosen_ref.1) | copy-start | bytes 24580

commit v10 on v9

--- a/solution.py
+++ b/solution.py
@@ -122,12 +122,9 @@
 
 
 def ready_kernel(
-    slots_ref, own_ref, w_in_ref, w_out_ref,
-    x_ref, u_ref, turned_ref, order_ref, held_ref, x_sem, u_sem, w_sem,
+    slots_ref, own_ref, w_in_ref, x_ref, u_ref, turned_ref, order_ref, x_sem, u_sem
 ):
-    weights = pltpu.make_async_copy(w_out_ref, held_ref, w_sem)
-    weights.start()
-    arrived = load_blocks(slots_ref, 0, own_ref, x_ref, u_ref, x_sem, u_sem) + (weights,)
+    arrived = load_blocks(slots_ref, 0, own_ref, x_ref, u_ref, x_sem, u_sem)
     turned_ref[...] = w_in_ref[...].T
     count, feats = slots_ref.shape[0] // 2, own_ref.shape[2] // 2
     for s in range(count):
@@ -148,14 +145,17 @@
 
 def main_kernel(
     slots_ref, oth_ref, x_in, u_in, turned_ref, order_ref, w_out_ref, score_ref,
-    x_ref, u_ref, back_ref, scaled_ref, gate_ref, send_ref, x_sem, u_sem,
+    x_ref, u_ref, back_ref, scaled_ref, gate_ref, send_ref, held_ref, x_sem, u_sem, w_sem,
 ):
+    weights = pltpu.make_async_copy(w_out_ref, held_ref, w_sem)
+    weights.start()
     count = oth_ref.shape[0] * oth_ref.shape[1]
     x_done, u_done = load_blocks(slots_ref, 3 * count, oth_ref, x_ref, u_ref, x_sem, u_sem)
     x_done.wait()
     preact = contract(turned_ref[...], x_ref[...], 1, 0)
     u_done.wait()
-    raw = contract(w_out_ref[...], u_ref[...], 1, 0)
+    weights.wait()
+    raw = contract(held_ref[...], u_ref[...], 1, 0)
     val, slope = gelu_parts(preact)
     hidden = val.astype(BF).astype(F32)
     score = score_ref[...]
@@ -315,21 +315,21 @@
     sems = [pltpu.SemaphoreType.DMA] * 2
     held = [((depth, rows), BF), ((depth, rows), BF)]
     weight = ((depth, units), BF)
-    x, u, turned, order, held_out = call(
-        ready_kernel, [SMEM, ANY, VMEM, HBM], held + [((units, depth), BF), weight, ((units, depth), BF)],
-        slots, own, w_in[0], in_hbm(w_out[0]),
-        scratch=sems + sems[:1], flops=2 * MIB, moved=6 * MIB,
+    x, u, turned, order = call(
+        ready_kernel, [SMEM, ANY, VMEM], held + [((units, depth), BF), weight],
+        slots, own, w_in[0],
+        scratch=sems, flops=2 * MIB, moved=6 * MIB,
     )
     near, pair, x, u, turned = lax.optimization_barrier((near, pair, x, u, turned))
     other = lax.ppermute(pair, "dp", SWAP)
     x, u = call(
-        more_kernel, [SMEM, ANY, ANY, VMEM, VMEM], held, slots, near, pair, x, u,
+        more_kernel, [SMEM, ANY, ANY, VMEM, VMEM], held, slots, in_hbm(near), pair, x, u,
         scratch=[pltpu.SemaphoreType.DMA((2,))] * 2, alias={3: 0, 4: 1},
         flops=2 * MIB, moved=3 * MIB,
     )
     x, u, back, scaled, gate, send = call(
         main_kernel,
-        [SMEM, ANY] + [VMEM] * 6,
+        [SMEM, ANY] + [VMEM] * 4 + [HBM, VMEM],
         held
         + [
             ((units, rows), BF),
@@ -337,8 +337,8 @@
             ((1, rows), F32),
             ((count * feats + 16, rows), BF),
         ],
-        slots, other, x, u, turned, order, held_out, gate_scores,
-        scratch=sems, alias={2: 0, 3: 1},
+        slots, other, x, u, turned, order, in_hbm(w_out[0]), gate_scores,
+        scratch=[pltpu.VMEM((units, depth), BF)] + [pltpu.SemaphoreType.DMA] * 3, alias={2: 0, 3: 1},
     )
     got = lax.ppermute(send, "dp", SWAP)
     weight_grads = call(

time: 140 us -> 139 us (level)
  waiting for transfers between devices: 7.76 us -> 9.56 us
  Pallas kernels: 16.1 us -> 14.7 us
  transfers between devices with their start and end apart: 4 -> 4, of which waited for: 1 -> 2; matrix products, arithmetic and copies ran while one was open for 1% -> 1% of each run, Pallas kernels for 6% -> 5%
where the time goes in v10:
time: 139 us
  blocking collectives  104 us (75%)
  Pallas kernels  14.7 us (11%)
  waiting for transfers between devices  9.56 us (7%)
  starting transfers between devices  8.63 us (6%)
    all_to_all x6, blocking collectives, exchange(): return lax.all_to_all(parts, axis, 0, 0, axis_index_groups=groups)  104 us
    pallas_call x10, Pallas kernels, call(): pl.pallas_call(kernel, out_shape=shapes[0] if single else shapes, in_spec...  14.7 us
    ppermute x1, waiting for transfers between devices, per_device(): pair = lax.ppermute(own, 'dp', NEIGHBOUR)  8.99 us
  transfers between devices with their start and end apart: 4, of which 2 were waited for; matrix products, arithmetic and copies ran while one was open for 1% of the time, Pallas kernels for 5%

profile of v10, /device:TPU:8, one launch (start us, length us, event | category | flops | bytes accessed | tf_op | source)
XLA Modules:
  0.0 138.8 jit_solution(18003377136240211998)
XLA Ops:
  0.6 1.4 shard_map.93
  2.0 16.0 %all_to_all.30.parts_ref = bf16[8,128,256]{2,1,0:T(8,128)(2,1)S(1)} all-to-all(bf16[8,128,256]{2,1,0:T(8,128)(2,1)S(1)} %shard_map.93), channel_id=1, replica_groups=mesh['dp'=64,'expert'=8] {'expert'}, dimensions={0} | all-to-all | bytes 1048576 | tf_op jit(solution)/shard_map/all_to_all | solution.py:260
  18.1 16.6 %all_to_all.31 = bf16[4,128,256]{2,1,0:T(8,128)(2,1)S(1)} all-to-all(bf16[4,128,256]{2,1,0:T(8,128)(2,1)S(1)} %shard_map.94), channel_id=1, replica_groups={{0,128,256,384},{16,144,272,400},{32,160,288,416},{48,176,304,432},{64,..., dimensions={0} | all-to-all | bytes 524288 | tf_op jit(solution)/shard_map/all_to_all | solution.py:260
  34.7 0.1 broadcast_in_dim.6
  34.8 27.5 %all_to_all.32.own_ref = bf16[4,4,128,256]{3,2,1,0:T(8,128)(2,1)S(1)} all-to-all(bf16[4,4,128,256]{3,2,1,0:T(8,128)(2,1)S(1)} %broadcast_in_dim.6), channel_id=1, replica_groups={{0,16,32,48},{64,80,96,112},{128,144,160,176},{192,208,224,240},{256,27..., dimensions={0} | all-to-all | bytes 2097152 | tf_op jit(solution)/shard_map/all_to_all | solution.py:260
  62.3 2.6 %collective-permute-start.1 = (bf16[4,4,128,256]{3,2,1,0:T(8,128)(2,1)S(1)}, bf16[4,4,128,256]{3,2,1,0:T(8,128)(2,1)S(1)}, u32[]{:S(2)}, u32[]{:S(2)}) collective-permute-start(bf16[4,4,128,256]{3,2,1,0:T(8,128)(2,1)S(1)} %all_to_all.32.own_ref), channel_id=1, source_target_pairs={{0,64},{8,456},{16,80},{24,472},{32,96},{40,488},{48,112},{56,504}... | collective-permute-start | bytes 3145736 | tf_op jit(solution)/shard_map/ppermute | solution.py:313
  64.9 1.9 %collective-permute-start = (bf16[4,4,128,256]{3,2,1,0:T(8,128)(2,1)S(1)}, bf16[4,4,128,256]{3,2,1,0:T(8,128)(2,1)}, u32[]{:S(2)}, u32[]{:S(2)}) collective-permute-start(bf16[4,4,128,256]{3,2,1,0:T(8,128)(2,1)S(1)} %all_to_all.32.own_ref), channel_id=1, source_target_pairs={{0,8},{8,0},{16,24},{24,16},{32,40},{40,32},{48,56},{56,48},{64,72... | collective-permute-start | bytes 3145736 | tf_op jit(solution)/shard_map/ppermute | solution.py:314
  67.0 0.1 reshape.173
  67.2 0.1 select_n.92
  67.7 2.3 %shard_map.95 = (bf16[4096,256]{1,0:T(8,128)(2,1)S(1)}, bf16[4096,256]{1,0:T(8,128)(2,1)S(1)}, bf16[128,4096]{1,0:T(8,128)(2,1)S(1)}, bf16[4096,128]{1,0:T(8,128)(2,1)S(1)}) custom-call(s32[128]{0:T(128)S(1)} %concatenate.3.slots_ref, bf16[4,4,128,256]{3,2,1,0:T(8,128)(2,1)S(1)} %all_to_all.32.own_ref, bf16[4096,128]{1,0:T(8,128)(2,1)S(1)} %bitcast.9), custom_call_target="tpu_custom_call" | custom-call | flops 2097152 | bytes 6291456 | tf_op jit(solution)/shard_map/pallas_call | solution.py:243
  70.0 9.0 %collective-permute-done.1.pair_ref = bf16[4,4,128,256]{3,2,1,0:T(8,128)(2,1)S(1)} collective-permute-done((bf16[4,4,128,256]{3,2,1,0:T(8,128)(2,1)S(1)}, bf16[4,4,128,256]{3,2,1,0:T(8,128)(2,1)S(1)}, u32[]{:S(2)}, u32[]{:S(2)}) %collective-permute-start.1) | collective-permute-done | bytes 1048608 | tf_op jit(solution)/shard_map/ppermute | solution.py:313
  79.0 2.0 %collective-permute-start.2 = (bf16[4,4,128,256]{3,2,1,0:T(8,128)(2,1)S(1)}, bf16[4,4,128,256]{3,2,1,0:T(8,128)(2,1)S(1)}, u32[]{:S(2)}, u32[]{:S(2)}) collective-permute-start(bf16[4,4,128,256]{3,2,1,0:T(8,128)(2,1)S(1)} %collective-permute-done.1.pair_ref), channel_id=1, source_target_pairs={{0,8},{8,0},{16,24},{24,16},{32,40},{40,32},{48,56},{56,48},{64,72... | collective-permute-start | bytes 3145736 | tf_op jit(solution)/shard_map/ppermute | solution.py:324
  81.0 2.0 %shard_map.96 = (bf16[4096,256]{1,0:T(8,128)(2,1)S(1)}, bf16[4096,256]{1,0:T(8,128)(2,1)S(1)}) custom-call(s32[128]{0:T(128)S(1)} %concatenate.3.slots_ref, bf16[4,4,128,256]{3,2,1,0:T(8,128)(2,1)} %collective-permute-done.oth_ref, bf16[4,4,128,256]{3,2,1,0:T(8,128)(2,1)S(1)} %collective-permute-done.1.pair_ref, ...), custom_call_target="tpu_custom_call", output_to_operand_aliasing={{0}: (3, {}), {1}: (4, {})} | custom-call | flops 2097152 | bytes 3145728 | tf_op jit(solution)/shard_map/pallas_call | solution.py:243
  83.1 0.6 collective-permute-done.2.oth_ref
  83.7 3.8 %shard_map.97 = (bf16[4096,256]{1,0:T(8,128)(2,1)S(1)}, bf16[4096,256]{1,0:T(8,128)(2,1)S(1)}, bf16[128,256]{1,0:T(8,128)(2,1)S(1)}, bf16[128,256]{1,0:T(8,128)(...) custom-call(s32[128]{0:T(128)S(1)} %concatenate.3.slots_ref, ...), custom_call_target="tpu_custom_call", output_to_operand_aliasing={{0}: (2, {}), {1}: (3, {})} | custom-call | tf_op jit(solution)/shard_map/pallas_call | solution.py:243
  87.4 2.0 %collective-permute-start.3 = (bf16[2064,256]{1,0:T(8,128)(2,1)S(1)}, bf16[2064,256]{1,0:T(8,128)(2,1)S(1)}, u32[]{:S(2)}, u32[]{:S(2)}) collective-permute-start(bf16[2064,256]{1,0:T(8,128)(2,1)S(1)} %get-tuple-element.39), channel_id=1, source_target_pairs={{0,8},{8,0},{16,24},{24,16},{32,40},{40,32},{48,56},{56,48},{64,72... | collective-permute-start | bytes 3170312 | tf_op jit(solution)/shard_map/ppermute | solution.py:343
  89.5 2.6 %shard_map.98 = (bf16[4096,128]{1,0:T(8,128)(2,1)}, bf16[128,4096]{1,0:T(8,128)(2,1)}) custom-call(bf16[4096,256]{1,0:T(8,128)(2,1)S(1)} %get-tuple-element.40.x_ref, bf16[4096,256]{1,0:T(8,128)(2,1)S(1)} %get-tuple-element.41.u_ref, bf16[128,256]{1,0:T(8,128)(2,1)S(1)} %get-tuple-element.42.back_ref, bf16[128,256]{1,0:T(8,128)(2,1)S(1)} %get-tuple-element.43.scaled_ref), custom_call_target="tpu_custom_call" | custom-call | flops 536870912 | bytes 6291456 | tf_op jit(solution)/shard_map/pallas_call | solution.py:243
  92.1 0.4 shard_map.99
  92.5 21.5 %all_to_all.33.got_ref = bf16[4,528,256]{2,1,0:T(8,128)(2,1)S(1)} all-to-all(bf16[4,528,256]{2,1,0:T(8,128)(2,1)S(1)} %shard_map.99), channel_id=1, replica_groups={{0,16,32,48},{64,80,96,112},{128,144,160,176},{192,208,224,240},{256,27..., dimensions={0} | all-to-all | bytes 2162688 | tf_op jit(solution)/shard_map/all_to_all | solution.py:260
  114.0 0.1 shard_map.100
  114.2 12.8 %all_to_all.34.got_ref = bf16[8,80,256]{2,1,0:T(8,128)(2,1)S(1)} all-to-all(bf16[8,80,256]{2,1,0:T(8,128)(2,1)S(1)} %shard_map.100), channel_id=1, replica_groups={{0,64,128,192,256,320,384,448},{16,80,144,208,272,336,400,464},{32,96,1..., dimensions={0} | all-to-all | bytes 655360 | tf_op jit(solution)/shard_map/all_to_all | solution.py:260
  127.0 0.6 shard_map.101
  127.6 9.8 %all_to_all.35.terms_ref = bf16[8,64,256]{2,1,0:T(8,128)(2,1)S(1)} all-to-all(bf16[8,64,256]{2,1,0:T(8,128)(2,1)S(1)} %get-tuple-element.50), channel_id=1, replica_groups=mesh['dp'=64,'expert'=8] {'expert'}, dimensions={0} | all-to-all | bytes 524288 | tf_op jit(solution)/shard_map/all_to_all | solution.py:260
  137.4 1.4 shard_map.102
  (21 shorter events, 0.7 us)
Async XLA Ops:
  18.1 49.6 %copy-start = (bf16[1,4096,128]{2,1,0:T(8,128)(2,1)S(1)}, bf16[1,4096,128]{2,1,0:T(8,128)(2,1)}, u32[]{:S(2)}) copy-start(bf16[1,4096,128]{2,1,0:T(8,128)(2,1)} %param.8) | copy-start | bytes 3145732
  62.3 16.7 %collective-permute-start.1 = (bf16[4,4,128,256]{3,2,1,0:T(8,128)(2,1)S(1)}, bf16[4,4,128,256]{3,2,1,0:T(8,128)(2,1)S(1)}, u32[]{:S(2)}, u32[]{:S(2)}) collective-permute-start(bf16[4,4,128,256]{3,2,1,0:T(8,128)(2,1)S(1)} %all_to_all.32.own_ref), channel_id=1, source_target_pairs={{0,64},{8,456},{16,80},{24,472},{32,96},{40,488},{48,112},{56,504}... | collective-permute-start | bytes 3145736 | tf_op jit(solution)/shard_map/ppermute | solution.py:313
  64.9 14.1 %collective-permute-start = (bf16[4,4,128,256]{3,2,1,0:T(8,128)(2,1)S(1)}, bf16[4,4,128,256]{3,2,1,0:T(8,128)(2,1)}, u32[]{:S(2)}, u32[]{:S(2)}) collective-permute-start(bf16[4,4,128,256]{3,2,1,0:T(8,128)(2,1)S(1)} %all_to_all.32.own_ref), channel_id=1, source_target_pairs={{0,8},{8,0},{16,24},{24,16},{32,40},{40,32},{48,56},{56,48},{64,72... | collective-permute-start | bytes 3145736 | tf_op jit(solution)/shard_map/ppermute | solution.py:314
  79.0 4.7 %copy-start.2 = (f32[1,256]{1,0:T(1,128)S(1)}, f32[1,256]{1,0:T(1,128)}, u32[]{:S(2)}) copy-start(f32[1,256]{1,0:T(1,128)} %score_ref.1) | copy-start | bytes 3076
  79.0 4.7 %collective-permute-start.2 = (bf16[4,4,128,256]{3,2,1,0:T(8,128)(2,1)S(1)}, bf16[4,4,128,256]{3,2,1,0:T(8,128)(2,1)S(1)}, u32[]{:S(2)}, u32[]{:S(2)}) collective-permute-start(bf16[4,4,128,256]{3,2,1,0:T(8,128)(2,1)S(1)} %collective-permute-done.1.pair_ref), channel_id=1, source_target_pairs={{0,8},{8,0},{16,24},{24,16},{32,40},{40,32},{48,56},{56,48},{64,72... | collective-permute-start | bytes 3145736 | tf_op jit(solution)/shard_map/ppermute | solution.py:324
  87.4 4.7 %collective-permute-start.3 = (bf16[2064,256]{1,0:T(8,128)(2,1)S(1)}, bf16[2064,256]{1,0:T(8,128)(2,1)S(1)}, u32[]{:S(2)}, u32[]{:S(2)}) collective-permute-start(bf16[2064,256]{1,0:T(8,128)(2,1)S(1)} %get-tuple-element.39), channel_id=1, source_target_pairs={{0,8},{8,0},{16,24},{24,16},{32,40},{40,32},{48,56},{56,48},{64,72... | collective-permute-start | bytes 3170312 | tf_op jit(solution)/shard_map/ppermute | solution.py:343
  92.5 44.9 %copy-start.1 = (s32[8,256]{1,0:T(8,128)S(1)}, s32[8,256]{1,0:T(8,128)}, u32[]{:S(2)}) copy-start(s32[8,256]{1,0:T(8,128)} %chosen_ref.1) | copy-start | bytes 24580
